TPU v7x, 256 devices: a whole 4x4x8 slice. The times are simulated.
256 devices in a mesh: sym: 8 (over y, core), rows: 32 (over z, x).
Axes of the slice: x: 4, y: 4, z: 8, core: 2. Of those that a mesh axis runs over, the one named last changes fastest.
Arguments:
- coeffs: bfloat16 [16384, 8192], P('rows', 'sym'), may hold values from -6 to 6
- beta_op: bfloat16 [8, 1024, 1024], P('sym'), may hold values from -0.1875 to 0.1875
- mix_op: bfloat16 [8, 8, 8, 128, 128], P('sym'), may hold values from -0.125 to 0.125
- pair_op: bfloat16 [8, 128, 128], replicated, may hold values from -0.1875 to 0.1875
- send_list: int32 [32, 32, 2], replicated, may hold values from -1 to 3, as said below
- mix_slot: int32 [128, 16], replicated, may hold values from 0 to 63, as said below
- mix_sign: int32 [128, 16], replicated, may hold values from 0 to 1
- mix_pair: int32 [128, 16], replicated, may hold values from 0 to 7
- aa_src: int32 [128, 8], replicated, may hold values from 0 to 127
- aa_sign: int32 [128, 8], replicated, may hold values from 0 to 1
- aa_pair: int32 [128, 8], replicated, may hold values from 0 to 7
Outputs:
- sigma: float32 [16384, 8192], P('rows', 'sym')
Inputs may be any that keep to these rules, and one draw needn't show every extreme that they name: send_list[s, r, c] is the block, counted within device s's own 4 alpha blocks, that s sends to device r in slot c, or -1 for an empty slot; live slots of a pair come first and hold distinct blocks; every device sends at least one block to itself; in every draw some device receives 2 blocks from every device. mix_slot[P, l] = s * 2 + c names slot c of send_list[s, P // 4], always a live one; every live slot sent to a device is named by some entry of that device's destination blocks.
All inputs are finite; a program needn't handle non-finite values.
Results may differ from a plain program's by a relative error of at most 0.0075.
Values may be sent and summed in bfloat16 or wider, within the bound.
No kernel may reach another device: no remote copies, remote signals or barrier semaphores. Data moves between devices by JAX's collectives and lax.ppermute only.
A program may use at most 128 MiB of HBM per device.

v0:
```python
import jax
import jax.numpy as jnp
from jax import lax
from jax.sharding import PartitionSpec as P

TILE = 128
BT = 8
ABLK = 4
CAP = 2
NPA = 8


def cut_along(array, dim, devices):
    dims = array.shape
    parts = array.reshape(*dims[:dim], devices, dims[dim] // devices, *dims[dim + 1 :])
    return jnp.moveaxis(parts, dim, 0)


def piece_ends(length, count):
    hop = length // count
    if hop >= 8:
        hop -= hop % 8
    return [hop * k for k in range(1, count)]


def laid_out(parts, dim):
    dims = list(parts.shape[1:])
    dims[dim] *= parts.shape[0]
    return jnp.moveaxis(parts, 0, dim).reshape(dims)


def exchange_in_pieces(array, axis, pieces, split_dim, concat_dim):
    parts = cut_along(array, split_dim, lax.axis_size(axis))
    widest = max(range(1, max(2, parts.ndim - 1)), key=lambda d: parts.shape[d])
    finished = []
    for slab in jnp.split(parts, piece_ends(parts.shape[widest], pieces), axis=widest):
        if slab.size:
            finished.append(lax.all_to_all(slab, axis, split_axis=0, concat_axis=0, tiled=True))
    return laid_out(jnp.concatenate(finished, axis=widest), concat_dim)


def per_device(
    coeffs,
    beta_op,
    mix_op,
    pair_op,
    send_list,
    mix_slot,
    mix_sign,
    mix_pair,
    aa_src,
    aa_sign,
    aa_pair,
):
    rows_here, beta_here = coeffs.shape
    sectors = lax.axis_size("sym")
    rank_count = lax.axis_size("rows")
    sector = lax.axis_index("sym")
    block_count = aa_src.shape[0]
    total_rows = block_count * TILE
    col_width = beta_here // rank_count
    local_term = jnp.dot(coeffs, beta_op[0], preferred_element_type=jnp.float32)
    flipped = coeffs.T
    columns = lax.all_to_all(flipped, "rows", split_axis=0, concat_axis=1, tiled=True)
    col_blocks = columns.reshape(col_width, block_count, TILE)
    picked = jnp.take(col_blocks, aa_src, axis=1)
    operator_ids = jnp.arange(NPA, dtype=jnp.int32)
    aa_weight = (
        (1 - 2 * aa_sign)[:, :, None]
        * (aa_pair[:, :, None] == operator_ids[None, None, :]).astype(jnp.int32)
    ).astype(jnp.bfloat16)
    combined = jnp.einsum(
        "cpki,pkg->cpgi", picked, aa_weight, preferred_element_type=jnp.float32
    ).astype(jnp.bfloat16)
    alpha_part = jnp.einsum(
        "cpgj,gij->cpi", combined, pair_op, preferred_element_type=jnp.float32
    ).reshape(col_width, total_rows)
    returned = lax.all_to_all(
        alpha_part.astype(jnp.bfloat16), "rows", split_axis=1, concat_axis=0, tiled=True
    ).astype(alpha_part.dtype)
    dest_ids = jnp.arange(sectors, dtype=jnp.int32)
    pair_of = jnp.bitwise_xor(sector, dest_ids)
    operators = jnp.take(mix_op[0], pair_of, axis=0)
    sign_all = (1 - 2 * mix_sign).astype(jnp.float32)
    slot_src = mix_slot // CAP
    slot_pos = mix_slot % CAP
    dest_rank = (jnp.arange(block_count, dtype=jnp.int32) // ABLK)[:, None]
    owned_blk = send_list[slot_src, dest_rank, slot_pos]
    source = slot_src * ABLK + owned_blk
    gathered = jnp.take(col_blocks, source, axis=1)
    mix_weight = (
        sign_all[None, :, :] * (mix_pair[None, :, :] == pair_of[:, None, None]).astype(jnp.float32)
    ).astype(jnp.bfloat16)
    combos = jnp.einsum(
        "cpli,dpl->dcpi", gathered, mix_weight, preferred_element_type=jnp.float32
    ).astype(jnp.bfloat16)
    combos = combos.reshape(sectors, col_width, total_rows)
    came_back = exchange_in_pieces(combos, "rows", 2, 2, 1)
    inputs = came_back.reshape(sectors, BT, TILE, rows_here)
    contract_eq = "dtkr,dtkj->drtj"
    row_count = lax.axis_size("sym") * rows_here
    products = jnp.einsum(contract_eq, inputs, operators, preferred_element_type=jnp.float32)
    mixed = lax.psum_scatter(
        products.reshape(row_count, beta_here).astype(jnp.bfloat16),
        "sym",
        scatter_dimension=0,
        tiled=True,
    ).astype(jnp.float32)
    return local_term + returned.T + mixed


def solution(mesh):
    in_specs = (
        P("rows", "sym"),
        P("sym", None, None),
        P("sym", None, None, None, None),
        P(),
        P(),
        P(),
        P(),
        P(),
        P(),
        P(),
        P(),
    )
    out_specs = P("rows", "sym")
    return jax.shard_map(
        per_device, mesh=mesh, in_specs=in_specs, out_specs=out_specs, check_vma=False
    )
```

profile of v0, /device:TPU:18, one launch (start us, length us, event | category | flops | bytes accessed | tf_op | source)
XLA Modules:
  0.0 472.6 jit_solution(12893267071110367578)
XLA Ops:
  9.0 11.6 %all-to-all-start = ((bf16[32,32,512]{2,1,0:T(8,128)(2,1)}), bf16[32,32,512]{2,1,0:T(8,128)(2,1)S(1)}, u32[]{:S(2)}, u32[]{:S(2)}) async-start(bf16[32,32,512]{2,1,0:T(8,128)(2,1)} %bitcast.84), calls=%async_computation | async-start | bytes 2097152 | tf_op jit(solution)/shard_map/all_to_all | solution.py:64
  21.5 20.1 %gather_fusion.2 = s32[2048]{0:T(1024)S(1)} fusion(s32[32,32,2]{1,2,0:T(2,128)S(1)} %copy-done.1, s32[2048]{0:T(1024)S(1)} %reshape.96), kind=kCustom, calls=%fused_computation.2 | custom fusion | bytes 40960 | tf_op jit(solution)/shard_map/gather | solution.py:88
  42.4 6.2 %all-to-all-done = bf16[32,32,512]{2,1,0:T(8,128)(2,1)S(1)} async-done(((bf16[32,32,512]{2,1,0:T(8,128)(2,1)}), bf16[32,32,512]{2,1,0:T(8,128)(2,1)S(1)}, u32[]{:S(2)}, u32[]{:S(2)}) %all-to-all-start) | async-done | bytes 1048608 | tf_op jit(solution)/shard_map/all_to_all | solution.py:64
  54.6 19.2 %gather_fusion.3 = bf16[2048,32,128]{2,1,0:T(8,128)(2,1)} fusion(bf16[32,128,128]{2,0,1:T(8,128)(2,1)S(1)} %copy.77, s32[2048]{0:T(1024)S(1)} %broadcast_clamp_fusion), kind=kCustom, calls=%fused_computation.3 | custom fusion | bytes 33562624 | tf_op jit(solution)/shard_map/jit(_take)/gather | solution.py:90
  73.8 14.4 %select_bitcast_fusion = bf16[32,128,16,128]{3,0,2,1:T(8,128)(2,1)} fusion(bf16[128,16,32,128]{3,2,1,0:T(8,128)(2,1)} %bitcast.76, pred[128,16]{1,0:T(8,128)(4,1)S(1)} %copy.86), kind=kLoop, calls=%fused_computation.6 | loop fusion | flops 8388608 | bytes 33556480 | tf_op jit(solution)/shard_map/jit(_take)/select_n | solution.py:90
  88.2 25.9 %convert_bitcast_fusion.1 = bf16[8,32,128,128]{3,0,1,2:T(8,128)(2,1)} fusion(bf16[32,128,16,128]{3,0,2,1:T(8,128)(2,1)} %select_bitcast_fusion, bf16[128,16]{1,0:T(8,128)(2,1)S(1)} %copy.83, s32[128,16]{1,0:T(8,128)S(1)} %copy.82, s32[8]{0:T(128)S(1)} %iota_xor_fusion), kind=kOutput, calls=%fused_computation.15 | convolution fusion | flops 138444800 | bytes 25178144 | tf_op jit(solution)/shard_map/cpli,dpl->dcpi/dot_general | solution.py:94
  114.1 12.0 %copy.90 = bf16[8,32,128,128]{3,2,1,0:T(8,128)(2,1)} copy(bf16[8,32,128,128]{3,0,1,2:T(8,128)(2,1)} %convert_bitcast_fusion.1) | data formatting | bytes 16777216 | tf_op jit(solution)/shard_map/convert_element_type | solution.py:96
  126.1 14.0 %reshape_reshape.6 = bf16[8,32,32,512]{3,2,1,0:T(8,128)(2,1)} reshape(bf16[8,32,128,128]{3,2,1,0:T(8,128)(2,1)} %copy.90) | data formatting | bytes 16777216 | tf_op jit(solution)/shard_map/reshape;reshape | solution.py:15
  140.1 5.3 %fusion.51 = (bf16[32,8,16,512]{3,0,2,1:T(8,128)(2,1)S(1)}, bf16[32,8,16,512]{3,0,2,1:T(8,128)(2,1)}) fusion(bf16[32,8,32,512]{3,0,2,1:T(8,128)(2,1)} %bitcast.79), kind=kLoop, calls=%fused_computation.83 | loop fusion | bytes 16777216 | tf_op jit(solution)/shard_map/split | solution.py:36
  149.7 5.6 %all-to-all-start.2 = ((bf16[32,8,16,512]{3,2,1,0:T(8,128)(2,1)}), bf16[32,8,16,512]{3,2,1,0:T(8,128)(2,1)}, u32[]{:S(2)}, u32[]{:S(2)}) async-start(bf16[32,8,16,512]{3,2,1,0:T(8,128)(2,1)} %copy.91), calls=%async_computation.2 | async-start | bytes 8388608 | tf_op jit(solution)/shard_map/all_to_all | solution.py:38
  155.3 6.5 %copy.92 = bf16[32,8,16,512]{3,2,1,0:T(8,128)(2,1)} copy(bf16[32,8,16,512]{3,0,2,1:T(8,128)(2,1)} %get-tuple-element.8) | data formatting | bytes 8388608 | tf_op jit(solution)/shard_map/split | solution.py:36
  161.8 85.3 %all-to-all-done.2 = bf16[32,8,16,512]{3,2,1,0:T(8,128)(2,1)} async-done(((bf16[32,8,16,512]{3,2,1,0:T(8,128)(2,1)}), bf16[32,8,16,512]{3,2,1,0:T(8,128)(2,1)}, u32[]{:S(2)}, u32[]{:S(2)}) %all-to-all-start.2) | async-done | bytes 4194336 | tf_op jit(solution)/shard_map/all_to_all | solution.py:38
  247.2 8.4 %all-to-all-start.3 = ((bf16[32,8,16,512]{3,2,1,0:T(8,128)(2,1)}), bf16[32,8,16,512]{3,2,1,0:T(8,128)(2,1)}, u32[]{:S(2)}, u32[]{:S(2)}) async-start(bf16[32,8,16,512]{3,2,1,0:T(8,128)(2,1)} %copy.92), calls=%async_computation.3 | async-start | bytes 8388608 | tf_op jit(solution)/shard_map/all_to_all | solution.py:38
  257.8 90.0 %all-to-all-done.3 = bf16[32,8,16,512]{3,2,1,0:T(8,128)(2,1)} async-done(((bf16[32,8,16,512]{3,2,1,0:T(8,128)(2,1)}), bf16[32,8,16,512]{3,2,1,0:T(8,128)(2,1)}, u32[]{:S(2)}, u32[]{:S(2)}) %all-to-all-start.3) | async-done | bytes 4194336 | tf_op jit(solution)/shard_map/all_to_all | solution.py:38
  347.8 8.2 %maximum_bitcast_fusion = bf16[8,32,32,512]{3,2,0,1:T(8,128)(2,1)} fusion(bf16[32,8,16,512]{3,2,1,0:T(8,128)(2,1)} %all-to-all-done.3, bf16[32,8,16,512]{3,2,1,0:T(8,128)(2,1)} %all-to-all-done.2), kind=kLoop, calls=%fused_computation.8 | loop fusion | flops 16777216 | bytes 16777216 | tf_op jit(solution)/shard_map/transpose | solution.py:29
  356.0 8.4 %copy.93 = bf16[8,32,32,512]{3,2,1,0:T(8,128)(2,1)} copy(bf16[8,32,32,512]{3,2,0,1:T(8,128)(2,1)} %maximum_bitcast_fusion) | data formatting | bytes 16777216 | tf_op jit(solution)/shard_map/transpose | solution.py:29
  364.5 9.1 %convert_bitcast_fusion = bf16[8,512,8,128]{1,3,2,0:T(8,128)(2,1)} fusion(bf16[8,8,128,512]{3,2,1,0:T(8,128)(2,1)} %bitcast.77, bf16[8,8,128,128]{3,2,1,0:T(8,128)(2,1)S(1)} %copy-done.2, pred[8]{0:T(512)(128)(4,1)S(1)} %compare_and_fusion.2), kind=kOutput, calls=%fused_computation.14 | convolution fusion | flops 1078984704 | bytes 18874376 | tf_op jit(solution)/shard_map/dtkr,dtkj->drtj/dot_general | solution.py:102
  373.5 12.7 %copy.95 = bf16[8,512,8,128]{3,2,1,0:T(8,128)(2,1)} copy(bf16[8,512,8,128]{1,3,2,0:T(8,128)(2,1)} %convert_bitcast_fusion) | data formatting | bytes 16777216 | tf_op jit(solution)/shard_map/convert_element_type | solution.py:104
  386.2 8.8 %copy.116 = bf16[512,8,8,128]{3,1,2,0:T(8,128)(2,1)} copy(bf16[512,8,8,128]{3,2,1,0:T(8,128)(2,1)} %bitcast.80) | data formatting | bytes 16777216
  396.2 9.9 %gather_fusion = bf16[1024,32,128]{2,1,0:T(8,128)(2,1)} fusion(bf16[32,128,128]{2,0,1:T(8,128)(2,1)S(1)} %copy.77, s32[1024]{0:T(1024)S(1)} %broadcast_clamp_fusion.1), kind=kCustom, calls=%fused_computation | custom fusion | bytes 16781312 | tf_op jit(solution)/shard_map/jit(_take)/gather | solution.py:66
  406.1 7.2 %convert_bitcast_fusion.2 = bf16[32,128,8,128]{3,2,0,1:T(8,128)(2,1)S(1)} fusion(bf16[128,8,32,128]{3,2,1,0:T(8,128)(2,1)} %bitcast.81, pred[128,8]{1,0:T(8,128)(4,1)S(1)} %copy.73, s32[128,8]{1,0:T(8,128)S(1)} %copy.72, s32[128,8]{1,0:T(8,128)S(1)} %copy.71), kind=kOutput, calls=%fused_computation.16 | convolution fusion | flops 75522048 | bytes 16786432 | tf_op jit(solution)/shard_map/cpki,pkg->cpgi/dot_general | solution.py:72
  413.3 6.1 %bitcast_convert_fusion = bf16[32,128,128]{2,1,0:T(8,128)(2,1)} fusion(bf16[32,128,8,128]{3,2,0,1:T(8,128)(2,1)S(1)} %convert_bitcast_fusion.2, bf16[8,128,128]{2,1,0:T(8,128)(2,1)S(1)} %copy-done.10), kind=kOutput, calls=%fused_computation.21 | convolution fusion | flops 1074266112 | bytes 9699328 | tf_op jit(solution)/shard_map/cpgj,gij->cpi/dot_general | solution.py:75
  421.7 34.0 %all_to_all.36 = bf16[32,32,512]{2,0,1:T(8,128)(2,1)S(1)} all-to-all(bf16[32,32,512]{2,0,1:T(8,128)(2,1)S(1)} %copy.80), channel_id=1, replica_groups=mesh['sym'=8,'rows'=32] {'rows'}, dimensions={1} | all-to-all | bytes 2097152 | tf_op jit(solution)/shard_map/all_to_all | solution.py:78
  460.3 5.1 %fusion.12 = f32[512,1024]{1,0:T(8,128)} fusion(f32[1024,512]{0,1:T(8,128)} %copy.81, bf16[512,1024]{1,0:T(8,128)(2,1)} %reduce-scatter.2.cloned.1.call-done, bf16[512,1024]{1,0:T(8,128)(2,1)S(1)} %copy-done.3, bf16[1,1024,1024]{2,1,0:T(8,128)(2,1)} %param.12), kind=kOutput, calls=%fused_computation.20 | convolution fusion | flops 1075314688 | bytes 8388608 | tf_op jit(solution)/shard_map/dot_general | solution.py:62
  (62 shorter events, 24.6 us)
Async XLA Ops:
  6.5 249.1 %copy-start = (bf16[1,8,8,128,128]{4,3,2,1,0:T(8,128)(2,1)S(1)}, bf16[1,8,8,128,128]{4,3,2,1,0:T(8,128)(2,1)}, u32[]{:S(2)}) copy-start(bf16[1,8,8,128,128]{4,3,2,1,0:T(8,128)(2,1)} %param.13) | copy-start | bytes 6291460
  6.5 15.0 %copy-start.1 = (s32[32,32,2]{1,2,0:T(2,128)S(1)}, s32[32,32,2]{1,2,0:T(2,128)}, u32[]{:S(2)}) copy-start(s32[32,32,2]{1,2,0:T(2,128)} %param.15) | copy-start | bytes 24580
  9.0 39.7 %all-to-all-start = ((bf16[32,32,512]{2,1,0:T(8,128)(2,1)}), bf16[32,32,512]{2,1,0:T(8,128)(2,1)S(1)}, u32[]{:S(2)}, u32[]{:S(2)}) async-start(bf16[32,32,512]{2,1,0:T(8,128)(2,1)} %bitcast.84), calls=%async_computation | async-start | bytes 2097152 | tf_op jit(solution)/shard_map/all_to_all | solution.py:64
  21.5 20.3 %copy-start.4 = (s32[128,16]{0,1:T(8,128)S(1)}, s32[128,16]{0,1:T(8,128)}, u32[]{:S(2)}) copy-start(s32[128,16]{0,1:T(8,128)} %param.16) | copy-start | bytes 24580
  21.5 20.6 %copy-start.6 = (s32[128,16]{0,1:T(8,128)S(1)}, s32[128,16]{0,1:T(8,128)}, u32[]{:S(2)}) copy-start(s32[128,16]{0,1:T(8,128)} %param.18) | copy-start | bytes 24580
  21.5 20.7 %copy-start.7 = (s32[128,16]{0,1:T(8,128)S(1)}, s32[128,16]{0,1:T(8,128)}, u32[]{:S(2)}) copy-start(s32[128,16]{0,1:T(8,128)} %param.17) | copy-start | bytes 24580
  149.7 97.5 %all-to-all-start.2 = ((bf16[32,8,16,512]{3,2,1,0:T(8,128)(2,1)}), bf16[32,8,16,512]{3,2,1,0:T(8,128)(2,1)}, u32[]{:S(2)}, u32[]{:S(2)}) async-start(bf16[32,8,16,512]{3,2,1,0:T(8,128)(2,1)} %copy.91), calls=%async_computation.2 | async-start | bytes 8388608 | tf_op jit(solution)/shard_map/all_to_all | solution.py:38
  247.2 100.6 %all-to-all-start.3 = ((bf16[32,8,16,512]{3,2,1,0:T(8,128)(2,1)}), bf16[32,8,16,512]{3,2,1,0:T(8,128)(2,1)}, u32[]{:S(2)}, u32[]{:S(2)}) async-start(bf16[32,8,16,512]{3,2,1,0:T(8,128)(2,1)} %copy.92), calls=%async_computation.3 | async-start | bytes 8388608 | tf_op jit(solution)/shard_map/all_to_all | solution.py:38
  255.6 204.7 %reduce-scatter.2.cloned.1.call-start = ((), (), s32[]{:S(2)}) async-start(), calls=%async_computation.5 | async-start | bytes 9437184 | tf_op jit(solution)/shard_map/reduce_scatter | solution.py:103
  356.0 8.4 %copy-start.2 = (bf16[8,8,128,128]{3,2,1,0:T(8,128)(2,1)S(1)}, bf16[8,8,128,128]{3,2,1,0:T(8,128)(2,1)}, u32[]{:S(2)}) copy-start(bf16[8,8,128,128]{3,2,1,0:T(8,128)(2,1)} %gather_fusion.1) | copy-start | bytes 6291460
  395.0 0.7 copy-start.5
  395.0 0.9 copy-start.9
  395.0 1.0 copy-start.8
  406.1 7.2 %copy-start.10 = (bf16[8,128,128]{2,1,0:T(8,128)(2,1)S(1)}, bf16[8,128,128]{2,1,0:T(8,128)(2,1)}, u32[]{:S(2)}) copy-start(bf16[8,128,128]{2,1,0:T(8,128)(2,1)} %param.14) | copy-start | bytes 786436
  421.7 38.6 %copy-start.3 = (bf16[512,1024]{1,0:T(8,128)(2,1)S(1)}, bf16[512,1024]{1,0:T(8,128)(2,1)}, u32[]{:S(2)}) copy-start(bf16[512,1024]{1,0:T(8,128)(2,1)} %param.11) | copy-start | bytes 3145732
Sparse Core Ops, SparseCore 0:
  395.1 51.5 reduce-scatter.1
where the time goes:
time: 480 us; the launch traced here: 473 us
  waiting for transfers between devices  182 us (38%)
  local copies, waits for them, and re-layouts  139 us (29%)
  matrix products  53.3 us (11%)
  blocking collectives  34 us (7%)
  starting transfers between devices  25.7 us (5%)
  other arithmetic  25 us (5%)
  between operations  14 us (3%)
    all_to_all x2, waiting for transfers between devices, exchange_in_pieces(): lax.all_to_all(slab, axis, split_axis=0, concat_axis=0, tiled=True)  175 us
    all_to_all x1, blocking collectives, per_device(): lax.all_to_all(alpha_part.astype(jnp.bfloat16), 'rows', split_axis=1, con...  34 us
    dot_general x1, matrix products, per_device(): jnp.einsum('cpli,dpl->dcpi', gathered, mix_weight, preferred_element_type...  25.9 us
    gather x3, local copies, waits for them, and re-layouts, per_device(): owned_blk = send_list[slot_src, dest_rank, slot_pos]  20.2 us
    gather x1, local copies, waits for them, and re-layouts, per_device(): gathered = jnp.take(col_blocks, source, axis=1)  19.2 us
    split x3, local copies, waits for them, and re-layouts, exchange_in_pieces(): jnp.split(parts, piece_ends(parts.shape[widest], pieces), axis=widest)  16.1 us
    select_n x1, other arithmetic, per_device(): gathered = jnp.take(col_blocks, source, axis=1)  14.4 us
    all_to_all x2, starting transfers between devices, exchange_in_pieces(): lax.all_to_all(slab, axis, split_axis=0, concat_axis=0, tiled=True)  14 us
  transfers between devices with their start and end apart: 4, of which 3 were waited for; matrix products, arithmetic and copies ran while one was open for 13% of the time, Pallas kernels for 0%

commit v1 on v0

v1 whole, which is shorter than its diff:
```python
import jax
import jax.numpy as jnp
from jax import lax
from jax.experimental import pallas as pl
from jax.experimental.pallas import tpu as pltpu
from jax.sharding import PartitionSpec as P

TILE = 128
ABLK = 4
CAP = 2
OPS = 8
SECTORS = 8
RANKS = 32
XDIM = 4
TILES = 8
NBLK = 128
BF = jnp.bfloat16
F32 = jnp.float32
VMEM_BYTES = 56 * 1024 * 1024


def interleave(rows, cols):
    r = lax.broadcasted_iota(jnp.int32, (rows, cols), 0)
    k = lax.broadcasted_iota(jnp.int32, (rows, cols), 1)
    return (k == (r % ABLK) * TILE + r // ABLK).astype(F32).astype(BF)


def deinterleave(rows, cols):
    r = lax.broadcasted_iota(jnp.int32, (rows, cols), 0)
    k = lax.broadcasted_iota(jnp.int32, (rows, cols), 1)
    return (r == (k % ABLK) * TILE + k // ABLK).astype(F32).astype(BF)


def pack_kernel(c_ref, send_ref):
    order = interleave(512, 512)
    for t in range(TILES):
        cols = slice(t * TILE, (t + 1) * TILE)
        block = c_ref[:, cols]
        turned = jnp.concatenate(
            [block[p * TILE : (p + 1) * TILE].astype(F32).T.astype(BF) for p in range(ABLK)], axis=0
        )
        both = jnp.concatenate([block, turned], axis=1)
        moved = jnp.dot(order, both, preferred_element_type=F32).astype(BF)
        for kind in range(2):
            part = moved[:, kind * TILE : (kind + 1) * TILE]
            send_ref[:, t, :, kind] = part.reshape(SECTORS, XDIM, 16, TILE)


def swap_halves(first, second):
    low = lax.broadcasted_iota(jnp.int32, first.shape, 1) < 4
    lo = jnp.where(low, first, pltpu.roll(second, 4, 1))
    hi = jnp.where(low, pltpu.roll(first, 4, 1), second)
    return lo, hi


def middle_kernel(recv_ref, mix_ref, pair_ref, wm_ref, wa_ref, out_ref, x_ref, c_ref):
    for kind in range(2):
        w_ref = (wm_ref, wa_ref)[kind]

        @pl.loop(0, SECTORS)
        def _(s):
            got = recv_ref[s, :, kind].astype(F32).reshape(16, 2, 2, 8, TILE)
            for h in range(2):
                lo, hi = swap_halves(got[:, 0, h], got[:, 1, h])
                x_ref[s, 2 * h] = lo.reshape(TILE, TILE).astype(BF)
                x_ref[s, 2 * h + 1] = hi.reshape(TILE, TILE).astype(BF)

        weights = jnp.concatenate(
            [w_ref[:, g * TILE : (g + 1) * TILE] for g in range(OPS)], axis=0
        )

        @pl.loop(0, SECTORS // 2)
        def _(half):
            s = half * 2
            for a in range(ABLK):
                pair = jnp.concatenate([x_ref[s, a], x_ref[s + 1, a]], axis=1)
                combo = jnp.dot(weights, pair, preferred_element_type=F32).astype(BF)
                for g in range(OPS):
                    rows = combo[g * TILE : (g + 1) * TILE]
                    for o in range(2):
                        dest = (s + o) ^ g if kind == 0 else s + o
                        c_ref[dest, a * TILE : (a + 1) * TILE, g * TILE : (g + 1) * TILE] = rows[
                            :, o * TILE : (o + 1) * TILE
                        ]

        @pl.loop(0, SECTORS)
        def _(d):
            if kind == 0:
                ops = jnp.concatenate([mix_ref[d ^ g, g] for g in range(OPS)], axis=0)
            else:
                ops = pair_ref[...]
            res = jnp.dot(c_ref[d], ops, preferred_element_type=F32)
            sides = []
            for h in range(2):
                first = res[2 * h * TILE : (2 * h + 1) * TILE].reshape(16, 8, TILE)
                second = res[(2 * h + 1) * TILE : (2 * h + 2) * TILE].reshape(16, 8, TILE)
                sides.append(swap_halves(first, second))
            for o in range(2):
                both = jnp.concatenate([sides[0][o][:, None], sides[1][o][:, None]], axis=1)
                out_ref[d, :, o, kind] = both.reshape(16, 16, TILE).astype(BF)


def unpack_kernel(recv_ref, beta_ref, out_ref):
    order = deinterleave(512, 512)
    for t in range(TILES):
        cols = slice(t * TILE, (t + 1) * TILE)
        both = jnp.concatenate(
            [recv_ref[:, t, :, kind].reshape(512, TILE) for kind in range(2)], axis=1
        )
        moved = jnp.dot(order, both, preferred_element_type=F32)
        for p in range(ABLK):
            rows = slice(p * TILE, (p + 1) * TILE)
            out_ref[rows, cols] = beta_ref[rows, cols] + moved[rows, :TILE] + moved[rows, TILE:].T


def call(kernel, out_shape, scratch=()):
    return pl.pallas_call(
        kernel,
        out_shape=out_shape,
        scratch_shapes=list(scratch),
        compiler_params=pltpu.CompilerParams(vmem_limit_bytes=VMEM_BYTES),
    )


def signed_weights(source, sign, pair):
    key = pair * NBLK + source
    ids = jnp.arange(OPS * NBLK, dtype=jnp.int32)
    hit = key[:, :, None] == ids[None, None, :]
    factor = (1 - 2 * sign).astype(F32)
    return jnp.sum(jnp.where(hit, factor[:, :, None], 0.0), axis=1).astype(BF)


def per_device(
    coeffs,
    beta_op,
    mix_op,
    pair_op,
    send_list,
    mix_slot,
    mix_sign,
    mix_pair,
    aa_src,
    aa_sign,
    aa_pair,
):
    tile = lax.axis_index("rows") // XDIM
    mine = lax.dynamic_index_in_dim(mix_op[0], tile, axis=1, keepdims=False)
    mix_all = lax.all_gather(mine, "sym", axis=0)

    send = call(
        pack_kernel, jax.ShapeDtypeStruct((SECTORS, TILES, XDIM, 2, 16, TILE), BF)
    )(coeffs)
    recv = lax.all_to_all(
        send.reshape(256, 32, TILE), ("sym", "rows"), split_axis=0, concat_axis=0, tiled=True
    )

    table = jnp.transpose(send_list, (1, 0, 2)).reshape(RANKS, RANKS * CAP)
    slots = jnp.arange(RANKS * CAP, dtype=jnp.int32)
    table = jnp.broadcast_to(table[:, None, :], (RANKS, ABLK, RANKS * CAP)).reshape(NBLK, 1, RANKS * CAP)
    owned = jnp.sum(jnp.where(mix_slot[:, :, None] == slots[None, None, :], table, 0), axis=2)
    source = (mix_slot // CAP) * ABLK + owned
    w_mix = signed_weights(source, mix_sign, mix_pair)
    w_alpha = signed_weights(aa_src, aa_sign, aa_pair)
    pairs = jnp.transpose(pair_op, (0, 2, 1)).reshape(OPS * TILE, TILE)

    back = call(
        middle_kernel,
        jax.ShapeDtypeStruct((SECTORS, 16, 2, 2, 16, TILE), BF),
        (
            pltpu.VMEM((SECTORS, ABLK, TILE, TILE), BF),
            pltpu.VMEM((SECTORS, 4 * TILE, OPS * TILE), BF),
        ),
    )(recv.reshape(SECTORS, RANKS, 2, 16, TILE), mix_all, pairs, w_mix, w_alpha)
    home = lax.all_to_all(
        back.reshape(256, 32, TILE), ("sym", "rows"), split_axis=0, concat_axis=0, tiled=True
    )
    beta_part = jnp.dot(coeffs, beta_op[0], preferred_element_type=F32)
    return call(unpack_kernel, jax.ShapeDtypeStruct(coeffs.shape, F32))(
        home.reshape(SECTORS, TILES, XDIM, 2, 16, TILE), beta_part
    )


def solution(mesh):
    in_specs = (
        P("rows", "sym"),
        P("sym", None, None),
        P("sym", None, None, None, None),
        P(),
        P(),
        P(),
        P(),
        P(),
        P(),
        P(),
        P(),
    )
    out_specs = P("rows", "sym")
    return jax.shard_map(
        per_device, mesh=mesh, in_specs=in_specs, out_specs=out_specs, check_vma=False
    )
```

time: 480 us -> 170 us (0.35)
  the two profiles are of different devices: /device:TPU:18 before, /device:TPU:1 now
where the time goes in v1:
time: 170 us
  waiting for transfers between devices  94.7 us (56%)
  Pallas kernels  27.6 us (16%)
  starting transfers between devices  23.7 us (14%)
  between operations  13.6 us (8%)
  other arithmetic  4.86 us (3%)
  local copies, waits for them, and re-layouts  3.13 us (2%)
  matrix products  2.56 us (2%)
    all_to_all x1, waiting for transfers between devices, per_device(): lax.all_to_all(back.reshape(256, 32, TILE), ('sym', 'rows'), split_axis=0...  50.1 us
    all_gather x1, waiting for transfers between devices, per_device(): mix_all = lax.all_gather(mine, 'sym', axis=0)  29.5 us
    pallas_call x1, Pallas kernels, per_device(): call(middle_kernel, jax.ShapeDtypeStruct((SECTORS, 16, 2, 2, 16, TILE), B...  18.7 us
    all_to_all x1, starting transfers between devices, per_device(): lax.all_to_all(send.reshape(256, 32, TILE), ('sym', 'rows'), split_axis=0...  16.7 us
    all_to_all x1, waiting for transfers between devices, per_device(): lax.all_to_all(send.reshape(256, 32, TILE), ('sym', 'rows'), split_axis=0...  15.1 us
    all_to_all x1, starting transfers between devices, per_device(): lax.all_to_all(back.reshape(256, 32, TILE), ('sym', 'rows'), split_axis=0...  6.98 us
    pallas_call x1, Pallas kernels, per_device(): call(unpack_kernel, jax.ShapeDtypeStruct(coeffs.shape, F32))  4.9 us
    reduce_sum x2, other arithmetic, signed_weights(): return jnp.sum(jnp.where(hit, factor[:, :, None], 0.0), axis=1).astype(BF)  4.76 us
  transfers between devices with their start and end apart: 3, of which 3 were waited for; matrix products, arithmetic and copies ran while one was open for 6% of the time, Pallas kernels for 0%

profile of v1, /device:TPU:1, one launch (start us, length us, event | category | flops | bytes accessed | tf_op | source)
XLA Modules:
  0.0 170.1 jit_solution(152274492047158315)
XLA Ops:
  6.5 4.1 %shard_map.109 = bf16[8,8,4,2,16,128]{5,4,3,2,1,0:T(8,128)(2,1)} custom-call(bf16[512,1024]{1,0:T(8,128)(2,1)} %c_ref.1), custom_call_target="tpu_custom_call" | custom-call | tf_op jit(solution)/shard_map/pallas_call | solution.py:150
  10.6 0.0 copy-start.9
  10.6 16.7 %all-to-all-start = ((bf16[256,32,128]{2,1,0:T(8,128)(2,1)}), bf16[256,32,128]{2,1,0:T(8,128)(2,1)}, u32[]{:S(2)}, u32[]{:S(2)}) async-start(bf16[256,32,128]{2,1,0:T(8,128)(2,1)} %bitcast.16), calls=%async_computation | async-start | bytes 4194304 | tf_op jit(solution)/shard_map/all_to_all | solution.py:153
  27.3 0.0 all-gather.3.cloned.1.call-start
  27.4 1.7 constant_dynamic-slice_fusion
  29.0 0.0 all-gather.3.cloned.1.call-update
  29.1 0.1 copy.33
  29.2 0.1 copy.34
  29.2 0.0 copy-done.4
  29.3 0.1 select_reduce_fusion.2
  29.4 0.1 copy.35
  29.5 0.1 copy.36
  29.6 0.1 copy.37
  29.7 0.1 copy.38
  29.8 0.8 copy.32
  30.7 2.1 %select_reduce_fusion.1.wa_ref = bf16[128,1024]{1,0:T(8,128)(2,1)} fusion(f32[128,8]{1,0:T(8,128)S(1)} %copy.38, s32[128,8]{1,0:T(8,128)S(1)} %copy.37), kind=kLoop, calls=%fused_computation.2 | loop fusion | flops 3014656 | bytes 270336 | tf_op jit(solution)/shard_map/reduce_sum | solution.py:130
  32.8 2.7 %select_reduce_fusion.wm_ref = bf16[128,1024]{1,0:T(8,128)(2,1)} fusion(f32[128,16]{1,0:T(8,128)S(1)} %copy.36, s32[128,16]{1,0:T(8,128)S(1)} %copy.35), kind=kLoop, calls=%fused_computation | loop fusion | flops 6160384 | bytes 278528 | tf_op jit(solution)/shard_map/reduce_sum | solution.py:130
  35.4 29.5 %all-gather.3.cloned.1.call-done = bf16[8,8,1,128,128]{4,3,2,1,0:T(8,128)(2,1)} async-done(((bf16[1,8,1,128,128]{4,3,2,1,0:T(8,128)(2,1)}), bf16[8,8,1,128,128]{4,3,2,1,0:T(8,128)(2,1)}) %all-gather.3.cloned.1.call-update) | async-done | bytes 2097168 | tf_op jit(solution)/shard_map/all_gather | solution.py:148
  65.0 15.1 %all-to-all-done = bf16[256,32,128]{2,1,0:T(8,128)(2,1)} async-done(((bf16[256,32,128]{2,1,0:T(8,128)(2,1)}), bf16[256,32,128]{2,1,0:T(8,128)(2,1)}, u32[]{:S(2)}, u32[]{:S(2)}) %all-to-all-start) | async-done | bytes 2097184 | tf_op jit(solution)/shard_map/all_to_all | solution.py:153
  80.1 18.7 %shard_map.110 = bf16[8,16,2,2,16,128]{5,4,3,2,1,0:T(8,128)(2,1)} custom-call(bf16[8,32,2,16,128]{4,3,2,1,0:T(8,128)(2,1)} %bitcast.1.recv_ref, bf16[8,8,128,128]{3,2,1,0:T(8,128)(2,1)} %bitcast.17, bf16[1024,128]{1,0:T(8,128)(2,1)} %bitcast.18, bf16[128,1024]{1,0:T(8,128)(2,1)} %select_reduce_fusion.wm_ref, bf16[128,1024]{1,0:T(8,128)(2,1)} %select_reduce_fusion.1.wa_ref), custom_call_target="tpu_custom_call" | custom-call | tf_op jit(solution)/shard_map/pallas_call | solution.py:166
  98.7 7.0 %all-to-all-start.1 = ((bf16[256,32,128]{2,1,0:T(8,128)(2,1)}), bf16[256,32,128]{2,1,0:T(8,128)(2,1)}, u32[]{:S(2)}, u32[]{:S(2)}) async-start(bf16[256,32,128]{2,1,0:T(8,128)(2,1)} %bitcast.15), calls=%async_computation.1 | async-start | bytes 4194304 | tf_op jit(solution)/shard_map/all_to_all | solution.py:174
  105.7 2.6 %fusion.beta_ref = f32[512,1024]{1,0:T(8,128)} fusion(bf16[512,1024]{1,0:T(8,128)(2,1)S(1)} %copy-done.1, bf16[1,1024,1024]{2,1,0:T(8,128)(2,1)S(1)} %copy-done), kind=kOutput, calls=%fused_computation.4 | convolution fusion | flops 1073741824 | bytes 5242880 | tf_op jit(solution)/shard_map/dot_general | solution.py:177
  108.3 50.1 %all-to-all-done.1 = bf16[256,32,128]{2,1,0:T(8,128)(2,1)} async-done(((bf16[256,32,128]{2,1,0:T(8,128)(2,1)}), bf16[256,32,128]{2,1,0:T(8,128)(2,1)}, u32[]{:S(2)}, u32[]{:S(2)}) %all-to-all-start.1) | async-done | bytes 2097184 | tf_op jit(solution)/shard_map/all_to_all | solution.py:174
  158.4 4.9 %shard_map.111 = f32[512,1024]{1,0:T(8,128)} custom-call(bf16[8,8,4,2,16,128]{5,4,3,2,1,0:T(8,128)(2,1)} %bitcast.9.recv_ref, f32[512,1024]{1,0:T(8,128)} %fusion.beta_ref), custom_call_target="tpu_custom_call" | custom-call | tf_op jit(solution)/shard_map/pallas_call | solution.py:178
  (23 shorter events, 0.1 us)
Async XLA Ops:
  6.5 99.2 %copy-start = (bf16[1,1024,1024]{2,1,0:T(8,128)(2,1)S(1)}, bf16[1,1024,1024]{2,1,0:T(8,128)(2,1)}, u32[]{:S(2)}) copy-start(bf16[1,1024,1024]{2,1,0:T(8,128)(2,1)} %param.12) | copy-start | bytes 6291460
  10.6 18.5 %copy-start.3 = (s32[32,32,2]{1,2,0:T(2,128)S(1)}, s32[32,32,2]{1,2,0:T(2,128)}, u32[]{:S(2)}) copy-start(s32[32,32,2]{1,2,0:T(2,128)} %param.15) | copy-start | bytes 24580
  10.6 18.7 %copy-start.4 = (s32[128,16]{0,1:T(8,128)S(1)}, s32[128,16]{0,1:T(8,128)}, u32[]{:S(2)}) copy-start(s32[128,16]{0,1:T(8,128)} %param.16) | copy-start | bytes 24580
  10.6 18.7 %copy-start.6 = (s32[128,16]{0,1:T(8,128)S(1)}, s32[128,16]{0,1:T(8,128)}, u32[]{:S(2)}) copy-start(s32[128,16]{0,1:T(8,128)} %param.18) | copy-start | bytes 24580
  10.6 18.9 %copy-start.5 = (s32[128,16]{0,1:T(8,128)S(1)}, s32[128,16]{0,1:T(8,128)}, u32[]{:S(2)}) copy-start(s32[128,16]{0,1:T(8,128)} %param.17) | copy-start | bytes 24580
  10.6 19.0 %copy-start.7 = (s32[128,8]{0,1:T(8,128)S(1)}, s32[128,8]{0,1:T(8,128)}, u32[]{:S(2)}) copy-start(s32[128,8]{0,1:T(8,128)} %param.19) | copy-start | bytes 12292
  10.6 19.0 %copy-start.8 = (s32[128,8]{0,1:T(8,128)S(1)}, s32[128,8]{0,1:T(8,128)}, u32[]{:S(2)}) copy-start(s32[128,8]{0,1:T(8,128)} %param.21) | copy-start | bytes 12292
  10.6 19.1 %copy-start.9 = (s32[128,8]{0,1:T(8,128)S(1)}, s32[128,8]{0,1:T(8,128)}, u32[]{:S(2)}) copy-start(s32[128,8]{0,1:T(8,128)} %param.20) | copy-start | bytes 12292
  10.6 19.2 %copy-start.2 = (bf16[8,128,128]{2,1,0:T(8,128)(2,1)S(1)}, bf16[8,128,128]{2,1,0:T(8,128)(2,1)}, u32[]{:S(2)}) copy-start(bf16[8,128,128]{2,1,0:T(8,128)(2,1)} %param.14) | copy-start | bytes 786436
  10.6 69.4 %all-to-all-start = ((bf16[256,32,128]{2,1,0:T(8,128)(2,1)}), bf16[256,32,128]{2,1,0:T(8,128)(2,1)}, u32[]{:S(2)}, u32[]{:S(2)}) async-start(bf16[256,32,128]{2,1,0:T(8,128)(2,1)} %bitcast.16), calls=%async_computation | async-start | bytes 4194304 | tf_op jit(solution)/shard_map/all_to_all | solution.py:153
  27.3 37.7 %all-gather.3.cloned.1.call-start = ((), (), s32[]{:S(2)}) async-start(), calls=%async_computation.2 | async-start | bytes 2359296 | tf_op jit(solution)/shard_map/all_gather | solution.py:148
  98.7 7.0 %copy-start.1 = (bf16[512,1024]{1,0:T(8,128)(2,1)S(1)}, bf16[512,1024]{1,0:T(8,128)(2,1)}, u32[]{:S(2)}) copy-start(bf16[512,1024]{1,0:T(8,128)(2,1)} %c_ref.1) | copy-start | bytes 3145732
  98.7 59.6 %all-to-all-start.1 = ((bf16[256,32,128]{2,1,0:T(8,128)(2,1)}), bf16[256,32,128]{2,1,0:T(8,128)(2,1)}, u32[]{:S(2)}, u32[]{:S(2)}) async-start(bf16[256,32,128]{2,1,0:T(8,128)(2,1)} %bitcast.15), calls=%async_computation.1 | async-start | bytes 4194304 | tf_op jit(solution)/shard_map/all_to_all | solution.py:174
Sparse Core Ops, SparseCore 0:
  30.0 34.9 all-gather.2

commit v2 on v1

--- a/solution.py
+++ b/solution.py
@@ -53,7 +53,13 @@
     return lo, hi
 
 
-def middle_kernel(recv_ref, mix_ref, pair_ref, wm_ref, wa_ref, out_ref, x_ref, c_ref):
+def middle_kernel(
+    recv_ref, same_ref, other_ref, pair_ref, wm_ref, wa_ref, out_ref, x_ref, c_ref, mix_ref
+):
+    sector = lax.axis_index("sym")
+    for k in range(SECTORS // 2):
+        mix_ref[2 * k] = same_ref[k]
+        mix_ref[2 * k + 1] = other_ref[k]
     for kind in range(2):
         w_ref = (wm_ref, wa_ref)[kind]
 
@@ -86,7 +92,7 @@
         @pl.loop(0, SECTORS)
         def _(d):
             if kind == 0:
-                ops = jnp.concatenate([mix_ref[d ^ g, g] for g in range(OPS)], axis=0)
+                ops = jnp.concatenate([mix_ref[sector ^ d ^ g, g] for g in range(OPS)], axis=0)
             else:
                 ops = pair_ref[...]
             res = jnp.dot(c_ref[d], ops, preferred_element_type=F32)
@@ -128,6 +134,10 @@
     hit = key[:, :, None] == ids[None, None, :]
     factor = (1 - 2 * sign).astype(F32)
     return jnp.sum(jnp.where(hit, factor[:, :, None], 0.0), axis=1).astype(BF)
+
+
+def swapped(array, mask):
+    return lax.ppermute(array, "sym", [(s, s ^ mask) for s in range(SECTORS)])
 
 
 def per_device(
@@ -145,7 +155,8 @@
 ):
     tile = lax.axis_index("rows") // XDIM
     mine = lax.dynamic_index_in_dim(mix_op[0], tile, axis=1, keepdims=False)
-    mix_all = lax.all_gather(mine, "sym", axis=0)
+    same = jnp.stack([mine] + [swapped(mine, k) for k in (2, 4, 6)])
+    other = swapped(same, 1)
 
     send = call(
         pack_kernel, jax.ShapeDtypeStruct((SECTORS, TILES, XDIM, 2, 16, TILE), BF)
@@ -169,8 +180,9 @@
         (
             pltpu.VMEM((SECTORS, ABLK, TILE, TILE), BF),
             pltpu.VMEM((SECTORS, 4 * TILE, OPS * TILE), BF),
+            pltpu.VMEM((SECTORS, OPS, TILE, TILE), BF),
         ),
-    )(recv.reshape(SECTORS, RANKS, 2, 16, TILE), mix_all, pairs, w_mix, w_alpha)
+    )(recv.reshape(SECTORS, RANKS, 2, 16, TILE), same, other, pairs, w_mix, w_alpha)
     home = lax.all_to_all(
         back.reshape(256, 32, TILE), ("sym", "rows"), split_axis=0, concat_axis=0, tiled=True
     )

time: 170 us -> 157 us (0.924)
  between operations: 13.6 us -> 0.19 us
  waiting for transfers between devices: 94.7 us -> 86.3 us
  starting transfers between devices: 23.7 us -> 29.7 us
    all_gather x1 -> x0, waiting for transfers between devices: 29.5 us -> none  [per_device(): mix_all = lax.all_gather(mine, 'sym', axis=0)]
    ppermute x0 -> x4, waiting for transfers between devices: none -> 21.4 us  [swapped(): return lax.ppermute(array, 'sym', [(s, s ^ mask) for s in range(SECTORS)])]
    ppermute x0 -> x4, starting transfers between devices: none -> 6.1 us  [swapped(): return lax.ppermute(array, 'sym', [(s, s ^ mask) for s in range(SECTORS)])]
  transfers between devices with their start and end apart: 3 -> 6, of which waited for: 3 -> 4; matrix products, arithmetic and copies ran while one was open for 6% -> 8% of each run, Pallas kernels for 0% -> 0%
where the time goes in v2:
time: 157 us
  waiting for transfers between devices  86.3 us (55%)
  starting transfers between devices  29.7 us (19%)
  Pallas kernels  27.8 us (18%)
  other arithmetic  6.07 us (4%)
  local copies, waits for them, and re-layouts  4.24 us (3%)
  matrix products  2.56 us (2%)
    all_to_all x1, waiting for transfers between devices, per_device(): lax.all_to_all(back.reshape(256, 32, TILE), ('sym', 'rows'), split_axis=0...  50 us
    ppermute x4, waiting for transfers between devices, swapped(): return lax.ppermute(array, 'sym', [(s, s ^ mask) for s in range(SECTORS)])  21.4 us
    pallas_call x1, Pallas kernels, per_device(): call(middle_kernel, jax.ShapeDtypeStruct((SECTORS, 16, 2, 2, 16, TILE), B...  18.8 us
    all_to_all x1, starting transfers between devices, per_device(): lax.all_to_all(send.reshape(256, 32, TILE), ('sym', 'rows'), split_axis=0...  16.6 us
    all_to_all x1, waiting for transfers between devices, per_device(): lax.all_to_all(send.reshape(256, 32, TILE), ('sym', 'rows'), split_axis=0...  14.8 us
    all_to_all x1, starting transfers between devices, per_device(): lax.all_to_all(back.reshape(256, 32, TILE), ('sym', 'rows'), split_axis=0...  6.98 us
    ppermute x4, starting transfers between devices, swapped(): return lax.ppermute(array, 'sym', [(s, s ^ mask) for s in range(SECTORS)])  6.1 us
    pallas_call x1, Pallas kernels, per_device(): call(unpack_kernel, jax.ShapeDtypeStruct(coeffs.shape, F32))  4.9 us
  transfers between devices with their start and end apart: 6, of which 4 were waited for; matrix products, arithmetic and copies ran while one was open for 8% of the time, Pallas kernels for 0%

profile of v2, /device:TPU:1, one launch (start us, length us, event | category | flops | bytes accessed | tf_op | source)
XLA Modules:
  0.0 156.8 jit_solution(3145554117134241637)
XLA Ops:
  0.0 4.1 %shard_map.109 = bf16[8,8,4,2,16,128]{5,4,3,2,1,0:T(8,128)(2,1)} custom-call(bf16[512,1024]{1,0:T(8,128)(2,1)} %c_ref.1), custom_call_target="tpu_custom_call" | custom-call | tf_op jit(solution)/shard_map/pallas_call | solution.py:161
  4.1 16.6 %all-to-all-start = ((bf16[256,32,128]{2,1,0:T(8,128)(2,1)}), bf16[256,32,128]{2,1,0:T(8,128)(2,1)}, u32[]{:S(2)}, u32[]{:S(2)}) async-start(bf16[256,32,128]{2,1,0:T(8,128)(2,1)} %bitcast.22), calls=%async_computation | async-start | bytes 4194304 | tf_op jit(solution)/shard_map/all_to_all | solution.py:164
  20.8 1.1 dynamic-slice_bitcast_fusion.1
  21.8 1.4 collective-permute-start
  23.3 2.5 %collective-permute-start.1 = (bf16[8,128,128]{2,1,0:T(8,128)(2,1)S(1)}, bf16[8,128,128]{2,1,0:T(8,128)(2,1)S(1)}, u32[]{:S(2)}, u32[]{:S(2)}) collective-permute-start(bf16[8,128,128]{2,1,0:T(8,128)(2,1)S(1)} %get-tuple-element.6), channel_id=1, source_target_pairs={{0,128},{32,160},{64,192},{96,224},{128,0},{160,32},{192,64},{224,... | collective-permute-start | bytes 786440 | tf_op jit(solution)/shard_map/ppermute | solution.py:140
  26.1 8.9 %collective-permute-done = bf16[8,128,128]{2,1,0:T(8,128)(2,1)S(1)} collective-permute-done((bf16[8,128,128]{2,1,0:T(8,128)(2,1)S(1)}, bf16[8,128,128]{2,1,0:T(8,128)(2,1)S(1)}, u32[]{:S(2)}, u32[]{:S(2)}) %collective-permute-start) | collective-permute-done | bytes 262176 | tf_op jit(solution)/shard_map/ppermute | solution.py:140
  34.9 12.5 %collective-permute-done.1 = bf16[8,128,128]{2,1,0:T(8,128)(2,1)S(1)} collective-permute-done((bf16[8,128,128]{2,1,0:T(8,128)(2,1)S(1)}, bf16[8,128,128]{2,1,0:T(8,128)(2,1)S(1)}, u32[]{:S(2)}, u32[]{:S(2)}) %collective-permute-start.1) | collective-permute-done | bytes 262176 | tf_op jit(solution)/shard_map/ppermute | solution.py:140
  47.5 0.7 copy-done.4
  48.1 0.1 copy-done.5
  48.3 1.2 pad_maximum_fusion.same_ref
  49.5 2.2 %collective-permute-start.3 = (bf16[4,8,128,128]{3,2,1,0:T(8,128)(2,1)S(1)}, bf16[4,8,128,128]{3,2,1,0:T(8,128)(2,1)}, u32[]{:S(2)}, u32[]{:S(2)}) collective-permute-start(bf16[4,8,128,128]{3,2,1,0:T(8,128)(2,1)S(1)} %pad_maximum_fusion.same_ref), channel_id=1, source_target_pairs={{0,32},{32,0},{64,96},{96,64},{128,160},{160,128},{192,224},{224,1... | collective-permute-start | bytes 3145736 | tf_op jit(solution)/shard_map/ppermute | solution.py:140
  51.7 0.1 copy.27
  51.8 0.1 copy.28
  51.9 0.1 copy.29
  52.0 0.1 copy.30
  52.1 1.8 %copy.24 = bf16[8,128,128]{2,1,0:T(8,128)(2,1)} copy(bf16[8,128,128]{1,2,0:T(8,128)(2,1)} %bitcast.25) | data formatting | bytes 524288 | tf_op jit(solution)/shard_map/transpose | solution.py:175
  53.9 2.1 %select_reduce_fusion.1.wa_ref = bf16[128,1024]{1,0:T(8,128)(2,1)} fusion(f32[128,8]{1,0:T(8,128)S(1)} %copy.30, s32[128,8]{1,0:T(8,128)S(1)} %copy.29), kind=kLoop, calls=%fused_computation.2 | loop fusion | flops 3014656 | bytes 270336 | tf_op jit(solution)/shard_map/reduce_sum | solution.py:136
  56.0 2.7 %select_reduce_fusion.wm_ref = bf16[128,1024]{1,0:T(8,128)(2,1)} fusion(f32[128,16]{1,0:T(8,128)S(1)} %copy.28, s32[128,16]{1,0:T(8,128)S(1)} %copy.27), kind=kLoop, calls=%fused_computation | loop fusion | flops 6160384 | bytes 278528 | tf_op jit(solution)/shard_map/reduce_sum | solution.py:136
  58.6 14.8 %all-to-all-done = bf16[256,32,128]{2,1,0:T(8,128)(2,1)} async-done(((bf16[256,32,128]{2,1,0:T(8,128)(2,1)}), bf16[256,32,128]{2,1,0:T(8,128)(2,1)}, u32[]{:S(2)}, u32[]{:S(2)}) %all-to-all-start) | async-done | bytes 2097184 | tf_op jit(solution)/shard_map/all_to_all | solution.py:164
  73.5 18.8 %shard_map.110 = bf16[8,16,2,2,16,128]{5,4,3,2,1,0:T(8,128)(2,1)} custom-call(bf16[8,32,2,16,128]{4,3,2,1,0:T(8,128)(2,1)} %bitcast.1.recv_ref, bf16[4,8,128,128]{3,2,1,0:T(8,128)(2,1)} %copy-done.1, bf16[4,8,128,128]{3,2,1,0:T(8,128)(2,1)} %collective-permute-done.3.other_ref, bf16[1024,128]{1,0:T(8,128)(2,1)} %bitcast.23, ...), custom_call_target="tpu_custom_call" | custom-call | tf_op jit(solution)/shard_map/pallas_call | solution.py:177
  92.3 7.0 %all-to-all-start.1 = ((bf16[256,32,128]{2,1,0:T(8,128)(2,1)}), bf16[256,32,128]{2,1,0:T(8,128)(2,1)}, u32[]{:S(2)}, u32[]{:S(2)}) async-start(bf16[256,32,128]{2,1,0:T(8,128)(2,1)} %bitcast.21), calls=%async_computation.1 | async-start | bytes 4194304 | tf_op jit(solution)/shard_map/all_to_all | solution.py:186
  99.3 2.6 %fusion.beta_ref = f32[512,1024]{1,0:T(8,128)} fusion(bf16[512,1024]{1,0:T(8,128)(2,1)S(1)} %copy-done.2, bf16[1,1024,1024]{2,1,0:T(8,128)(2,1)S(1)} %copy-done), kind=kOutput, calls=%fused_computation.4 | convolution fusion | flops 1073741824 | bytes 5242880 | tf_op jit(solution)/shard_map/dot_general | solution.py:189
  101.9 50.0 %all-to-all-done.1 = bf16[256,32,128]{2,1,0:T(8,128)(2,1)} async-done(((bf16[256,32,128]{2,1,0:T(8,128)(2,1)}), bf16[256,32,128]{2,1,0:T(8,128)(2,1)}, u32[]{:S(2)}, u32[]{:S(2)}) %all-to-all-start.1) | async-done | bytes 2097184 | tf_op jit(solution)/shard_map/all_to_all | solution.py:186
  151.9 4.9 %shard_map.111 = f32[512,1024]{1,0:T(8,128)} custom-call(bf16[8,8,4,2,16,128]{5,4,3,2,1,0:T(8,128)(2,1)} %bitcast.13.recv_ref, f32[512,1024]{1,0:T(8,128)} %fusion.beta_ref), custom_call_target="tpu_custom_call" | custom-call | tf_op jit(solution)/shard_map/pallas_call | solution.py:190
  (35 shorter events, 0.4 us)
Async XLA Ops:
  0.0 99.3 %copy-start = (bf16[1,1024,1024]{2,1,0:T(8,128)(2,1)S(1)}, bf16[1,1024,1024]{2,1,0:T(8,128)(2,1)}, u32[]{:S(2)}) copy-start(bf16[1,1024,1024]{2,1,0:T(8,128)(2,1)} %param.12) | copy-start | bytes 6291460
  4.1 21.7 %copy-start.6 = (s32[32,32,2]{1,2,0:T(2,128)S(1)}, s32[32,32,2]{1,2,0:T(2,128)}, u32[]{:S(2)}) copy-start(s32[32,32,2]{1,2,0:T(2,128)} %param.15) | copy-start | bytes 24580
  4.1 21.9 %copy-start.7 = (s32[128,16]{0,1:T(8,128)S(1)}, s32[128,16]{0,1:T(8,128)}, u32[]{:S(2)}) copy-start(s32[128,16]{0,1:T(8,128)} %param.16) | copy-start | bytes 24580
  4.1 22.0 %copy-start.9 = (s32[128,16]{0,1:T(8,128)S(1)}, s32[128,16]{0,1:T(8,128)}, u32[]{:S(2)}) copy-start(s32[128,16]{0,1:T(8,128)} %param.18) | copy-start | bytes 24580
  4.1 69.4 %all-to-all-start = ((bf16[256,32,128]{2,1,0:T(8,128)(2,1)}), bf16[256,32,128]{2,1,0:T(8,128)(2,1)}, u32[]{:S(2)}, u32[]{:S(2)}) async-start(bf16[256,32,128]{2,1,0:T(8,128)(2,1)} %bitcast.22), calls=%async_computation | async-start | bytes 4194304 | tf_op jit(solution)/shard_map/all_to_all | solution.py:164
  20.7 30.9 %copy-start.8 = (s32[128,16]{0,1:T(8,128)S(1)}, s32[128,16]{0,1:T(8,128)}, u32[]{:S(2)}) copy-start(s32[128,16]{0,1:T(8,128)} %param.17) | copy-start | bytes 24580
  20.7 31.1 %copy-start.10 = (s32[128,8]{0,1:T(8,128)S(1)}, s32[128,8]{0,1:T(8,128)}, u32[]{:S(2)}) copy-start(s32[128,8]{0,1:T(8,128)} %param.19) | copy-start | bytes 12292
  20.7 31.1 %copy-start.11 = (s32[128,8]{0,1:T(8,128)S(1)}, s32[128,8]{0,1:T(8,128)}, u32[]{:S(2)}) copy-start(s32[128,8]{0,1:T(8,128)} %param.21) | copy-start | bytes 12292
  20.8 31.3 %copy-start.12 = (s32[128,8]{0,1:T(8,128)S(1)}, s32[128,8]{0,1:T(8,128)}, u32[]{:S(2)}) copy-start(s32[128,8]{0,1:T(8,128)} %param.20) | copy-start | bytes 12292
  21.8 13.1 %collective-permute-start = (bf16[8,128,128]{2,1,0:T(8,128)(2,1)S(1)}, bf16[8,128,128]{2,1,0:T(8,128)(2,1)S(1)}, u32[]{:S(2)}, u32[]{:S(2)}) collective-permute-start(bf16[8,128,128]{2,1,0:T(8,128)(2,1)S(1)} %get-tuple-element.6), channel_id=1, source_target_pairs={{0,64},{32,96},{64,0},{96,32},{128,192},{160,224},{192,128},{224,1... | collective-permute-start | bytes 786440 | tf_op jit(solution)/shard_map/ppermute | solution.py:140
  23.3 24.2 %collective-permute-start.1 = (bf16[8,128,128]{2,1,0:T(8,128)(2,1)S(1)}, bf16[8,128,128]{2,1,0:T(8,128)(2,1)S(1)}, u32[]{:S(2)}, u32[]{:S(2)}) collective-permute-start(bf16[8,128,128]{2,1,0:T(8,128)(2,1)S(1)} %get-tuple-element.6), channel_id=1, source_target_pairs={{0,128},{32,160},{64,192},{96,224},{128,0},{160,32},{192,64},{224,... | collective-permute-start | bytes 786440 | tf_op jit(solution)/shard_map/ppermute | solution.py:140
  25.7 21.7 %collective-permute-start.2 = (bf16[8,128,128]{2,1,0:T(8,128)(2,1)S(1)}, bf16[8,128,128]{2,1,0:T(8,128)(2,1)S(1)}, u32[]{:S(2)}, u32[]{:S(2)}) collective-permute-start(bf16[8,128,128]{2,1,0:T(8,128)(2,1)S(1)} %get-tuple-element.6), channel_id=1, source_target_pairs={{0,192},{32,224},{64,128},{96,160},{128,64},{160,96},{192,0},{224,... | collective-permute-start | bytes 786440 | tf_op jit(solution)/shard_map/ppermute | solution.py:140
  34.9 12.5 %copy-start.3 = (bf16[8,128,128]{2,1,0:T(8,128)(2,1)}, bf16[8,128,128]{2,1,0:T(8,128)(2,1)S(1)}, u32[]{:S(2)}) copy-start(bf16[8,128,128]{2,1,0:T(8,128)(2,1)S(1)} %collective-permute-done) | copy-start | bytes 786436
  47.5 0.7 copy-start.4
  47.5 0.8 copy-start.5
  49.5 24.0 %copy-start.1 = (bf16[4,8,128,128]{3,2,1,0:T(8,128)(2,1)}, bf16[4,8,128,128]{3,2,1,0:T(8,128)(2,1)S(1)}, u32[]{:S(2)}) copy-start(bf16[4,8,128,128]{3,2,1,0:T(8,128)(2,1)S(1)} %pad_maximum_fusion.same_ref) | copy-start | bytes 3145732
  49.5 9.1 %collective-permute-start.3 = (bf16[4,8,128,128]{3,2,1,0:T(8,128)(2,1)S(1)}, bf16[4,8,128,128]{3,2,1,0:T(8,128)(2,1)}, u32[]{:S(2)}, u32[]{:S(2)}) collective-permute-start(bf16[4,8,128,128]{3,2,1,0:T(8,128)(2,1)S(1)} %pad_maximum_fusion.same_ref), channel_id=1, source_target_pairs={{0,32},{32,0},{64,96},{96,64},{128,160},{160,128},{192,224},{224,1... | collective-permute-start | bytes 3145736 | tf_op jit(solution)/shard_map/ppermute | solution.py:140
  92.3 7.0 %copy-start.2 = (bf16[512,1024]{1,0:T(8,128)(2,1)S(1)}, bf16[512,1024]{1,0:T(8,128)(2,1)}, u32[]{:S(2)}) copy-start(bf16[512,1024]{1,0:T(8,128)(2,1)} %c_ref.1) | copy-start | bytes 3145732
  92.3 59.6 %all-to-all-start.1 = ((bf16[256,32,128]{2,1,0:T(8,128)(2,1)}), bf16[256,32,128]{2,1,0:T(8,128)(2,1)}, u32[]{:S(2)}, u32[]{:S(2)}) async-start(bf16[256,32,128]{2,1,0:T(8,128)(2,1)} %bitcast.21), calls=%async_computation.1 | async-start | bytes 4194304 | tf_op jit(solution)/shard_map/all_to_all | solution.py:186

commit v3 on v2

v3 whole, which is shorter than its diff:
```python
import jax
import jax.numpy as jnp
from jax import lax
from jax.experimental import pallas as pl
from jax.experimental.pallas import tpu as pltpu
from jax.sharding import Mesh, PartitionSpec as P

TILE = 128
ABLK = 4
CAP = 2
OPS = 8
SECTORS = 8
RANKS = 32
XDIM = 4
TILES = 8
NBLK = 128
BF = jnp.bfloat16
F32 = jnp.float32
VMEM_BYTES = 56 * 1024 * 1024


def interleave(rows, cols):
    r = lax.broadcasted_iota(jnp.int32, (rows, cols), 0)
    k = lax.broadcasted_iota(jnp.int32, (rows, cols), 1)
    return (k == (r % ABLK) * TILE + r // ABLK).astype(F32).astype(BF)


def deinterleave(rows, cols):
    r = lax.broadcasted_iota(jnp.int32, (rows, cols), 0)
    k = lax.broadcasted_iota(jnp.int32, (rows, cols), 1)
    return (r == (k % ABLK) * TILE + k // ABLK).astype(F32).astype(BF)


def pack_kernel(c_ref, send_ref):
    order = interleave(512, 512)
    for t in range(0, TILES, 2):
        turned = []
        for u in (t, t + 1):
            block = c_ref[:, u * TILE : (u + 1) * TILE].astype(F32)
            turned.append(
                jnp.concatenate(
                    [block[p * TILE : (p + 1) * TILE].T.astype(BF) for p in range(ABLK)], axis=0
                )
            )
        both = jnp.concatenate(turned, axis=1)
        moved = jnp.dot(order, both, preferred_element_type=F32).astype(BF)
        send_ref[t] = moved[:, :TILE]
        send_ref[t + 1] = moved[:, TILE:]


def swap_halves(first, second):
    low = lax.broadcasted_iota(jnp.int32, first.shape, 1) < 4
    lo = jnp.where(low, first, pltpu.roll(second, 4, 1))
    hi = jnp.where(low, pltpu.roll(first, 4, 1), second)
    return lo, hi


def blocks_of(recv_ref, c):
    got = recv_ref[:, c].astype(F32).reshape(16, 2, 2, 8, TILE)
    blocks = []
    for h in range(2):
        blocks += [b.reshape(TILE, TILE) for b in swap_halves(got[:, 0, h], got[:, 1, h])]
    return blocks


def regroup(blocks, out_ref, c):
    sides = []
    for h in range(2):
        first = blocks[2 * h].reshape(16, 8, TILE)
        second = blocks[2 * h + 1].reshape(16, 8, TILE)
        sides.append(swap_halves(first, second))
    for o in range(2):
        both = jnp.concatenate([sides[0][o][:, None], sides[1][o][:, None]], axis=1)
        out_ref[:, o, c] = both.reshape(16, 16, TILE).astype(BF)


def turn_kernel(recv_ref, out_ref):
    @pl.loop(0, TILES)
    def _(c):
        regroup([b.T for b in blocks_of(recv_ref, c)], out_ref, c)


def stacked(w_ref):
    return jnp.concatenate([w_ref[:, g * TILE : (g + 1) * TILE] for g in range(OPS)], axis=0)


def combine(weights, x_ref, c_ref, flip):
    @pl.loop(0, SECTORS // 2)
    def _(half):
        s = half * 2
        for a in range(ABLK):
            pair = jnp.concatenate([x_ref[s, a], x_ref[s + 1, a]], axis=1)
            combo = jnp.dot(weights, pair, preferred_element_type=F32).astype(BF)
            for g in range(OPS):
                rows = combo[g * TILE : (g + 1) * TILE]
                for o in range(2):
                    dest = (s + o) ^ g if flip else s + o
                    c_ref[dest, a * TILE : (a + 1) * TILE, g * TILE : (g + 1) * TILE] = rows[
                        :, o * TILE : (o + 1) * TILE
                    ]


def alpha_kernel(recv_ref, pair_ref, w_ref, out_ref, x_ref, c_ref):
    @pl.loop(0, SECTORS)
    def _(c):
        for a, block in enumerate(blocks_of(recv_ref, c)):
            x_ref[c, a] = block.astype(BF)

    combine(stacked(w_ref), x_ref, c_ref, False)

    @pl.loop(0, SECTORS)
    def _(c):
        res = jnp.dot(c_ref[c], pair_ref[...], preferred_element_type=F32)
        regroup([res[a * TILE : (a + 1) * TILE].T for a in range(ABLK)], out_ref, c)


def landed(land_ref, s, order):
    both = jnp.concatenate([land_ref[s], land_ref[s + 1]], axis=1)
    return jnp.dot(order, both, preferred_element_type=F32)


def mixed_kernel(land_ref, same_ref, other_ref, w_ref, res_ref, x_ref, c_ref, mix_ref):
    sector = lax.axis_index("sym")
    for k in range(SECTORS // 2):
        mix_ref[2 * k] = same_ref[k]
        mix_ref[2 * k + 1] = other_ref[k]
    order = deinterleave(512, 512)

    @pl.loop(0, SECTORS // 2)
    def _(half):
        moved = landed(land_ref, 2 * half, order)
        for a in range(ABLK):
            for o in range(2):
                block = moved[a * TILE : (a + 1) * TILE, o * TILE : (o + 1) * TILE]
                x_ref[2 * half + o, a] = block.T.astype(BF)

    combine(stacked(w_ref), x_ref, c_ref, True)

    @pl.loop(0, SECTORS)
    def _(d):
        ops = jnp.concatenate([mix_ref[sector ^ d ^ g, g] for g in range(OPS)], axis=0)
        res_ref[d] = jnp.dot(c_ref[d], ops, preferred_element_type=F32)


def merge_kernel(res_ref, land_ref, out_ref):
    order = deinterleave(512, 512)

    @pl.loop(0, SECTORS // 2)
    def _(half):
        moved = landed(land_ref, 2 * half, order)
        for o in range(2):
            d = 2 * half + o
            blocks = []
            for a in range(ABLK):
                rows = slice(a * TILE, (a + 1) * TILE)
                blocks.append(res_ref[d, rows] + moved[rows, o * TILE : (o + 1) * TILE].T)
            sides = []
            for h in range(2):
                first = blocks[2 * h].reshape(16, 8, TILE)
                second = blocks[2 * h + 1].reshape(16, 8, TILE)
                sides.append(swap_halves(first, second))
            for side in range(2):
                both = jnp.concatenate([sides[0][side][:, None], sides[1][side][:, None]], axis=1)
                out_ref[d, :, side] = both.reshape(16, 16, TILE).astype(BF)


def unpack_kernel(recv_ref, beta_ref, out_ref):
    order = deinterleave(512, 512)
    for t in range(0, TILES, 2):
        cols = slice(t * TILE, (t + 2) * TILE)
        both = jnp.concatenate(
            [recv_ref[:, u].reshape(512, TILE) for u in (t, t + 1)], axis=1
        )
        out_ref[:, cols] = beta_ref[:, cols] + jnp.dot(order, both, preferred_element_type=F32)


def call(kernel, out_shape, scratch=()):
    return pl.pallas_call(
        kernel,
        out_shape=out_shape,
        scratch_shapes=list(scratch),
        compiler_params=pltpu.CompilerParams(vmem_limit_bytes=VMEM_BYTES),
    )


def signed_weights(source, sign, pair):
    key = pair * NBLK + source
    ids = jnp.arange(OPS * NBLK, dtype=jnp.int32)
    hit = key[:, :, None] == ids[None, None, :]
    factor = (1 - 2 * sign).astype(F32)
    return jnp.sum(jnp.where(hit, factor[:, :, None], 0.0), axis=1).astype(BF)


def swapped(array, mask):
    return lax.ppermute(array, "sym", [(s, s ^ mask) for s in range(SECTORS)])


def per_device(
    coeffs,
    beta_op,
    mix_op,
    pair_op,
    send_list,
    mix_slot,
    mix_sign,
    mix_pair,
    aa_src,
    aa_sign,
    aa_pair,
):
    tile = lax.axis_index("z")
    mine = lax.dynamic_index_in_dim(mix_op[0], tile, axis=1, keepdims=False)
    same = jnp.stack([mine] + [swapped(mine, k) for k in (2, 4, 6)])
    other = swapped(same, 1)

    send = call(pack_kernel, jax.ShapeDtypeStruct((TILES, 512, TILE), BF))(coeffs)
    recv = exchange(send.reshape(32, TILE, TILE), ("z", "x"))
    recv = recv.reshape(RANKS, TILES, 16, TILE)
    grouped = jax.ShapeDtypeStruct((16, 2, TILES, 16, TILE), BF)
    turned = call(turn_kernel, grouped)(recv)
    land = exchange(turned.reshape(32, TILE, TILE), ("sym", "x"))

    table = jnp.transpose(send_list, (1, 0, 2)).reshape(RANKS, RANKS * CAP)
    slots = jnp.arange(RANKS * CAP, dtype=jnp.int32)
    table = jnp.broadcast_to(table[:, None, :], (RANKS, ABLK, RANKS * CAP)).reshape(NBLK, 1, RANKS * CAP)
    owned = jnp.sum(jnp.where(mix_slot[:, :, None] == slots[None, None, :], table, 0), axis=2)
    source = (mix_slot // CAP) * ABLK + owned
    w_mix = signed_weights(source, mix_sign, mix_pair)
    w_alpha = signed_weights(aa_src, aa_sign, aa_pair)
    pairs = jnp.transpose(pair_op, (0, 2, 1)).reshape(OPS * TILE, TILE)

    blocks = pltpu.VMEM((SECTORS, ABLK, TILE, TILE), BF)
    combos = pltpu.VMEM((SECTORS, 4 * TILE, OPS * TILE), BF)
    alpha = call(alpha_kernel, grouped, (blocks, combos))(recv, pairs, w_alpha)
    alpha_land = exchange(alpha.reshape(32, TILE, TILE), ("sym", "x"))
    mixed = call(
        mixed_kernel,
        jax.ShapeDtypeStruct((SECTORS, 512, TILE), F32),
        (blocks, combos, pltpu.VMEM((SECTORS, OPS, TILE, TILE), BF)),
    )(land.reshape(SECTORS, 512, TILE), same, other, w_mix)
    back = call(merge_kernel, jax.ShapeDtypeStruct((SECTORS, 16, 2, 16, TILE), BF))(
        mixed, alpha_land.reshape(SECTORS, 512, TILE)
    )
    home = exchange(back.reshape(256, 16, TILE), ("sym", "z", "x"))
    beta_part = jnp.dot(coeffs, beta_op[0], preferred_element_type=F32)
    return call(unpack_kernel, jax.ShapeDtypeStruct(coeffs.shape, F32))(
        home.reshape(SECTORS, TILES, XDIM, 16, TILE), beta_part
    )


def exchange(array, axes):
    return lax.all_to_all(array, axes, split_axis=0, concat_axis=0, tiled=True)


def solution(mesh):
    fine = Mesh(mesh.devices.reshape(SECTORS, TILES, XDIM), ("sym", "z", "x"))
    rows = ("z", "x")
    in_specs = (
        P(rows, "sym"),
        P("sym", None, None),
        P("sym", None, None, None, None),
        P(),
        P(),
        P(),
        P(),
        P(),
        P(),
        P(),
        P(),
    )
    out_specs = P(rows, "sym")
    return jax.shard_map(
        per_device, mesh=fine, in_specs=in_specs, out_specs=out_specs, check_vma=False
    )
```

time: 157 us -> 169 us (1.076)
  blocking collectives: 0 us -> 38.2 us
  waiting for transfers between devices: 86.3 us -> 48.6 us
  Pallas kernels: 27.8 us -> 37.4 us
  starting transfers between devices: 29.7 us -> 27.8 us
    all_to_all x0 -> x1, blocking collectives: none -> 38.2 us  [exchange(): return lax.all_to_all(array, axes, split_axis=0, concat_axis=0, tiled=True)]
    all_to_all x2 -> x3, waiting for transfers between devices: 64.9 us -> 27.8 us  [exchange(): return lax.all_to_all(array, axes, split_axis=0, concat_axis=0, tiled=True)]
    pallas_call x2 -> x5, Pallas kernels: 22.9 us -> 33.5 us  [the longest x1 12.5 us: per_device(): call(mixed_kernel, jax.ShapeDtypeStruct((SECTORS, 512, TILE), F32), (bloc...]
    ppermute x4, starting transfers between devices: 6.1 us -> 4.06 us  [swapped(): return lax.ppermute(array, 'sym', [(s, s ^ mask) for s in range(SECTORS)])]
    all_to_all x2 -> x3, starting transfers between devices: 23.6 us -> 23.7 us  [exchange(): return lax.all_to_all(array, axes, split_axis=0, concat_axis=0, tiled=True)]
  transfers between devices with their start and end apart: 6 -> 7, of which waited for: 4 -> 3; matrix products, arithmetic and copies ran while one was open for 8% -> 9% of each run, Pallas kernels for 0% -> 13%
where the time goes in v3:
time: 169 us; the launch traced here: 168 us
  waiting for transfers between devices  48.6 us (29%)
  blocking collectives  38.2 us (23%)
  Pallas kernels  37.4 us (22%)
  starting transfers between devices  27.8 us (16%)
  other arithmetic  7.08 us (4%)
  local copies, waits for them, and re-layouts  5.15 us (3%)
  matrix products  3.81 us (2%)
    all_to_all x1, blocking collectives, exchange(): return lax.all_to_all(array, axes, split_axis=0, concat_axis=0, tiled=True)  38.2 us
    all_to_all x3, waiting for transfers between devices, exchange(): return lax.all_to_all(array, axes, split_axis=0, concat_axis=0, tiled=True)  27.8 us
    all_to_all x3, starting transfers between devices, exchange(): return lax.all_to_all(array, axes, split_axis=0, concat_axis=0, tiled=True)  23.7 us
    ppermute x4, waiting for transfers between devices, swapped(): return lax.ppermute(array, 'sym', [(s, s ^ mask) for s in range(SECTORS)])  20.9 us
    pallas_call x1, Pallas kernels, per_device(): call(mixed_kernel, jax.ShapeDtypeStruct((SECTORS, 512, TILE), F32), (bloc...  12.5 us
    pallas_call x1, Pallas kernels, per_device(): alpha = call(alpha_kernel, grouped, (blocks, combos))(recv, pairs, w_alpha)  10.1 us
    reduce_sum x2, other arithmetic, signed_weights(): return jnp.sum(jnp.where(hit, factor[:, :, None], 0.0), axis=1).astype(BF)  4.74 us
    pallas_call x1, Pallas kernels, per_device(): call(merge_kernel, jax.ShapeDtypeStruct((SECTORS, 16, 2, 16, TILE), BF))  4.58 us
  transfers between devices with their start and end apart: 7, of which 3 were waited for; matrix products, arithmetic and copies ran while one was open for 9% of the time, Pallas kernels for 13%

profile of v3, /device:TPU:1, one launch (start us, length us, event | category | flops | bytes accessed | tf_op | source)
XLA Modules:
  0.0 168.1 jit_solution(1783636009339449897)
XLA Ops:
  0.0 3.2 %shard_map.109 = bf16[8,512,128]{2,1,0:T(8,128)(2,1)} custom-call(bf16[512,1024]{1,0:T(8,128)(2,1)} %c_ref.1), custom_call_target="tpu_custom_call" | custom-call | tf_op jit(solution)/shard_map/pallas_call | solution.py:216
  3.2 38.2 %all_to_all.20 = bf16[32,128,128]{2,1,0:T(8,128)(2,1)} all-to-all(bf16[32,128,128]{2,1,0:T(8,128)(2,1)} %bitcast.30), channel_id=1, replica_groups=mesh['sym'=8,'z'=8,'x'=4] {'z','x'}, dimensions={0} | all-to-all | bytes 2097152 | tf_op jit(solution)/shard_map/all_to_all | solution.py:252
  41.3 3.1 %shard_map.110 = bf16[16,2,8,16,128]{4,3,2,1,0:T(8,128)(2,1)} custom-call(bf16[32,8,16,128]{3,2,1,0:T(8,128)(2,1)} %bitcast.25), custom_call_target="tpu_custom_call" | custom-call | tf_op jit(solution)/shard_map/pallas_call | solution.py:220
  44.4 10.2 %all-to-all-start.1 = ((bf16[32,128,128]{2,1,0:T(8,128)(2,1)}), bf16[32,128,128]{2,1,0:T(8,128)(2,1)S(1)}, u32[]{:S(2)}, u32[]{:S(2)}) async-start(bf16[32,128,128]{2,1,0:T(8,128)(2,1)} %bitcast.28), calls=%async_computation.1 | async-start | bytes 2097152 | tf_op jit(solution)/shard_map/all_to_all | solution.py:252
  54.6 1.8 %dynamic-slice_bitcast_fusion.1 = (bf16[1,8,128,128]{3,2,1,0:T(8,128)(2,1)S(1)}, bf16[8,128,128]{2,1,0:T(8,128)(2,1)}) fusion(bf16[1,8,8,128,128]{4,3,2,1,0:T(8,128)(2,1)} %param.13, s32[]{:T(128)S(6)} %select_n.21), kind=kLoop, calls=%fused_computation.10 | loop fusion | bytes 786436 | tf_op jit(solution)/shard_map/stack | solution.py:213
  56.4 2.6 %collective-permute-start.2 = (bf16[8,128,128]{2,1,0:T(8,128)(2,1)}, bf16[8,128,128]{2,1,0:T(8,128)(2,1)}, u32[]{:S(2)}, u32[]{:S(2)}) collective-permute-start(bf16[8,128,128]{2,1,0:T(8,128)(2,1)} %get-tuple-element.6), channel_id=1, source_target_pairs={{0,192},{32,224},{64,128},{96,160},{128,64},{160,96},{192,0},{224,... | collective-permute-start | bytes 786440 | tf_op jit(solution)/shard_map/ppermute | solution.py:195
  59.1 0.5 collective-permute-start.1
  59.6 0.1 collective-permute-start
  59.9 20.9 %collective-permute-done.2 = bf16[8,128,128]{2,1,0:T(8,128)(2,1)} collective-permute-done((bf16[8,128,128]{2,1,0:T(8,128)(2,1)}, bf16[8,128,128]{2,1,0:T(8,128)(2,1)}, u32[]{:S(2)}, u32[]{:S(2)}) %collective-permute-start.2) | collective-permute-done | bytes 262176 | tf_op jit(solution)/shard_map/ppermute | solution.py:195
  80.8 2.2 %pad_maximum_fusion.same_ref = bf16[4,8,128,128]{3,2,1,0:T(8,128)(2,1)} fusion(bf16[1,8,128,128]{3,2,1,0:T(8,128)(2,1)} %bitcast.8, bf16[1,8,128,128]{3,2,1,0:T(8,128)(2,1)} %bitcast.7, bf16[1,8,128,128]{3,2,1,0:T(8,128)(2,1)} %bitcast.6, bf16[1,8,128,128]{3,2,1,0:T(8,128)(2,1)S(1)} %get-tuple-element.5), kind=kLoop, calls=%fused_computation.6 | loop fusion | flops 1572864 | bytes 2097152 | tf_op jit(solution)/shard_map/stack | solution.py:213
  83.0 0.8 collective-permute-start.3
  83.8 2.1 %select_reduce_fusion.1.w_ref = bf16[128,1024]{1,0:T(8,128)(2,1)} fusion(f32[128,8]{1,0:T(8,128)S(1)} %copy.30, s32[128,8]{1,0:T(8,128)S(1)} %copy.29), kind=kLoop, calls=%fused_computation.2 | loop fusion | flops 3014656 | bytes 270336 | tf_op jit(solution)/shard_map/reduce_sum | solution.py:191
  85.9 1.8 %copy.28 = bf16[8,128,128]{2,1,0:T(8,128)(2,1)} copy(bf16[8,128,128]{1,2,0:T(8,128)(2,1)} %bitcast.35) | data formatting | bytes 524288 | tf_op jit(solution)/shard_map/transpose | solution.py:230
  87.7 10.1 %shard_map.112 = bf16[16,2,8,16,128]{4,3,2,1,0:T(8,128)(2,1)} custom-call(bf16[32,8,16,128]{3,2,1,0:T(8,128)(2,1)} %bitcast.26, bf16[1024,128]{1,0:T(8,128)(2,1)} %bitcast.33, bf16[128,1024]{1,0:T(8,128)(2,1)} %select_reduce_fusion.1.w_ref), custom_call_target="tpu_custom_call" | custom-call | tf_op jit(solution)/shard_map/pallas_call | solution.py:234
  97.8 5.5 %all-to-all-start.2 = ((bf16[32,128,128]{2,1,0:T(8,128)(2,1)}), bf16[32,128,128]{2,1,0:T(8,128)(2,1)}, u32[]{:S(2)}, u32[]{:S(2)}) async-start(bf16[32,128,128]{2,1,0:T(8,128)(2,1)} %bitcast.29), calls=%async_computation.2 | async-start | bytes 2097152 | tf_op jit(solution)/shard_map/all_to_all | solution.py:252
  103.8 2.7 %select_reduce_fusion.w_ref = bf16[128,1024]{1,0:T(8,128)(2,1)} fusion(f32[128,16]{1,0:T(8,128)S(1)} %copy.27, s32[128,16]{1,0:T(8,128)S(1)} %copy.26), kind=kLoop, calls=%fused_computation | loop fusion | flops 6160384 | bytes 278528 | tf_op jit(solution)/shard_map/reduce_sum | solution.py:191
  106.5 12.5 %shard_map.111.res_ref = f32[8,512,128]{2,1,0:T(8,128)} custom-call(bf16[8,512,128]{2,1,0:T(8,128)(2,1)} %bitcast.31, bf16[4,8,128,128]{3,2,1,0:T(8,128)(2,1)} %pad_maximum_fusion.same_ref, bf16[4,8,128,128]{3,2,1,0:T(8,128)(2,1)} %collective-permute-done.3.other_ref, bf16[128,1024]{1,0:T(8,128)(2,1)} %select_reduce_fusion.w_ref), custom_call_target="tpu_custom_call" | custom-call | tf_op jit(solution)/shard_map/pallas_call | solution.py:236
  119.0 0.4 all-to-all-done.2
  119.4 4.6 %shard_map.113 = bf16[8,16,2,16,128]{4,3,2,1,0:T(8,128)(2,1)} custom-call(f32[8,512,128]{2,1,0:T(8,128)} %shard_map.111.res_ref, bf16[8,512,128]{2,1,0:T(8,128)(2,1)} %bitcast.15.land_ref), custom_call_target="tpu_custom_call" | custom-call | tf_op jit(solution)/shard_map/pallas_call | solution.py:241
  123.9 8.1 %all-to-all-start.3 = ((bf16[256,16,128]{2,1,0:T(8,128)(2,1)}), bf16[256,16,128]{2,1,0:T(8,128)(2,1)S(1)}, u32[]{:S(2)}, u32[]{:S(2)}) async-start(bf16[256,16,128]{2,1,0:T(8,128)(2,1)} %bitcast.32), calls=%async_computation.3 | async-start | bytes 2097152 | tf_op jit(solution)/shard_map/all_to_all | solution.py:252
  132.0 3.8 %fusion.beta_ref = f32[512,1024]{1,0:T(8,128)} fusion(bf16[512,1024]{1,0:T(8,128)(2,1)} %c_ref.1, bf16[1,1024,1024]{2,1,0:T(8,128)(2,1)S(1)} %copy-done), kind=kOutput, calls=%fused_computation.4 | convolution fusion | flops 1073741824 | bytes 5242880 | tf_op jit(solution)/shard_map/dot_general | solution.py:245
  135.8 27.4 %all-to-all-done.3 = bf16[256,16,128]{2,1,0:T(8,128)(2,1)S(1)} async-done(((bf16[256,16,128]{2,1,0:T(8,128)(2,1)}), bf16[256,16,128]{2,1,0:T(8,128)(2,1)S(1)}, u32[]{:S(2)}, u32[]{:S(2)}) %all-to-all-start.3) | async-done | bytes 1048608 | tf_op jit(solution)/shard_map/all_to_all | solution.py:252
  163.2 1.0 copy-done.1
  164.2 3.9 %shard_map.114 = f32[512,1024]{1,0:T(8,128)} custom-call(bf16[8,8,4,16,128]{4,3,2,1,0:T(8,128)(2,1)} %bitcast.27, f32[512,1024]{1,0:T(8,128)} %fusion.beta_ref), custom_call_target="tpu_custom_call" | custom-call | tf_op jit(solution)/shard_map/pallas_call | solution.py:246
  (35 shorter events, 0.7 us)
Async XLA Ops:
  0.0 132.0 %copy-start = (bf16[1,1024,1024]{2,1,0:T(8,128)(2,1)S(1)}, bf16[1,1024,1024]{2,1,0:T(8,128)(2,1)}, u32[]{:S(2)}) copy-start(bf16[1,1024,1024]{2,1,0:T(8,128)(2,1)} %param.12) | copy-start | bytes 6291460
  41.3 18.4 %copy-start.9 = (s32[128,8]{0,1:T(8,128)S(1)}, s32[128,8]{0,1:T(8,128)}, u32[]{:S(2)}) copy-start(s32[128,8]{0,1:T(8,128)} %param.20) | copy-start | bytes 12292
  41.3 18.5 %copy-start.7 = (s32[128,8]{0,1:T(8,128)S(1)}, s32[128,8]{0,1:T(8,128)}, u32[]{:S(2)}) copy-start(s32[128,8]{0,1:T(8,128)} %param.19) | copy-start | bytes 12292
  41.3 18.5 %copy-start.8 = (s32[128,8]{0,1:T(8,128)S(1)}, s32[128,8]{0,1:T(8,128)}, u32[]{:S(2)}) copy-start(s32[128,8]{0,1:T(8,128)} %param.21) | copy-start | bytes 12292
  44.4 53.4 %all-to-all-start.1 = ((bf16[32,128,128]{2,1,0:T(8,128)(2,1)}), bf16[32,128,128]{2,1,0:T(8,128)(2,1)S(1)}, u32[]{:S(2)}, u32[]{:S(2)}) async-start(bf16[32,128,128]{2,1,0:T(8,128)(2,1)} %bitcast.28), calls=%async_computation.1 | async-start | bytes 2097152 | tf_op jit(solution)/shard_map/all_to_all | solution.py:252
  56.4 24.3 %collective-permute-start.2 = (bf16[8,128,128]{2,1,0:T(8,128)(2,1)}, bf16[8,128,128]{2,1,0:T(8,128)(2,1)}, u32[]{:S(2)}, u32[]{:S(2)}) collective-permute-start(bf16[8,128,128]{2,1,0:T(8,128)(2,1)} %get-tuple-element.6), channel_id=1, source_target_pairs={{0,192},{32,224},{64,128},{96,160},{128,64},{160,96},{192,0},{224,... | collective-permute-start | bytes 786440 | tf_op jit(solution)/shard_map/ppermute | solution.py:195
  59.1 21.7 %collective-permute-start.1 = (bf16[8,128,128]{2,1,0:T(8,128)(2,1)}, bf16[8,128,128]{2,1,0:T(8,128)(2,1)}, u32[]{:S(2)}, u32[]{:S(2)}) collective-permute-start(bf16[8,128,128]{2,1,0:T(8,128)(2,1)} %get-tuple-element.6), channel_id=1, source_target_pairs={{0,128},{32,160},{64,192},{96,224},{128,0},{160,32},{192,64},{224,... | collective-permute-start | bytes 786440 | tf_op jit(solution)/shard_map/ppermute | solution.py:195
  59.6 21.2 %collective-permute-start = (bf16[8,128,128]{2,1,0:T(8,128)(2,1)}, bf16[8,128,128]{2,1,0:T(8,128)(2,1)}, u32[]{:S(2)}, u32[]{:S(2)}) collective-permute-start(bf16[8,128,128]{2,1,0:T(8,128)(2,1)} %get-tuple-element.6), channel_id=1, source_target_pairs={{0,64},{32,96},{64,0},{96,32},{128,192},{160,224},{192,128},{224,1... | collective-permute-start | bytes 786440 | tf_op jit(solution)/shard_map/ppermute | solution.py:195
  83.0 23.5 %collective-permute-start.3 = (bf16[4,8,128,128]{3,2,1,0:T(8,128)(2,1)}, bf16[4,8,128,128]{3,2,1,0:T(8,128)(2,1)}, u32[]{:S(2)}, u32[]{:S(2)}) collective-permute-start(bf16[4,8,128,128]{3,2,1,0:T(8,128)(2,1)} %pad_maximum_fusion.same_ref), channel_id=1, source_target_pairs={{0,32},{32,0},{64,96},{96,64},{128,160},{160,128},{192,224},{224,1... | collective-permute-start | bytes 3145736 | tf_op jit(solution)/shard_map/ppermute | solution.py:195
  87.7 15.6 %copy-start.3 = (s32[32,32,2]{1,2,0:T(2,128)S(1)}, s32[32,32,2]{1,2,0:T(2,128)}, u32[]{:S(2)}) copy-start(s32[32,32,2]{1,2,0:T(2,128)} %param.15) | copy-start | bytes 24580
  87.7 15.8 %copy-start.4 = (s32[128,16]{0,1:T(8,128)S(1)}, s32[128,16]{0,1:T(8,128)}, u32[]{:S(2)}) copy-start(s32[128,16]{0,1:T(8,128)} %param.16) | copy-start | bytes 24580
  87.7 15.9 %copy-start.6 = (s32[128,16]{0,1:T(8,128)S(1)}, s32[128,16]{0,1:T(8,128)}, u32[]{:S(2)}) copy-start(s32[128,16]{0,1:T(8,128)} %param.18) | copy-start | bytes 24580
  87.7 16.0 %copy-start.5 = (s32[128,16]{0,1:T(8,128)S(1)}, s32[128,16]{0,1:T(8,128)}, u32[]{:S(2)}) copy-start(s32[128,16]{0,1:T(8,128)} %param.17) | copy-start | bytes 24580
  97.8 8.7 %copy-start.2 = (bf16[32,128,128]{2,1,0:T(8,128)(2,1)}, bf16[32,128,128]{2,1,0:T(8,128)(2,1)S(1)}, u32[]{:S(2)}) copy-start(bf16[32,128,128]{2,1,0:T(8,128)(2,1)S(1)} %all-to-all-done.1) | copy-start | bytes 3145732
  97.8 21.5 %all-to-all-start.2 = ((bf16[32,128,128]{2,1,0:T(8,128)(2,1)}), bf16[32,128,128]{2,1,0:T(8,128)(2,1)}, u32[]{:S(2)}, u32[]{:S(2)}) async-start(bf16[32,128,128]{2,1,0:T(8,128)(2,1)} %bitcast.29), calls=%async_computation.2 | async-start | bytes 2097152 | tf_op jit(solution)/shard_map/all_to_all | solution.py:252
  123.9 39.3 %all-to-all-start.3 = ((bf16[256,16,128]{2,1,0:T(8,128)(2,1)}), bf16[256,16,128]{2,1,0:T(8,128)(2,1)S(1)}, u32[]{:S(2)}, u32[]{:S(2)}) async-start(bf16[256,16,128]{2,1,0:T(8,128)(2,1)} %bitcast.32), calls=%async_computation.3 | async-start | bytes 2097152 | tf_op jit(solution)/shard_map/all_to_all | solution.py:252
  163.2 1.0 copy-start.1

commit v4 on v3

--- a/solution.py
+++ b/solution.py
@@ -215,11 +215,6 @@
 
     send = call(pack_kernel, jax.ShapeDtypeStruct((TILES, 512, TILE), BF))(coeffs)
     recv = exchange(send.reshape(32, TILE, TILE), ("z", "x"))
-    recv = recv.reshape(RANKS, TILES, 16, TILE)
-    grouped = jax.ShapeDtypeStruct((16, 2, TILES, 16, TILE), BF)
-    turned = call(turn_kernel, grouped)(recv)
-    land = exchange(turned.reshape(32, TILE, TILE), ("sym", "x"))
-
     table = jnp.transpose(send_list, (1, 0, 2)).reshape(RANKS, RANKS * CAP)
     slots = jnp.arange(RANKS * CAP, dtype=jnp.int32)
     table = jnp.broadcast_to(table[:, None, :], (RANKS, ABLK, RANKS * CAP)).reshape(NBLK, 1, RANKS * CAP)
@@ -228,6 +223,14 @@
     w_mix = signed_weights(source, mix_sign, mix_pair)
     w_alpha = signed_weights(aa_src, aa_sign, aa_pair)
     pairs = jnp.transpose(pair_op, (0, 2, 1)).reshape(OPS * TILE, TILE)
+
+    recv, same, other, w_mix, w_alpha, pairs = lax.optimization_barrier(
+        (recv, same, other, w_mix, w_alpha, pairs)
+    )
+    recv = recv.reshape(RANKS, TILES, 16, TILE)
+    grouped = jax.ShapeDtypeStruct((16, 2, TILES, 16, TILE), BF)
+    turned = call(turn_kernel, grouped)(recv)
+    land = exchange(turned.reshape(32, TILE, TILE), ("sym", "x"))
 
     blocks = pltpu.VMEM((SECTORS, ABLK, TILE, TILE), BF)
     combos = pltpu.VMEM((SECTORS, 4 * TILE, OPS * TILE), BF)

time: 169 us -> 144 us (0.85)
  blocking collectives: 38.2 us -> 0 us
  starting transfers between devices: 27.8 us -> 40.4 us
    all_to_all x1 -> x0, blocking collectives: 38.2 us -> none  [exchange(): return lax.all_to_all(array, axes, split_axis=0, concat_axis=0, tiled=True)]
    all_to_all x3 -> x4, starting transfers between devices: 23.7 us -> 35.1 us  [exchange(): return lax.all_to_all(array, axes, split_axis=0, concat_axis=0, tiled=True)]
    ppermute x4, waiting for transfers between devices: 20.9 us -> 11 us  [swapped(): return lax.ppermute(array, 'sym', [(s, s ^ mask) for s in range(SECTORS)])]
    all_to_all x3 -> x4, waiting for transfers between devices: 27.8 us -> 37 us  [exchange(): return lax.all_to_all(array, axes, split_axis=0, concat_axis=0, tiled=True)]
  transfers between devices with their start and end apart: 7 -> 8, of which waited for: 3 -> 5; matrix products, arithmetic and copies ran while one was open for 9% -> 10% of each run, Pallas kernels for 13% -> 16%
where the time goes in v4:
time: 144 us; the launch traced here: 143 us
  waiting for transfers between devices  48 us (33%)
  starting transfers between devices  40.4 us (28%)
  Pallas kernels  37.3 us (26%)
  other arithmetic  7.06 us (5%)
  local copies, waits for them, and re-layouts  6.1 us (4%)
  matrix products  3.81 us (3%)
    all_to_all x4, waiting for transfers between devices, exchange(): return lax.all_to_all(array, axes, split_axis=0, concat_axis=0, tiled=True)  37 us
    all_to_all x4, starting transfers between devices, exchange(): return lax.all_to_all(array, axes, split_axis=0, concat_axis=0, tiled=True)  35.1 us
    pallas_call x1, Pallas kernels, per_device(): call(mixed_kernel, jax.ShapeDtypeStruct((SECTORS, 512, TILE), F32), (bloc...  12.5 us
    ppermute x4, waiting for transfers between devices, swapped(): return lax.ppermute(array, 'sym', [(s, s ^ mask) for s in range(SECTORS)])  11 us
    pallas_call x1, Pallas kernels, per_device(): alpha = call(alpha_kernel, grouped, (blocks, combos))(recv, pairs, w_alpha)  10.1 us
    ppermute x4, starting transfers between devices, swapped(): return lax.ppermute(array, 'sym', [(s, s ^ mask) for s in range(SECTORS)])  5.3 us
    reduce_sum x2, other arithmetic, signed_weights(): return jnp.sum(jnp.where(hit, factor[:, :, None], 0.0), axis=1).astype(BF)  4.75 us
    pallas_call x1, Pallas kernels, per_device(): call(merge_kernel, jax.ShapeDtypeStruct((SECTORS, 16, 2, 16, TILE), BF))  4.58 us
  transfers between devices with their start and end apart: 8, of which 5 were waited for; matrix products, arithmetic and copies ran while one was open for 10% of the time, Pallas kernels for 16%

profile of v4, /device:TPU:1, one launch (start us, length us, event | category | flops | bytes accessed | tf_op | source)
XLA Modules:
  0.0 142.9 jit_solution(7323601104303229617)
XLA Ops:
  0.0 3.2 %shard_map.109 = bf16[8,512,128]{2,1,0:T(8,128)(2,1)} custom-call(bf16[512,1024]{1,0:T(8,128)(2,1)} %c_ref.1), custom_call_target="tpu_custom_call" | custom-call | tf_op jit(solution)/shard_map/pallas_call | solution.py:216
  3.2 12.0 %all-to-all-start = ((bf16[32,128,128]{2,1,0:T(8,128)(2,1)}), bf16[32,128,128]{2,1,0:T(8,128)(2,1)S(1)}, u32[]{:S(2)}, u32[]{:S(2)}) async-start(bf16[32,128,128]{2,1,0:T(8,128)(2,1)} %bitcast.28), calls=%async_computation | async-start | bytes 2097152 | tf_op jit(solution)/shard_map/all_to_all | solution.py:255
  15.2 1.8 %dynamic-slice_bitcast_fusion.1 = (bf16[1,8,128,128]{3,2,1,0:T(8,128)(2,1)S(1)}, bf16[8,128,128]{2,1,0:T(8,128)(2,1)}) fusion(bf16[1,8,8,128,128]{4,3,2,1,0:T(8,128)(2,1)} %param.13, s32[]{:T(128)S(6)} %select_n.21), kind=kLoop, calls=%fused_computation.10 | loop fusion | bytes 786436 | tf_op jit(solution)/shard_map/stack | solution.py:213
  17.0 2.7 %collective-permute-start.2 = (bf16[8,128,128]{2,1,0:T(8,128)(2,1)}, bf16[8,128,128]{2,1,0:T(8,128)(2,1)}, u32[]{:S(2)}, u32[]{:S(2)}) collective-permute-start(bf16[8,128,128]{2,1,0:T(8,128)(2,1)} %get-tuple-element.18), channel_id=1, source_target_pairs={{0,192},{32,224},{64,128},{96,160},{128,64},{160,96},{192,0},{224,... | collective-permute-start | bytes 786440 | tf_op jit(solution)/shard_map/ppermute | solution.py:195
  20.6 10.8 %collective-permute-done.2 = bf16[8,128,128]{2,1,0:T(8,128)(2,1)} collective-permute-done((bf16[8,128,128]{2,1,0:T(8,128)(2,1)}, bf16[8,128,128]{2,1,0:T(8,128)(2,1)}, u32[]{:S(2)}, u32[]{:S(2)}) %collective-permute-start.2) | collective-permute-done | bytes 262176 | tf_op jit(solution)/shard_map/ppermute | solution.py:195
  31.6 2.2 %pad_maximum_fusion.same_ref = bf16[4,8,128,128]{3,2,1,0:T(8,128)(2,1)} fusion(bf16[1,8,128,128]{3,2,1,0:T(8,128)(2,1)} %bitcast.5, bf16[1,8,128,128]{3,2,1,0:T(8,128)(2,1)} %bitcast.4, bf16[1,8,128,128]{3,2,1,0:T(8,128)(2,1)} %bitcast.3, bf16[1,8,128,128]{3,2,1,0:T(8,128)(2,1)S(1)} %get-tuple-element.17), kind=kLoop, calls=%fused_computation.6 | loop fusion | flops 1572864 | bytes 2097152 | tf_op jit(solution)/shard_map/stack | solution.py:213
  33.8 2.0 %collective-permute-start.3 = (bf16[4,8,128,128]{3,2,1,0:T(8,128)(2,1)}, bf16[4,8,128,128]{3,2,1,0:T(8,128)(2,1)}, u32[]{:S(2)}, u32[]{:S(2)}) collective-permute-start(bf16[4,8,128,128]{3,2,1,0:T(8,128)(2,1)} %pad_maximum_fusion.same_ref), channel_id=1, source_target_pairs={{0,32},{32,0},{64,96},{96,64},{128,160},{160,128},{192,224},{224,1... | collective-permute-start | bytes 3145736 | tf_op jit(solution)/shard_map/ppermute | solution.py:195
  36.2 1.8 %copy.30 = bf16[8,128,128]{2,1,0:T(8,128)(2,1)} copy(bf16[8,128,128]{1,2,0:T(8,128)(2,1)} %bitcast.35) | data formatting | bytes 524288 | tf_op jit(solution)/shard_map/transpose | solution.py:225
  38.0 2.1 %select_reduce_fusion.1.w_ref = bf16[128,1024]{1,0:T(8,128)(2,1)} fusion(f32[128,8]{1,0:T(8,128)S(1)} %copy.29, s32[128,8]{1,0:T(8,128)S(1)} %copy.28), kind=kLoop, calls=%fused_computation.2 | loop fusion | flops 3014656 | bytes 270336 | tf_op jit(solution)/shard_map/reduce_sum | solution.py:191
  40.1 2.7 %select_reduce_fusion.w_ref = bf16[128,1024]{1,0:T(8,128)(2,1)} fusion(f32[128,16]{1,0:T(8,128)S(1)} %copy.27, s32[128,16]{1,0:T(8,128)S(1)} %copy.26), kind=kLoop, calls=%fused_computation | loop fusion | flops 6160384 | bytes 278528 | tf_op jit(solution)/shard_map/reduce_sum | solution.py:191
  42.8 1.0 copy-done.1
  43.7 3.1 %shard_map.110 = bf16[16,2,8,16,128]{4,3,2,1,0:T(8,128)(2,1)} custom-call(bf16[32,8,16,128]{3,2,1,0:T(8,128)(2,1)} %bitcast.25), custom_call_target="tpu_custom_call" | custom-call | tf_op jit(solution)/shard_map/pallas_call | solution.py:232
  46.8 8.8 %all-to-all-start.1 = ((bf16[32,128,128]{2,1,0:T(8,128)(2,1)}), bf16[32,128,128]{2,1,0:T(8,128)(2,1)S(1)}, u32[]{:S(2)}, u32[]{:S(2)}) async-start(bf16[32,128,128]{2,1,0:T(8,128)(2,1)} %bitcast.30), calls=%async_computation.1 | async-start | bytes 2097152 | tf_op jit(solution)/shard_map/all_to_all | solution.py:255
  55.6 10.1 %shard_map.112 = bf16[16,2,8,16,128]{4,3,2,1,0:T(8,128)(2,1)} custom-call(bf16[32,8,16,128]{3,2,1,0:T(8,128)(2,1)} %bitcast.26, bf16[1024,128]{1,0:T(8,128)(2,1)} %bitcast.33, bf16[128,1024]{1,0:T(8,128)(2,1)} %select_reduce_fusion.1.w_ref), custom_call_target="tpu_custom_call" | custom-call | tf_op jit(solution)/shard_map/pallas_call | solution.py:237
  65.7 5.9 %all-to-all-done.1 = bf16[32,128,128]{2,1,0:T(8,128)(2,1)S(1)} async-done(((bf16[32,128,128]{2,1,0:T(8,128)(2,1)}), bf16[32,128,128]{2,1,0:T(8,128)(2,1)S(1)}, u32[]{:S(2)}, u32[]{:S(2)}) %all-to-all-start.1) | async-done | bytes 1048608 | tf_op jit(solution)/shard_map/all_to_all | solution.py:255
  71.7 5.5 %all-to-all-start.2 = ((bf16[32,128,128]{2,1,0:T(8,128)(2,1)}), bf16[32,128,128]{2,1,0:T(8,128)(2,1)}, u32[]{:S(2)}, u32[]{:S(2)}) async-start(bf16[32,128,128]{2,1,0:T(8,128)(2,1)} %bitcast.29), calls=%async_computation.2 | async-start | bytes 2097152 | tf_op jit(solution)/shard_map/all_to_all | solution.py:255
  77.2 12.5 %shard_map.111.res_ref = f32[8,512,128]{2,1,0:T(8,128)} custom-call(bf16[8,512,128]{2,1,0:T(8,128)(2,1)} %bitcast.31, bf16[4,8,128,128]{3,2,1,0:T(8,128)(2,1)} %pad_maximum_fusion.same_ref, bf16[4,8,128,128]{3,2,1,0:T(8,128)(2,1)} %collective-permute-done.3.other_ref, bf16[128,1024]{1,0:T(8,128)(2,1)} %select_reduce_fusion.w_ref), custom_call_target="tpu_custom_call" | custom-call | tf_op jit(solution)/shard_map/pallas_call | solution.py:239
  89.7 3.7 %all-to-all-done.2 = bf16[32,128,128]{2,1,0:T(8,128)(2,1)} async-done(((bf16[32,128,128]{2,1,0:T(8,128)(2,1)}), bf16[32,128,128]{2,1,0:T(8,128)(2,1)}, u32[]{:S(2)}, u32[]{:S(2)}) %all-to-all-start.2) | async-done | bytes 1048608 | tf_op jit(solution)/shard_map/all_to_all | solution.py:255
  93.3 4.6 %shard_map.113 = bf16[8,16,2,16,128]{4,3,2,1,0:T(8,128)(2,1)} custom-call(f32[8,512,128]{2,1,0:T(8,128)} %shard_map.111.res_ref, bf16[8,512,128]{2,1,0:T(8,128)(2,1)} %bitcast.15.land_ref), custom_call_target="tpu_custom_call" | custom-call | tf_op jit(solution)/shard_map/pallas_call | solution.py:244
  97.9 8.9 %all-to-all-start.3 = ((bf16[256,16,128]{2,1,0:T(8,128)(2,1)}), bf16[256,16,128]{2,1,0:T(8,128)(2,1)S(1)}, u32[]{:S(2)}, u32[]{:S(2)}) async-start(bf16[256,16,128]{2,1,0:T(8,128)(2,1)} %bitcast.32), calls=%async_computation.3 | async-start | bytes 2097152 | tf_op jit(solution)/shard_map/all_to_all | solution.py:255
  106.8 3.8 %fusion.beta_ref = f32[512,1024]{1,0:T(8,128)} fusion(bf16[512,1024]{1,0:T(8,128)(2,1)} %c_ref.1, bf16[1,1024,1024]{2,1,0:T(8,128)(2,1)S(1)} %copy-done), kind=kOutput, calls=%fused_computation.4 | convolution fusion | flops 1073741824 | bytes 5242880 | tf_op jit(solution)/shard_map/dot_general | solution.py:248
  110.6 27.4 %all-to-all-done.3 = bf16[256,16,128]{2,1,0:T(8,128)(2,1)S(1)} async-done(((bf16[256,16,128]{2,1,0:T(8,128)(2,1)}), bf16[256,16,128]{2,1,0:T(8,128)(2,1)S(1)}, u32[]{:S(2)}, u32[]{:S(2)}) %all-to-all-start.3) | async-done | bytes 1048608 | tf_op jit(solution)/shard_map/all_to_all | solution.py:255
  138.0 1.0 copy-done.2
  139.0 3.9 %shard_map.114 = f32[512,1024]{1,0:T(8,128)} custom-call(bf16[8,8,4,16,128]{4,3,2,1,0:T(8,128)(2,1)} %bitcast.27, f32[512,1024]{1,0:T(8,128)} %fusion.beta_ref), custom_call_target="tpu_custom_call" | custom-call | tf_op jit(solution)/shard_map/pallas_call | solution.py:249
  (38 shorter events, 1.5 us)
Async XLA Ops:
  0.0 106.8 %copy-start = (bf16[1,1024,1024]{2,1,0:T(8,128)(2,1)S(1)}, bf16[1,1024,1024]{2,1,0:T(8,128)(2,1)}, u32[]{:S(2)}) copy-start(bf16[1,1024,1024]{2,1,0:T(8,128)(2,1)} %param.12) | copy-start | bytes 6291460
  0.0 20.3 %copy-start.4 = (s32[32,32,2]{1,2,0:T(2,128)S(1)}, s32[32,32,2]{1,2,0:T(2,128)}, u32[]{:S(2)}) copy-start(s32[32,32,2]{1,2,0:T(2,128)} %param.15) | copy-start | bytes 24580
  0.0 20.5 %copy-start.5 = (s32[128,16]{0,1:T(8,128)S(1)}, s32[128,16]{0,1:T(8,128)}, u32[]{:S(2)}) copy-start(s32[128,16]{0,1:T(8,128)} %param.16) | copy-start | bytes 24580
  3.2 17.4 %copy-start.7 = (s32[128,16]{0,1:T(8,128)S(1)}, s32[128,16]{0,1:T(8,128)}, u32[]{:S(2)}) copy-start(s32[128,16]{0,1:T(8,128)} %param.18) | copy-start | bytes 24580
  3.2 39.6 %all-to-all-start = ((bf16[32,128,128]{2,1,0:T(8,128)(2,1)}), bf16[32,128,128]{2,1,0:T(8,128)(2,1)S(1)}, u32[]{:S(2)}, u32[]{:S(2)}) async-start(bf16[32,128,128]{2,1,0:T(8,128)(2,1)} %bitcast.28), calls=%async_computation | async-start | bytes 2097152 | tf_op jit(solution)/shard_map/all_to_all | solution.py:255
  15.2 20.6 %copy-start.6 = (s32[128,16]{0,1:T(8,128)S(1)}, s32[128,16]{0,1:T(8,128)}, u32[]{:S(2)}) copy-start(s32[128,16]{0,1:T(8,128)} %param.17) | copy-start | bytes 24580
  15.2 20.8 %copy-start.10 = (s32[128,8]{0,1:T(8,128)S(1)}, s32[128,8]{0,1:T(8,128)}, u32[]{:S(2)}) copy-start(s32[128,8]{0,1:T(8,128)} %param.20) | copy-start | bytes 12292
  15.2 20.9 %copy-start.8 = (s32[128,8]{0,1:T(8,128)S(1)}, s32[128,8]{0,1:T(8,128)}, u32[]{:S(2)}) copy-start(s32[128,8]{0,1:T(8,128)} %param.19) | copy-start | bytes 12292
  15.2 20.9 %copy-start.9 = (s32[128,8]{0,1:T(8,128)S(1)}, s32[128,8]{0,1:T(8,128)}, u32[]{:S(2)}) copy-start(s32[128,8]{0,1:T(8,128)} %param.21) | copy-start | bytes 12292
  17.0 14.4 %collective-permute-start.2 = (bf16[8,128,128]{2,1,0:T(8,128)(2,1)}, bf16[8,128,128]{2,1,0:T(8,128)(2,1)}, u32[]{:S(2)}, u32[]{:S(2)}) collective-permute-start(bf16[8,128,128]{2,1,0:T(8,128)(2,1)} %get-tuple-element.18), channel_id=1, source_target_pairs={{0,192},{32,224},{64,128},{96,160},{128,64},{160,96},{192,0},{224,... | collective-permute-start | bytes 786440 | tf_op jit(solution)/shard_map/ppermute | solution.py:195
  19.7 11.7 %collective-permute-start.1 = (bf16[8,128,128]{2,1,0:T(8,128)(2,1)}, bf16[8,128,128]{2,1,0:T(8,128)(2,1)}, u32[]{:S(2)}, u32[]{:S(2)}) collective-permute-start(bf16[8,128,128]{2,1,0:T(8,128)(2,1)} %get-tuple-element.18), channel_id=1, source_target_pairs={{0,128},{32,160},{64,192},{96,224},{128,0},{160,32},{192,64},{224,... | collective-permute-start | bytes 786440 | tf_op jit(solution)/shard_map/ppermute | solution.py:195
  20.1 11.5 %collective-permute-start = (bf16[8,128,128]{2,1,0:T(8,128)(2,1)}, bf16[8,128,128]{2,1,0:T(8,128)(2,1)}, u32[]{:S(2)}, u32[]{:S(2)}) collective-permute-start(bf16[8,128,128]{2,1,0:T(8,128)(2,1)} %get-tuple-element.18), channel_id=1, source_target_pairs={{0,64},{32,96},{64,0},{96,32},{128,192},{160,224},{192,128},{224,1... | collective-permute-start | bytes 786440 | tf_op jit(solution)/shard_map/ppermute | solution.py:195
  33.8 9.0 %collective-permute-start.3 = (bf16[4,8,128,128]{3,2,1,0:T(8,128)(2,1)}, bf16[4,8,128,128]{3,2,1,0:T(8,128)(2,1)}, u32[]{:S(2)}, u32[]{:S(2)}) collective-permute-start(bf16[4,8,128,128]{3,2,1,0:T(8,128)(2,1)} %pad_maximum_fusion.same_ref), channel_id=1, source_target_pairs={{0,32},{32,0},{64,96},{96,64},{128,160},{160,128},{192,224},{224,1... | collective-permute-start | bytes 3145736 | tf_op jit(solution)/shard_map/ppermute | solution.py:195
  42.8 1.0 copy-start.1
  46.8 24.8 %all-to-all-start.1 = ((bf16[32,128,128]{2,1,0:T(8,128)(2,1)}), bf16[32,128,128]{2,1,0:T(8,128)(2,1)S(1)}, u32[]{:S(2)}, u32[]{:S(2)}) async-start(bf16[32,128,128]{2,1,0:T(8,128)(2,1)} %bitcast.30), calls=%async_computation.1 | async-start | bytes 2097152 | tf_op jit(solution)/shard_map/all_to_all | solution.py:255
  71.7 5.5 %copy-start.3 = (bf16[32,128,128]{2,1,0:T(8,128)(2,1)}, bf16[32,128,128]{2,1,0:T(8,128)(2,1)S(1)}, u32[]{:S(2)}) copy-start(bf16[32,128,128]{2,1,0:T(8,128)(2,1)S(1)} %all-to-all-done.1) | copy-start | bytes 3145732
  71.7 21.7 %all-to-all-start.2 = ((bf16[32,128,128]{2,1,0:T(8,128)(2,1)}), bf16[32,128,128]{2,1,0:T(8,128)(2,1)}, u32[]{:S(2)}, u32[]{:S(2)}) async-start(bf16[32,128,128]{2,1,0:T(8,128)(2,1)} %bitcast.29), calls=%async_computation.2 | async-start | bytes 2097152 | tf_op jit(solution)/shard_map/all_to_all | solution.py:255
  97.9 40.1 %all-to-all-start.3 = ((bf16[256,16,128]{2,1,0:T(8,128)(2,1)}), bf16[256,16,128]{2,1,0:T(8,128)(2,1)S(1)}, u32[]{:S(2)}, u32[]{:S(2)}) async-start(bf16[256,16,128]{2,1,0:T(8,128)(2,1)} %bitcast.32), calls=%async_computation.3 | async-start | bytes 2097152 | tf_op jit(solution)/shard_map/all_to_all | solution.py:255
  138.0 1.0 copy-start.2

commit v5 on v4

--- a/solution.py
+++ b/solution.py
@@ -16,7 +16,7 @@
 NBLK = 128
 BF = jnp.bfloat16
 F32 = jnp.float32
-VMEM_BYTES = 56 * 1024 * 1024
+MIB = 1024 * 1024
 
 
 def interleave(rows, cols):
@@ -31,21 +31,32 @@
     return (r == (k % ABLK) * TILE + k // ABLK).astype(F32).astype(BF)
 
 
-def pack_kernel(c_ref, send_ref):
+def pack_kernel(c_hbm, send_hbm, c_ref, t_ref, send_ref, in_sem, out_sem):
+    loads = []
+    for p in range(ABLK):
+        rows = pl.ds(p * TILE, TILE)
+        loads.append(pltpu.make_async_copy(c_hbm.at[rows], c_ref.at[rows], in_sem.at[p]))
+        loads[-1].start()
     order = interleave(512, 512)
-    for t in range(0, TILES, 2):
-        turned = []
-        for u in (t, t + 1):
-            block = c_ref[:, u * TILE : (u + 1) * TILE].astype(F32)
-            turned.append(
-                jnp.concatenate(
-                    [block[p * TILE : (p + 1) * TILE].T.astype(BF) for p in range(ABLK)], axis=0
-                )
-            )
-        both = jnp.concatenate(turned, axis=1)
+    for p in range(ABLK):
+        loads[p].wait()
+        for t in range(TILES):
+            block = c_ref[p * TILE : (p + 1) * TILE, t * TILE : (t + 1) * TILE].astype(F32)
+            t_ref[p * TILE : (p + 1) * TILE, t * TILE : (t + 1) * TILE] = block.T.astype(BF)
+    stores = []
+    for k in range(4):
+        both = t_ref[:, k * 2 * TILE : (k + 1) * 2 * TILE]
         moved = jnp.dot(order, both, preferred_element_type=F32).astype(BF)
-        send_ref[t] = moved[:, :TILE]
-        send_ref[t + 1] = moved[:, TILE:]
+        for o in range(2):
+            part = moved[:, o * TILE : (o + 1) * TILE]
+            send_ref[:, 2 * k + o] = part.reshape(XDIM, TILE, TILE)
+        here = pl.ds(2 * k, 2)
+        stores.append(
+            pltpu.make_async_copy(send_ref.at[:, here], send_hbm.at[:, here], out_sem.at[k])
+        )
+        stores[-1].start()
+    for copy in stores:
+        copy.wait()
 
 
 def swap_halves(first, second):
@@ -74,10 +85,16 @@
         out_ref[:, o, c] = both.reshape(16, 16, TILE).astype(BF)
 
 
-def turn_kernel(recv_ref, out_ref):
-    @pl.loop(0, TILES)
-    def _(c):
+def turn_kernel(recv_ref, out_hbm, out_ref, out_sem):
+    stores = []
+    for c in range(TILES):
         regroup([b.T for b in blocks_of(recv_ref, c)], out_ref, c)
+        stores.append(
+            pltpu.make_async_copy(out_ref.at[:, :, c], out_hbm.at[:, :, c], out_sem.at[c])
+        )
+        stores[-1].start()
+    for copy in stores:
+        copy.wait()
 
 
 def stacked(w_ref):
@@ -115,15 +132,16 @@
 
 
 def landed(land_ref, s, order):
-    both = jnp.concatenate([land_ref[s], land_ref[s + 1]], axis=1)
+    both = jnp.concatenate([land_ref[:, s + o].reshape(512, TILE) for o in range(2)], axis=1)
     return jnp.dot(order, both, preferred_element_type=F32)
 
 
-def mixed_kernel(land_ref, same_ref, other_ref, w_ref, res_ref, x_ref, c_ref, mix_ref):
+def mixed_kernel(
+    land_ref, o0, o1, o2, o3, o4, o5, o6, o7, w_ref, res_hbm, x_ref, c_ref, mix_ref, res_ref, out_sem
+):
     sector = lax.axis_index("sym")
-    for k in range(SECTORS // 2):
-        mix_ref[2 * k] = same_ref[k]
-        mix_ref[2 * k + 1] = other_ref[k]
+    for k, op_ref in enumerate((o0, o1, o2, o3, o4, o5, o6, o7)):
+        mix_ref[k] = op_ref[...]
     order = deinterleave(512, 512)
 
     @pl.loop(0, SECTORS // 2)
@@ -140,14 +158,33 @@
     def _(d):
         ops = jnp.concatenate([mix_ref[sector ^ d ^ g, g] for g in range(OPS)], axis=0)
         res_ref[d] = jnp.dot(c_ref[d], ops, preferred_element_type=F32)
-
-
-def merge_kernel(res_ref, land_ref, out_ref):
+        pltpu.make_async_copy(res_ref.at[d], res_hbm.at[d], out_sem.at[d]).start()
+
+    @pl.loop(0, SECTORS)
+    def _(d):
+        pltpu.make_async_copy(res_ref.at[d], res_hbm.at[d], out_sem.at[d]).wait()
+
+
+def merge_kernel(
+    res_hbm, land_hbm, out_hbm, res_ref, land_ref, out_ref, in_sem, land_sem, out_sem
+):
+    loads, lands = [], []
+    for half in range(SECTORS // 2):
+        here = pl.ds(2 * half, 2)
+        lands.append(
+            pltpu.make_async_copy(land_hbm.at[:, here], land_ref.at[:, here], land_sem.at[half])
+        )
+        loads.append(
+            pltpu.make_async_copy(res_hbm.at[here], res_ref.at[here], in_sem.at[half])
+        )
+        lands[-1].start()
+        loads[-1].start()
     order = deinterleave(512, 512)
-
-    @pl.loop(0, SECTORS // 2)
-    def _(half):
+    stores = []
+    for half in range(SECTORS // 2):
+        lands[half].wait()
         moved = landed(land_ref, 2 * half, order)
+        loads[half].wait()
         for o in range(2):
             d = 2 * half + o
             blocks = []
@@ -161,26 +198,88 @@
                 sides.append(swap_halves(first, second))
             for side in range(2):
                 both = jnp.concatenate([sides[0][side][:, None], sides[1][side][:, None]], axis=1)
-                out_ref[d, :, side] = both.reshape(16, 16, TILE).astype(BF)
-
-
-def unpack_kernel(recv_ref, beta_ref, out_ref):
+                both = both.reshape(TILES, 2, 16, TILE).astype(BF)
+                for v in range(2):
+                    out_ref[2 * v + side, d] = both[:, v]
+            stores.append(
+                pltpu.make_async_copy(out_ref.at[:, d], out_hbm.at[:, d], out_sem.at[d])
+            )
+            stores[-1].start()
+    for copy in stores:
+        copy.wait()
+
+
+def beta_kernel(c_hbm, op_hbm, out_hbm, c_ref, op_ref, out_ref, in_sem, out_sem):
+    loads = [
+        pltpu.make_async_copy(c_hbm, c_ref, in_sem.at[0]),
+        pltpu.make_async_copy(op_hbm, op_ref, in_sem.at[1]),
+    ]
+    for copy in loads:
+        copy.start()
+    for copy in loads:
+        copy.wait()
+    for k in range(4):
+        cols = slice(k * 2 * TILE, (k + 1) * 2 * TILE)
+        out_ref[:, cols] = jnp.dot(c_ref[...], op_ref[:, cols], preferred_element_type=F32)
+    store = pltpu.make_async_copy(out_ref, out_hbm, out_sem)
+    store.start()
+    store.wait()
+
+
+def unpack_kernel(recv_ref, beta_hbm, out_hbm, beta_ref, out_ref, in_sem, out_sem):
+    loads = []
+    for k in range(4):
+        cols = pl.ds(k * 2 * TILE, 2 * TILE)
+        loads.append(
+            pltpu.make_async_copy(beta_hbm.at[:, cols], beta_ref.at[:, cols], in_sem.at[k])
+        )
+        loads[-1].start()
     order = deinterleave(512, 512)
-    for t in range(0, TILES, 2):
-        cols = slice(t * TILE, (t + 2) * TILE)
+    stores = []
+    for k in range(4):
         both = jnp.concatenate(
-            [recv_ref[:, u].reshape(512, TILE) for u in (t, t + 1)], axis=1
-        )
-        out_ref[:, cols] = beta_ref[:, cols] + jnp.dot(order, both, preferred_element_type=F32)
-
-
-def call(kernel, out_shape, scratch=()):
-    return pl.pallas_call(
+            [recv_ref[:, :, u].reshape(512, TILE) for u in (2 * k, 2 * k + 1)], axis=1
+        )
+        moved = jnp.dot(order, both, preferred_element_type=F32)
+        loads[k].wait()
+        cols = pl.ds(k * 2 * TILE, 2 * TILE)
+        out_ref[:, cols] = beta_ref[:, cols] + moved
+        stores.append(
+            pltpu.make_async_copy(out_ref.at[:, cols], out_hbm.at[:, cols], out_sem.at[k])
+        )
+        stores[-1].start()
+    for copy in stores:
+        copy.wait()
+
+
+HBM, VMEM = pltpu.HBM, pltpu.VMEM
+
+
+def call(kernel, out_shape, mib, ins, out, scratch):
+    if out is HBM:
+        out_shape = HBM(out_shape.shape, out_shape.dtype)
+    run = pl.pallas_call(
         kernel,
         out_shape=out_shape,
-        scratch_shapes=list(scratch),
-        compiler_params=pltpu.CompilerParams(vmem_limit_bytes=VMEM_BYTES),
-    )
+        in_specs=[pl.BlockSpec(memory_space=place) for place in ins],
+        out_specs=pl.BlockSpec(memory_space=out),
+        scratch_shapes=scratch,
+        compiler_params=pltpu.CompilerParams(vmem_limit_bytes=mib * MIB),
+    )
+
+    def placed(*args):
+        return run(
+            *(
+                pltpu.with_memory_space_constraint(x, HBM) if place is HBM else x
+                for x, place in zip(args, ins)
+            )
+        )
+
+    return placed
+
+
+def sems(count):
+    return pltpu.SemaphoreType.DMA((count,))
 
 
 def signed_weights(source, sign, pair):
@@ -210,45 +309,111 @@
 ):
     tile = lax.axis_index("z")
     mine = lax.dynamic_index_in_dim(mix_op[0], tile, axis=1, keepdims=False)
-    same = jnp.stack([mine] + [swapped(mine, k) for k in (2, 4, 6)])
-    other = swapped(same, 1)
-
-    send = call(pack_kernel, jax.ShapeDtypeStruct((TILES, 512, TILE), BF))(coeffs)
-    recv = exchange(send.reshape(32, TILE, TILE), ("z", "x"))
+    ops = {0: mine}
+    for k in (2, 4, 6, 1):
+        ops[k] = swapped(mine, k)
+
+    sent = (XDIM, TILES, TILE, TILE)
+    send = call(
+        pack_kernel,
+        jax.ShapeDtypeStruct(sent, BF),
+        8,
+        [HBM],
+        HBM,
+        [pltpu.VMEM((512, 1024), BF)] * 2 + [pltpu.VMEM(sent, BF), sems(4), sems(4)],
+    )(coeffs)
+    recv = exchange(send.reshape(32, TILE, TILE), ("x", "z"))
+
     table = jnp.transpose(send_list, (1, 0, 2)).reshape(RANKS, RANKS * CAP)
     slots = jnp.arange(RANKS * CAP, dtype=jnp.int32)
     table = jnp.broadcast_to(table[:, None, :], (RANKS, ABLK, RANKS * CAP)).reshape(NBLK, 1, RANKS * CAP)
     owned = jnp.sum(jnp.where(mix_slot[:, :, None] == slots[None, None, :], table, 0), axis=2)
     source = (mix_slot // CAP) * ABLK + owned
-    w_mix = signed_weights(source, mix_sign, mix_pair)
-    w_alpha = signed_weights(aa_src, aa_sign, aa_pair)
+    w_mix = signed_weights(arrival(source), mix_sign, mix_pair)
+    w_alpha = signed_weights(arrival(aa_src), aa_sign, aa_pair)
     pairs = jnp.transpose(pair_op, (0, 2, 1)).reshape(OPS * TILE, TILE)
-
-    recv, same, other, w_mix, w_alpha, pairs = lax.optimization_barrier(
-        (recv, same, other, w_mix, w_alpha, pairs)
+    ops[2], ops[4], ops[6], w_mix, w_alpha, pairs = lax.optimization_barrier(
+        (ops[2], ops[4], ops[6], w_mix, w_alpha, pairs)
+    )
+    for k in (2, 4, 6):
+        ops[k + 1] = swapped(ops[k], 1)
+    held = [ops[k] for k in range(SECTORS)]
+    recv, held, w_mix, w_alpha, pairs = lax.optimization_barrier(
+        (recv, held, w_mix, w_alpha, pairs)
     )
     recv = recv.reshape(RANKS, TILES, 16, TILE)
-    grouped = jax.ShapeDtypeStruct((16, 2, TILES, 16, TILE), BF)
-    turned = call(turn_kernel, grouped)(recv)
-    land = exchange(turned.reshape(32, TILE, TILE), ("sym", "x"))
+    parted = (16, 2, TILES, 16, TILE)
+    grouped = jax.ShapeDtypeStruct(parted, BF)
+    turned = call(turn_kernel, grouped, 6, [VMEM], HBM, [pltpu.VMEM(parted, BF), sems(8)])(recv)
+    land = exchange(turned.reshape(32, TILE, TILE), ("x", "sym"))
 
     blocks = pltpu.VMEM((SECTORS, ABLK, TILE, TILE), BF)
     combos = pltpu.VMEM((SECTORS, 4 * TILE, OPS * TILE), BF)
-    alpha = call(alpha_kernel, grouped, (blocks, combos))(recv, pairs, w_alpha)
-    alpha_land = exchange(alpha.reshape(32, TILE, TILE), ("sym", "x"))
+    alpha = call(alpha_kernel, grouped, 18, [VMEM] * 3, VMEM, [blocks, combos])(
+        recv, pairs, w_alpha
+    )
+    alpha_land = exchange(alpha.reshape(32, TILE, TILE), ("x", "sym"))
+    landing = (XDIM, SECTORS, TILE, TILE)
+    result = (SECTORS, 512, TILE)
     mixed = call(
         mixed_kernel,
-        jax.ShapeDtypeStruct((SECTORS, 512, TILE), F32),
-        (blocks, combos, pltpu.VMEM((SECTORS, OPS, TILE, TILE), BF)),
-    )(land.reshape(SECTORS, 512, TILE), same, other, w_mix)
-    back = call(merge_kernel, jax.ShapeDtypeStruct((SECTORS, 16, 2, 16, TILE), BF))(
-        mixed, alpha_land.reshape(SECTORS, 512, TILE)
-    )
-    home = exchange(back.reshape(256, 16, TILE), ("sym", "z", "x"))
-    beta_part = jnp.dot(coeffs, beta_op[0], preferred_element_type=F32)
-    return call(unpack_kernel, jax.ShapeDtypeStruct(coeffs.shape, F32))(
-        home.reshape(SECTORS, TILES, XDIM, 16, TILE), beta_part
-    )
+        jax.ShapeDtypeStruct(result, F32),
+        24,
+        [VMEM] * 10,
+        HBM,
+        [
+            blocks,
+            combos,
+            pltpu.VMEM((SECTORS, OPS, TILE, TILE), BF),
+            pltpu.VMEM(result, F32),
+            sems(8),
+        ],
+    )(land.reshape(landing), *held, w_mix)
+    out = (XDIM, SECTORS, TILES, 16, TILE)
+    back = call(
+        merge_kernel,
+        jax.ShapeDtypeStruct(out, BF),
+        12,
+        [HBM, HBM],
+        HBM,
+        [
+            pltpu.VMEM(result, F32),
+            pltpu.VMEM(landing, BF),
+            pltpu.VMEM(out, BF),
+            sems(4),
+            sems(4),
+            sems(8),
+        ],
+    )(mixed, alpha_land.reshape(landing))
+    back, later, beta_late = lax.optimization_barrier((back, coeffs, beta_op[0]))
+    home = exchange(back.reshape(256, 16, TILE), ("x", "sym", "z"))
+    beta_part = call(
+        beta_kernel,
+        jax.ShapeDtypeStruct(coeffs.shape, F32),
+        12,
+        [HBM, HBM],
+        HBM,
+        [
+            pltpu.VMEM(coeffs.shape, BF),
+            pltpu.VMEM(beta_late.shape, BF),
+            pltpu.VMEM(coeffs.shape, F32),
+            sems(2),
+            pltpu.SemaphoreType.DMA,
+        ],
+    )(later, beta_late)
+    return call(
+        unpack_kernel,
+        jax.ShapeDtypeStruct(coeffs.shape, F32),
+        12,
+        [VMEM, HBM],
+        HBM,
+        [pltpu.VMEM(coeffs.shape, F32), pltpu.VMEM(coeffs.shape, F32), sems(4), sems(4)],
+    )(home.reshape(out), beta_part)
+
+
+def arrival(block):
+    rank = block // ABLK
+    return ((rank % XDIM) * TILES + rank // XDIM) * ABLK + block % ABLK
 
 
 def exchange(array, axes):

time: 144 us -> 138 us (0.958)
  matrix products: 3.81 us -> 0 us
  local copies, waits for them, and re-layouts: 6.1 us -> 9.29 us
  waiting for transfers between devices: 48 us -> 45.1 us
  other arithmetic: 7.06 us -> 4.88 us
  Pallas kernels: 37.3 us -> 35.8 us
    ppermute x4 -> x7, waiting for transfers between devices: 11 us -> 3.74 us  [swapped(): return lax.ppermute(array, 'sym', [(s, s ^ mask) for s in range(SECTORS)])]
    unnamed x22 -> x34, local copies, waits for them, and re-layouts: 2 us -> 6.91 us
    all_to_all x4, waiting for transfers between devices: 37 us -> 41.3 us  [exchange(): return lax.all_to_all(array, axes, split_axis=0, concat_axis=0, tiled=True)]
    dot_general x1 -> x0, matrix products: 3.81 us -> none  [per_device(): beta_part = jnp.dot(coeffs, beta_op[0], preferred_element_type=F32)]
    ppermute x4 -> x7, starting transfers between devices: 5.3 us -> 7.54 us  [swapped(): return lax.ppermute(array, 'sym', [(s, s ^ mask) for s in range(SECTORS)])]
    another operation x1 -> x0, other arithmetic: 2.22 us -> none  [per_device(): same = jnp.stack([mine] + [swapped(mine, k) for k in (2, 4, 6)])]
    another operation x1 -> x0, local copies, waits for them, and re-layouts: 1.77 us -> none  [per_device(): same = jnp.stack([mine] + [swapped(mine, k) for k in (2, 4, 6)])]
    pallas_call x6 -> x7, Pallas kernels: 37.3 us -> 35.8 us  [placed(): run(*(pltpu.with_memory_space_constraint(x, HBM) if place is HBM else x f...]
  transfers between devices with their start and end apart: 8 -> 11, of which waited for: 5 -> 7; matrix products, arithmetic and copies ran while one was open for 10% -> 5% of each run, Pallas kernels for 16% -> 17%
where the time goes in v5:
time: 138 us; the launch traced here: 137 us
  waiting for transfers between devices  45.1 us (33%)
  starting transfers between devices  41.7 us (30%)
  Pallas kernels  35.8 us (26%)
  local copies, waits for them, and re-layouts  9.29 us (7%)
  other arithmetic  4.88 us (4%)
    all_to_all x4, waiting for transfers between devices, exchange(): return lax.all_to_all(array, axes, split_axis=0, concat_axis=0, tiled=True)  41.3 us
    pallas_call x7, Pallas kernels, placed(): run(*(pltpu.with_memory_space_constraint(x, HBM) if place is HBM else x f...  35.8 us
    all_to_all x4, starting transfers between devices, exchange(): return lax.all_to_all(array, axes, split_axis=0, concat_axis=0, tiled=True)  34.1 us
    ppermute x7, starting transfers between devices, swapped(): return lax.ppermute(array, 'sym', [(s, s ^ mask) for s in range(SECTORS)])  7.54 us
    unnamed x34, local copies, waits for them, and re-layouts  6.91 us
    reduce_sum x2, other arithmetic, signed_weights(): return jnp.sum(jnp.where(hit, factor[:, :, None], 0.0), axis=1).astype(BF)  4.74 us
    ppermute x7, waiting for transfers between devices, swapped(): return lax.ppermute(array, 'sym', [(s, s ^ mask) for s in range(SECTORS)])  3.74 us
  transfers between devices with their start and end apart: 11, of which 7 were waited for; matrix products, arithmetic and copies ran while one was open for 5% of the time, Pallas kernels for 17%

profile of v5, /device:TPU:1, one launch (start us, length us, event | category | flops | bytes accessed | tf_op | source)
XLA Modules:
  0.0 137.1 jit_solution(2491530532459850280)
XLA Ops:
  0.1 3.1 %shard_map.109 = bf16[4,8,128,128]{3,2,1,0:T(8,128)(2,1)} custom-call(bf16[512,1024]{1,0:T(8,128)(2,1)} %c_hbm.2), custom_call_target="tpu_custom_call" | custom-call | tf_op jit(solution)/shard_map/pallas_call | solution.py:271
  3.2 11.9 %all-to-all-start = ((bf16[32,128,128]{2,1,0:T(8,128)(2,1)}), bf16[32,128,128]{2,1,0:T(8,128)(2,1)S(1)}, u32[]{:S(2)}, u32[]{:S(2)}) async-start(bf16[32,128,128]{2,1,0:T(8,128)(2,1)} %bitcast.22), calls=%async_computation | async-start | bytes 2097152 | tf_op jit(solution)/shard_map/all_to_all | solution.py:420
  15.8 2.7 %collective-permute-start.3 = (bf16[8,128,128]{2,1,0:T(8,128)(2,1)}, bf16[8,128,128]{2,1,0:T(8,128)(2,1)}, u32[]{:S(2)}, u32[]{:S(2)}) collective-permute-start(bf16[8,128,128]{2,1,0:T(8,128)(2,1)} %dynamic-slice_bitcast_fusion.o0), channel_id=1, source_target_pairs={{0,192},{32,224},{64,128},{96,160},{128,64},{160,96},{192,0},{224,... | collective-permute-start | bytes 786440 | tf_op jit(solution)/shard_map/ppermute | solution.py:294
  19.1 1.7 %collective-permute-start = (bf16[8,128,128]{2,1,0:T(8,128)(2,1)}, bf16[8,128,128]{2,1,0:T(8,128)(2,1)}, u32[]{:S(2)}, u32[]{:S(2)}) collective-permute-start(bf16[8,128,128]{2,1,0:T(8,128)(2,1)} %dynamic-slice_bitcast_fusion.o0), channel_id=1, source_target_pairs={{0,32},{32,0},{64,96},{96,64},{128,160},{160,128},{192,224},{224,1... | collective-permute-start | bytes 786440 | tf_op jit(solution)/shard_map/ppermute | solution.py:294
  21.4 2.7 %select_reduce_fusion.w_ref = bf16[128,1024]{1,0:T(8,128)(2,1)} fusion(f32[128,16]{1,0:T(8,128)S(1)} %copy.27, s32[128,16]{1,0:T(8,128)S(1)} %copy.26), kind=kLoop, calls=%fused_computation | loop fusion | flops 6160384 | bytes 278528 | tf_op jit(solution)/shard_map/reduce_sum | solution.py:290
  24.3 1.1 copy.30
  25.4 2.0 %select_reduce_fusion.1.w_ref = bf16[128,1024]{1,0:T(8,128)(2,1)} fusion(f32[128,8]{1,0:T(8,128)S(1)} %copy.29, s32[128,8]{1,0:T(8,128)S(1)} %copy.28), kind=kLoop, calls=%fused_computation.2 | loop fusion | flops 3014656 | bytes 270336 | tf_op jit(solution)/shard_map/reduce_sum | solution.py:290
  27.5 2.7 %collective-permute-done.3.o6 = bf16[8,128,128]{2,1,0:T(8,128)(2,1)} collective-permute-done((bf16[8,128,128]{2,1,0:T(8,128)(2,1)}, bf16[8,128,128]{2,1,0:T(8,128)(2,1)}, u32[]{:S(2)}, u32[]{:S(2)}) %collective-permute-start.3) | collective-permute-done | bytes 262176 | tf_op jit(solution)/shard_map/ppermute | solution.py:294
  30.4 2.0 %collective-permute-start.4 = (bf16[8,128,128]{2,1,0:T(8,128)(2,1)}, bf16[8,128,128]{2,1,0:T(8,128)(2,1)S(1)}, u32[]{:S(2)}, u32[]{:S(2)}) collective-permute-start(bf16[8,128,128]{2,1,0:T(8,128)(2,1)} %collective-permute-done.1.o2), channel_id=1, source_target_pairs={{0,32},{32,0},{64,96},{96,64},{128,160},{160,128},{192,224},{224,1... | collective-permute-start | bytes 786440 | tf_op jit(solution)/shard_map/ppermute | solution.py:294
  35.8 4.1 %all-to-all-done = bf16[32,128,128]{2,1,0:T(8,128)(2,1)S(1)} async-done(((bf16[32,128,128]{2,1,0:T(8,128)(2,1)}), bf16[32,128,128]{2,1,0:T(8,128)(2,1)S(1)}, u32[]{:S(2)}, u32[]{:S(2)}) %all-to-all-start) | async-done | bytes 1048608 | tf_op jit(solution)/shard_map/all_to_all | solution.py:420
  39.9 1.2 shard_map.110
  41.2 9.6 %all-to-all-start.1 = ((bf16[32,128,128]{2,1,0:T(8,128)(2,1)}), bf16[32,128,128]{2,1,0:T(8,128)(2,1)}, u32[]{:S(2)}, u32[]{:S(2)}) async-start(bf16[32,128,128]{2,1,0:T(8,128)(2,1)} %bitcast.23), calls=%async_computation.1 | async-start | bytes 2097152 | tf_op jit(solution)/shard_map/all_to_all | solution.py:420
  51.8 7.7 %shard_map.112 = bf16[16,2,8,16,128]{4,3,2,1,0:T(8,128)(2,1)S(1)} custom-call(bf16[32,8,16,128]{3,2,1,0:T(8,128)(2,1)S(1)} %bitcast.18, bf16[1024,128]{1,0:T(8,128)(2,1)S(1)} %bitcast.21, bf16[128,1024]{1,0:T(8,128)(2,1)S(1)} %copy-done.2), custom_call_target="tpu_custom_call" | custom-call | tf_op jit(solution)/shard_map/pallas_call | solution.py:271
  59.5 1.0 copy-done.1
  60.5 7.3 %all-to-all-done.1 = bf16[32,128,128]{2,1,0:T(8,128)(2,1)} async-done(((bf16[32,128,128]{2,1,0:T(8,128)(2,1)}), bf16[32,128,128]{2,1,0:T(8,128)(2,1)}, u32[]{:S(2)}, u32[]{:S(2)}) %all-to-all-start.1) | async-done | bytes 1048608 | tf_op jit(solution)/shard_map/all_to_all | solution.py:420
  67.8 4.6 %all-to-all-start.2 = ((bf16[32,128,128]{2,1,0:T(8,128)(2,1)}), bf16[32,128,128]{2,1,0:T(8,128)(2,1)}, u32[]{:S(2)}, u32[]{:S(2)}) async-start(bf16[32,128,128]{2,1,0:T(8,128)(2,1)} %bitcast.20), calls=%async_computation.2 | async-start | bytes 2097152 | tf_op jit(solution)/shard_map/all_to_all | solution.py:420
  74.3 0.9 copy-done.9
  75.3 11.6 %shard_map.111.res_hbm = f32[8,512,128]{2,1,0:T(8,128)} custom-call(bf16[4,8,128,128]{3,2,1,0:T(8,128)(2,1)} %bitcast.9.land_ref, bf16[8,128,128]{2,1,0:T(8,128)(2,1)} %dynamic-slice_bitcast_fusion.o0, bf16[8,128,128]{2,1,0:T(8,128)(2,1)} %collective-permute-done.o1, bf16[8,128,128]{2,1,0:T(8,128)(2,1)} %collective-permute-done.1.o2, ...), custom_call_target="tpu_custom_call" | custom-call | tf_op jit(solution)/shard_map/pallas_call | solution.py:271
  86.9 2.3 %all-to-all-done.2 = bf16[32,128,128]{2,1,0:T(8,128)(2,1)} async-done(((bf16[32,128,128]{2,1,0:T(8,128)(2,1)}), bf16[32,128,128]{2,1,0:T(8,128)(2,1)}, u32[]{:S(2)}, u32[]{:S(2)}) %all-to-all-start.2) | async-done | bytes 1048608 | tf_op jit(solution)/shard_map/all_to_all | solution.py:420
  89.2 4.2 %shard_map.113 = bf16[4,8,8,16,128]{4,3,2,1,0:T(8,128)(2,1)} custom-call(f32[8,512,128]{2,1,0:T(8,128)} %shard_map.111.res_hbm, bf16[4,8,128,128]{3,2,1,0:T(8,128)(2,1)} %bitcast.11.land_hbm), custom_call_target="tpu_custom_call" | custom-call | tf_op jit(solution)/shard_map/pallas_call | solution.py:271
  93.4 8.0 %all-to-all-start.3 = ((bf16[256,16,128]{2,1,0:T(8,128)(2,1)}), bf16[256,16,128]{2,1,0:T(8,128)(2,1)S(1)}, u32[]{:S(2)}, u32[]{:S(2)}) async-start(bf16[256,16,128]{2,1,0:T(8,128)(2,1)} %bitcast.24), calls=%async_computation.3 | async-start | bytes 2097152 | tf_op jit(solution)/shard_map/all_to_all | solution.py:420
  101.4 4.5 %shard_map.114.beta_hbm = f32[512,1024]{1,0:T(8,128)} custom-call(bf16[512,1024]{1,0:T(8,128)(2,1)} %c_hbm.2, bf16[1024,1024]{1,0:T(8,128)(2,1)} %bitcast.25), custom_call_target="tpu_custom_call" | custom-call | tf_op jit(solution)/shard_map/pallas_call | solution.py:271
  106.0 27.6 %all-to-all-done.3 = bf16[256,16,128]{2,1,0:T(8,128)(2,1)S(1)} async-done(((bf16[256,16,128]{2,1,0:T(8,128)(2,1)}), bf16[256,16,128]{2,1,0:T(8,128)(2,1)S(1)}, u32[]{:S(2)}, u32[]{:S(2)}) %all-to-all-start.3) | async-done | bytes 1048608 | tf_op jit(solution)/shard_map/all_to_all | solution.py:420
  133.6 3.4 %shard_map.115 = f32[512,1024]{1,0:T(8,128)} custom-call(bf16[4,8,8,16,128]{4,3,2,1,0:T(8,128)(2,1)S(1)} %bitcast.19, f32[512,1024]{1,0:T(8,128)} %shard_map.114.beta_hbm), custom_call_target="tpu_custom_call" | custom-call | tf_op jit(solution)/shard_map/pallas_call | solution.py:271
  (55 shorter events, 8.5 us)
Async XLA Ops:
  0.0 15.1 %copy-start = (bf16[1,8,8,128,128]{4,3,2,1,0:T(8,128)(2,1)S(1)}, bf16[1,8,8,128,128]{4,3,2,1,0:T(8,128)(2,1)}, u32[]{:S(2)}) copy-start(bf16[1,8,8,128,128]{4,3,2,1,0:T(8,128)(2,1)} %param.13) | copy-start | bytes 6291460
  0.0 20.8 %copy-start.10 = (s32[32,32,2]{1,2,0:T(2,128)S(1)}, s32[32,32,2]{1,2,0:T(2,128)}, u32[]{:S(2)}) copy-start(s32[32,32,2]{1,2,0:T(2,128)} %param.15) | copy-start | bytes 24580
  0.0 21.0 %copy-start.11 = (s32[128,16]{0,1:T(8,128)S(1)}, s32[128,16]{0,1:T(8,128)}, u32[]{:S(2)}) copy-start(s32[128,16]{0,1:T(8,128)} %param.16) | copy-start | bytes 24580
  0.0 21.1 %copy-start.13 = (s32[128,16]{0,1:T(8,128)S(1)}, s32[128,16]{0,1:T(8,128)}, u32[]{:S(2)}) copy-start(s32[128,16]{0,1:T(8,128)} %param.18) | copy-start | bytes 24580
  0.0 21.2 %copy-start.12 = (s32[128,16]{0,1:T(8,128)S(1)}, s32[128,16]{0,1:T(8,128)}, u32[]{:S(2)}) copy-start(s32[128,16]{0,1:T(8,128)} %param.17) | copy-start | bytes 24580
  0.0 21.3 %copy-start.14 = (s32[128,8]{0,1:T(8,128)S(1)}, s32[128,8]{0,1:T(8,128)}, u32[]{:S(2)}) copy-start(s32[128,8]{0,1:T(8,128)} %param.21) | copy-start | bytes 12292
  0.0 21.3 %copy-start.15 = (s32[128,8]{0,1:T(8,128)S(1)}, s32[128,8]{0,1:T(8,128)}, u32[]{:S(2)}) copy-start(s32[128,8]{0,1:T(8,128)} %param.19) | copy-start | bytes 12292
  3.2 20.9 %copy-start.16 = (s32[128,8]{0,1:T(8,128)S(1)}, s32[128,8]{0,1:T(8,128)}, u32[]{:S(2)}) copy-start(s32[128,8]{0,1:T(8,128)} %param.20) | copy-start | bytes 12292
  3.2 36.7 %all-to-all-start = ((bf16[32,128,128]{2,1,0:T(8,128)(2,1)}), bf16[32,128,128]{2,1,0:T(8,128)(2,1)S(1)}, u32[]{:S(2)}, u32[]{:S(2)}) async-start(bf16[32,128,128]{2,1,0:T(8,128)(2,1)} %bitcast.22), calls=%async_computation | async-start | bytes 2097152 | tf_op jit(solution)/shard_map/all_to_all | solution.py:420
  15.8 14.4 %collective-permute-start.3 = (bf16[8,128,128]{2,1,0:T(8,128)(2,1)}, bf16[8,128,128]{2,1,0:T(8,128)(2,1)}, u32[]{:S(2)}, u32[]{:S(2)}) collective-permute-start(bf16[8,128,128]{2,1,0:T(8,128)(2,1)} %dynamic-slice_bitcast_fusion.o0), channel_id=1, source_target_pairs={{0,192},{32,224},{64,128},{96,160},{128,64},{160,96},{192,0},{224,... | collective-permute-start | bytes 786440 | tf_op jit(solution)/shard_map/ppermute | solution.py:294
  18.5 11.7 %collective-permute-start.2 = (bf16[8,128,128]{2,1,0:T(8,128)(2,1)}, bf16[8,128,128]{2,1,0:T(8,128)(2,1)}, u32[]{:S(2)}, u32[]{:S(2)}) collective-permute-start(bf16[8,128,128]{2,1,0:T(8,128)(2,1)} %dynamic-slice_bitcast_fusion.o0), channel_id=1, source_target_pairs={{0,128},{32,160},{64,192},{96,224},{128,0},{160,32},{192,64},{224,... | collective-permute-start | bytes 786440 | tf_op jit(solution)/shard_map/ppermute | solution.py:294
  18.9 11.5 %collective-permute-start.1 = (bf16[8,128,128]{2,1,0:T(8,128)(2,1)}, bf16[8,128,128]{2,1,0:T(8,128)(2,1)}, u32[]{:S(2)}, u32[]{:S(2)}) collective-permute-start(bf16[8,128,128]{2,1,0:T(8,128)(2,1)} %dynamic-slice_bitcast_fusion.o0), channel_id=1, source_target_pairs={{0,64},{32,96},{64,0},{96,32},{128,192},{160,224},{192,128},{224,1... | collective-permute-start | bytes 786440 | tf_op jit(solution)/shard_map/ppermute | solution.py:294
  19.1 13.8 %collective-permute-start = (bf16[8,128,128]{2,1,0:T(8,128)(2,1)}, bf16[8,128,128]{2,1,0:T(8,128)(2,1)}, u32[]{:S(2)}, u32[]{:S(2)}) collective-permute-start(bf16[8,128,128]{2,1,0:T(8,128)(2,1)} %dynamic-slice_bitcast_fusion.o0), channel_id=1, source_target_pairs={{0,32},{32,0},{64,96},{96,64},{128,160},{160,128},{192,224},{224,1... | collective-permute-start | bytes 786440 | tf_op jit(solution)/shard_map/ppermute | solution.py:294
  30.4 3.4 %collective-permute-start.4 = (bf16[8,128,128]{2,1,0:T(8,128)(2,1)}, bf16[8,128,128]{2,1,0:T(8,128)(2,1)S(1)}, u32[]{:S(2)}, u32[]{:S(2)}) collective-permute-start(bf16[8,128,128]{2,1,0:T(8,128)(2,1)} %collective-permute-done.1.o2), channel_id=1, source_target_pairs={{0,32},{32,0},{64,96},{96,64},{128,160},{160,128},{192,224},{224,1... | collective-permute-start | bytes 786440 | tf_op jit(solution)/shard_map/ppermute | solution.py:294
  32.3 2.1 %collective-permute-start.5 = (bf16[8,128,128]{2,1,0:T(8,128)(2,1)}, bf16[8,128,128]{2,1,0:T(8,128)(2,1)S(1)}, u32[]{:S(2)}, u32[]{:S(2)}) collective-permute-start(bf16[8,128,128]{2,1,0:T(8,128)(2,1)} %collective-permute-done.2.o4), channel_id=1, source_target_pairs={{0,32},{32,0},{64,96},{96,64},{128,160},{160,128},{192,224},{224,1... | collective-permute-start | bytes 786440 | tf_op jit(solution)/shard_map/ppermute | solution.py:294
  32.3 2.8 %collective-permute-start.6 = (bf16[8,128,128]{2,1,0:T(8,128)(2,1)}, bf16[8,128,128]{2,1,0:T(8,128)(2,1)S(1)}, u32[]{:S(2)}, u32[]{:S(2)}) collective-permute-start(bf16[8,128,128]{2,1,0:T(8,128)(2,1)} %collective-permute-done.3.o6), channel_id=1, source_target_pairs={{0,32},{32,0},{64,96},{96,64},{128,160},{160,128},{192,224},{224,1... | collective-permute-start | bytes 786440 | tf_op jit(solution)/shard_map/ppermute | solution.py:294
  41.2 26.6 %all-to-all-start.1 = ((bf16[32,128,128]{2,1,0:T(8,128)(2,1)}), bf16[32,128,128]{2,1,0:T(8,128)(2,1)}, u32[]{:S(2)}, u32[]{:S(2)}) async-start(bf16[32,128,128]{2,1,0:T(8,128)(2,1)} %bitcast.23), calls=%async_computation.1 | async-start | bytes 2097152 | tf_op jit(solution)/shard_map/all_to_all | solution.py:420
  50.8 1.0 copy-start.2
  59.5 1.0 copy-start.1
  60.5 11.9 %copy-start.3 = (bf16[128,1024]{1,0:T(8,128)(2,1)S(1)}, bf16[128,1024]{1,0:T(8,128)(2,1)}, u32[]{:S(2)}) copy-start(bf16[128,1024]{1,0:T(8,128)(2,1)} %select_reduce_fusion.w_ref) | copy-start | bytes 786436
  67.8 21.4 %all-to-all-start.2 = ((bf16[32,128,128]{2,1,0:T(8,128)(2,1)}), bf16[32,128,128]{2,1,0:T(8,128)(2,1)}, u32[]{:S(2)}, u32[]{:S(2)}) async-start(bf16[32,128,128]{2,1,0:T(8,128)(2,1)} %bitcast.20), calls=%async_computation.2 | async-start | bytes 2097152 | tf_op jit(solution)/shard_map/all_to_all | solution.py:420
  72.4 1.0 copy-start.5
  73.4 0.9 copy-start.7
  93.4 40.2 %all-to-all-start.3 = ((bf16[256,16,128]{2,1,0:T(8,128)(2,1)}), bf16[256,16,128]{2,1,0:T(8,128)(2,1)S(1)}, u32[]{:S(2)}, u32[]{:S(2)}) async-start(bf16[256,16,128]{2,1,0:T(8,128)(2,1)} %bitcast.24), calls=%async_computation.3 | async-start | bytes 2097152 | tf_op jit(solution)/shard_map/all_to_all | solution.py:420
  (4 other events, 3.1 us)

commit v6 on v5

--- a/solution.py
+++ b/solution.py
@@ -59,6 +59,16 @@
         copy.wait()
 
 
+def pick_kernel(op_hbm, out_hbm, op_ref, in_sem, out_sem):
+    tile = lax.axis_index("z")
+    load = pltpu.make_async_copy(op_hbm.at[0, :, tile], op_ref, in_sem)
+    load.start()
+    load.wait()
+    store = pltpu.make_async_copy(op_ref, out_hbm, out_sem)
+    store.start()
+    store.wait()
+
+
 def swap_halves(first, second):
     low = lax.broadcasted_iota(jnp.int32, first.shape, 1) < 4
     lo = jnp.where(low, first, pltpu.roll(second, 4, 1))
@@ -137,15 +147,23 @@
 
 
 def mixed_kernel(
-    land_ref, o0, o1, o2, o3, o4, o5, o6, o7, w_ref, res_hbm, x_ref, c_ref, mix_ref, res_ref, out_sem
+    land_hbm, o0, o1, o2, o3, o4, o5, o6, o7, w_ref, res_hbm,
+    land_ref, x_ref, c_ref, mix_ref, res_ref, land_sem, op_sem, out_sem,
 ):
     sector = lax.axis_index("sym")
-    for k, op_ref in enumerate((o0, o1, o2, o3, o4, o5, o6, o7)):
-        mix_ref[k] = op_ref[...]
+    lands, loads = [], []
+    for half in range(SECTORS // 2):
+        here = pl.ds(2 * half, 2)
+        lands.append(
+            pltpu.make_async_copy(land_hbm.at[:, here], land_ref.at[:, here], land_sem.at[half])
+        )
+        lands[-1].start()
+    for k, op_hbm in enumerate((o0, o1, o2, o3, o4, o5, o6, o7)):
+        loads.append(pltpu.make_async_copy(op_hbm, mix_ref.at[k], op_sem.at[k]))
+        loads[-1].start()
     order = deinterleave(512, 512)
-
-    @pl.loop(0, SECTORS // 2)
-    def _(half):
+    for half in range(SECTORS // 2):
+        lands[half].wait()
         moved = landed(land_ref, 2 * half, order)
         for a in range(ABLK):
             for o in range(2):
@@ -153,11 +171,13 @@
                 x_ref[2 * half + o, a] = block.T.astype(BF)
 
     combine(stacked(w_ref), x_ref, c_ref, True)
+    for copy in loads:
+        copy.wait()
 
     @pl.loop(0, SECTORS)
     def _(d):
         ops = jnp.concatenate([mix_ref[sector ^ d ^ g, g] for g in range(OPS)], axis=0)
-        res_ref[d] = jnp.dot(c_ref[d], ops, preferred_element_type=F32)
+        res_ref[d] = jnp.dot(c_ref[d], ops, preferred_element_type=F32).astype(BF)
         pltpu.make_async_copy(res_ref.at[d], res_hbm.at[d], out_sem.at[d]).start()
 
     @pl.loop(0, SECTORS)
@@ -165,24 +185,17 @@
         pltpu.make_async_copy(res_ref.at[d], res_hbm.at[d], out_sem.at[d]).wait()
 
 
-def merge_kernel(
-    res_hbm, land_hbm, out_hbm, res_ref, land_ref, out_ref, in_sem, land_sem, out_sem
-):
-    loads, lands = [], []
+def merge_kernel(res_hbm, land_ref, out_hbm, res_ref, out_ref, in_sem, out_sem):
+    loads = []
     for half in range(SECTORS // 2):
         here = pl.ds(2 * half, 2)
-        lands.append(
-            pltpu.make_async_copy(land_hbm.at[:, here], land_ref.at[:, here], land_sem.at[half])
-        )
         loads.append(
             pltpu.make_async_copy(res_hbm.at[here], res_ref.at[here], in_sem.at[half])
         )
-        lands[-1].start()
         loads[-1].start()
     order = deinterleave(512, 512)
     stores = []
     for half in range(SECTORS // 2):
-        lands[half].wait()
         moved = landed(land_ref, 2 * half, order)
         loads[half].wait()
         for o in range(2):
@@ -190,7 +203,7 @@
             blocks = []
             for a in range(ABLK):
                 rows = slice(a * TILE, (a + 1) * TILE)
-                blocks.append(res_ref[d, rows] + moved[rows, o * TILE : (o + 1) * TILE].T)
+                blocks.append(res_ref[d, rows].astype(F32) + moved[rows, o * TILE : (o + 1) * TILE].T)
             sides = []
             for h in range(2):
                 first = blocks[2 * h].reshape(16, 8, TILE)
@@ -307,12 +320,6 @@
     aa_sign,
     aa_pair,
 ):
-    tile = lax.axis_index("z")
-    mine = lax.dynamic_index_in_dim(mix_op[0], tile, axis=1, keepdims=False)
-    ops = {0: mine}
-    for k in (2, 4, 6, 1):
-        ops[k] = swapped(mine, k)
-
     sent = (XDIM, TILES, TILE, TILE)
     send = call(
         pack_kernel,
@@ -322,6 +329,18 @@
         HBM,
         [pltpu.VMEM((512, 1024), BF)] * 2 + [pltpu.VMEM(sent, BF), sems(4), sems(4)],
     )(coeffs)
+    send, picked = lax.optimization_barrier((send, mix_op))
+    mine = call(
+        pick_kernel,
+        jax.ShapeDtypeStruct((OPS, TILE, TILE), BF),
+        4,
+        [HBM],
+        HBM,
+        [pltpu.VMEM((OPS, TILE, TILE), BF), pltpu.SemaphoreType.DMA, pltpu.SemaphoreType.DMA],
+    )(picked)
+    ops = {0: mine}
+    for k in (2, 4, 6, 1):
+        ops[k] = swapped(mine, k)
     recv = exchange(send.reshape(32, TILE, TILE), ("x", "z"))
 
     table = jnp.transpose(send_list, (1, 0, 2)).reshape(RANKS, RANKS * CAP)
@@ -357,15 +376,18 @@
     result = (SECTORS, 512, TILE)
     mixed = call(
         mixed_kernel,
-        jax.ShapeDtypeStruct(result, F32),
+        jax.ShapeDtypeStruct(result, BF),
         24,
-        [VMEM] * 10,
+        [HBM] * 9 + [VMEM],
         HBM,
         [
+            pltpu.VMEM(landing, BF),
             blocks,
             combos,
             pltpu.VMEM((SECTORS, OPS, TILE, TILE), BF),
-            pltpu.VMEM(result, F32),
+            pltpu.VMEM(result, BF),
+            sems(4),
+            sems(8),
             sems(8),
         ],
     )(land.reshape(landing), *held, w_mix)
@@ -373,17 +395,10 @@
     back = call(
         merge_kernel,
         jax.ShapeDtypeStruct(out, BF),
-        12,
-        [HBM, HBM],
-        HBM,
-        [
-            pltpu.VMEM(result, F32),
-            pltpu.VMEM(landing, BF),
-            pltpu.VMEM(out, BF),
-            sems(4),
-            sems(4),
-            sems(8),
-        ],
+        8,
+        [HBM, VMEM],
+        HBM,
+        [pltpu.VMEM(result, BF), pltpu.VMEM(out, BF), sems(4), sems(8)],
     )(mixed, alpha_land.reshape(landing))
     back, later, beta_late = lax.optimization_barrier((back, coeffs, beta_op[0]))
     home = exchange(back.reshape(256, 16, TILE), ("x", "sym", "z"))

time: 138 us -> 135 us (0.978)
  local copies, waits for them, and re-layouts: 9.29 us -> 0.81 us
  waiting for transfers between devices: 45.1 us -> 52.3 us
  starting transfers between devices: 41.7 us -> 40 us
  Pallas kernels: 35.8 us -> 37.3 us
  other arithmetic: 4.88 us -> 3.47 us
    unnamed x34 -> x30, local copies, waits for them, and re-layouts: 6.91 us -> 0.09 us
    all_to_all x4, waiting for transfers between devices: 41.3 us -> 45.5 us  [exchange(): return lax.all_to_all(array, axes, split_axis=0, concat_axis=0, tiled=True)]
    ppermute x7, waiting for transfers between devices: 3.74 us -> 6.8 us  [swapped(): return lax.ppermute(array, 'sym', [(s, s ^ mask) for s in range(SECTORS)])]
    all_to_all x4, starting transfers between devices: 34.1 us -> 32.5 us  [exchange(): return lax.all_to_all(array, axes, split_axis=0, concat_axis=0, tiled=True)]
    pallas_call x7 -> x8, Pallas kernels: 35.8 us -> 37.3 us  [placed(): run(*(pltpu.with_memory_space_constraint(x, HBM) if place is HBM else x f...]
    reduce_sum x2, other arithmetic: 4.74 us -> 3.33 us  [signed_weights(): return jnp.sum(jnp.where(hit, factor[:, :, None], 0.0), axis=1).astype(BF)]
  transfers between devices with their start and end apart: 11 -> 11, of which waited for: 7 -> 9; matrix products, arithmetic and copies ran while one was open for 5% -> 3% of each run, Pallas kernels for 17% -> 20%
where the time goes in v6:
time: 135 us; the launch traced here: 134 us
  waiting for transfers between devices  52.3 us (39%)
  starting transfers between devices  40 us (30%)
  Pallas kernels  37.3 us (28%)
  other arithmetic  3.47 us (3%)
    all_to_all x4, waiting for transfers between devices, exchange(): return lax.all_to_all(array, axes, split_axis=0, concat_axis=0, tiled=True)  45.5 us
    pallas_call x8, Pallas kernels, placed(): run(*(pltpu.with_memory_space_constraint(x, HBM) if place is HBM else x f...  37.3 us
    all_to_all x4, starting transfers between devices, exchange(): return lax.all_to_all(array, axes, split_axis=0, concat_axis=0, tiled=True)  32.5 us
    ppermute x7, starting transfers between devices, swapped(): return lax.ppermute(array, 'sym', [(s, s ^ mask) for s in range(SECTORS)])  7.53 us
    ppermute x7, waiting for transfers between devices, swapped(): return lax.ppermute(array, 'sym', [(s, s ^ mask) for s in range(SECTORS)])  6.8 us
    reduce_sum x2, other arithmetic, signed_weights(): return jnp.sum(jnp.where(hit, factor[:, :, None], 0.0), axis=1).astype(BF)  3.33 us
  transfers between devices with their start and end apart: 11, of which 9 were waited for; matrix products, arithmetic and copies ran while one was open for 3% of the time, Pallas kernels for 20%

profile of v6, /device:TPU:1, one launch (start us, length us, event | category | flops | bytes accessed | tf_op | source)
XLA Modules:
  0.0 134.5 jit_solution(5417524863547858593)
XLA Ops:
  0.0 3.0 %shard_map.109 = bf16[4,8,128,128]{3,2,1,0:T(8,128)(2,1)} custom-call(bf16[512,1024]{1,0:T(8,128)(2,1)} %c_hbm.2), custom_call_target="tpu_custom_call" | custom-call | tf_op jit(solution)/shard_map/pallas_call | solution.py:284
  3.1 12.0 %all-to-all-start = ((bf16[32,128,128]{2,1,0:T(8,128)(2,1)}), bf16[32,128,128]{2,1,0:T(8,128)(2,1)S(1)}, u32[]{:S(2)}, u32[]{:S(2)}) async-start(bf16[32,128,128]{2,1,0:T(8,128)(2,1)} %bitcast.22), calls=%async_computation | async-start | bytes 2097152 | tf_op jit(solution)/shard_map/all_to_all | solution.py:435
  15.1 1.7 %shard_map.110.o0 = bf16[8,128,128]{2,1,0:T(8,128)(2,1)} custom-call(bf16[1,8,8,128,128]{4,3,2,1,0:T(8,128)(2,1)} %op_hbm), custom_call_target="tpu_custom_call" | custom-call | tf_op jit(solution)/shard_map/pallas_call | solution.py:284
  16.8 2.8 %collective-permute-start.3 = (bf16[8,128,128]{2,1,0:T(8,128)(2,1)}, bf16[8,128,128]{2,1,0:T(8,128)(2,1)S(1)}, u32[]{:S(2)}, u32[]{:S(2)}) collective-permute-start(bf16[8,128,128]{2,1,0:T(8,128)(2,1)} %shard_map.110.o0), channel_id=1, source_target_pairs={{0,192},{32,224},{64,128},{96,160},{128,64},{160,96},{192,0},{224,... | collective-permute-start | bytes 786440 | tf_op jit(solution)/shard_map/ppermute | solution.py:307
  20.3 1.6 %collective-permute-start = (bf16[8,128,128]{2,1,0:T(8,128)(2,1)}, bf16[8,128,128]{2,1,0:T(8,128)(2,1)S(1)}, u32[]{:S(2)}, u32[]{:S(2)}) collective-permute-start(bf16[8,128,128]{2,1,0:T(8,128)(2,1)} %shard_map.110.o0), channel_id=1, source_target_pairs={{0,32},{32,0},{64,96},{96,64},{128,160},{160,128},{192,224},{224,1... | collective-permute-start | bytes 786440 | tf_op jit(solution)/shard_map/ppermute | solution.py:307
  22.5 2.0 %select_reduce_fusion.w_ref = bf16[128,1024]{1,0:T(8,128)(2,1)S(1)} fusion(f32[128,16]{1,0:T(8,128)S(1)} %copy.27, s32[128,16]{1,0:T(8,128)S(1)} %copy.26), kind=kLoop, calls=%fused_computation | loop fusion | flops 6160384 | bytes 278528 | tf_op jit(solution)/shard_map/reduce_sum | solution.py:303
  24.9 1.3 %select_reduce_fusion.1.w_ref = bf16[128,1024]{1,0:T(8,128)(2,1)S(1)} fusion(f32[128,8]{1,0:T(8,128)S(1)} %copy.29, s32[128,8]{1,0:T(8,128)S(1)} %copy.28), kind=kLoop, calls=%fused_computation.2 | loop fusion | flops 3014656 | bytes 270336 | tf_op jit(solution)/shard_map/reduce_sum | solution.py:303
  26.3 4.9 %collective-permute-done.3.o6 = bf16[8,128,128]{2,1,0:T(8,128)(2,1)S(1)} collective-permute-done((bf16[8,128,128]{2,1,0:T(8,128)(2,1)}, bf16[8,128,128]{2,1,0:T(8,128)(2,1)S(1)}, u32[]{:S(2)}, u32[]{:S(2)}) %collective-permute-start.3) | collective-permute-done | bytes 262176 | tf_op jit(solution)/shard_map/ppermute | solution.py:307
  31.6 1.9 %collective-permute-start.4 = (bf16[8,128,128]{2,1,0:T(8,128)(2,1)S(1)}, bf16[8,128,128]{2,1,0:T(8,128)(2,1)S(1)}, u32[]{:S(2)}, u32[]{:S(2)}) collective-permute-start(bf16[8,128,128]{2,1,0:T(8,128)(2,1)S(1)} %collective-permute-done.1.o2), channel_id=1, source_target_pairs={{0,32},{32,0},{64,96},{96,64},{128,160},{160,128},{192,224},{224,1... | collective-permute-start | bytes 786440 | tf_op jit(solution)/shard_map/ppermute | solution.py:307
  33.4 0.5 collective-permute-start.6
  34.0 0.6 collective-permute-done.4.o3
  35.5 4.4 %all-to-all-done = bf16[32,128,128]{2,1,0:T(8,128)(2,1)S(1)} async-done(((bf16[32,128,128]{2,1,0:T(8,128)(2,1)}), bf16[32,128,128]{2,1,0:T(8,128)(2,1)S(1)}, u32[]{:S(2)}, u32[]{:S(2)}) %all-to-all-start) | async-done | bytes 1048608 | tf_op jit(solution)/shard_map/all_to_all | solution.py:435
  39.9 1.2 shard_map.111
  41.2 9.6 %all-to-all-start.1 = ((bf16[32,128,128]{2,1,0:T(8,128)(2,1)}), bf16[32,128,128]{2,1,0:T(8,128)(2,1)S(1)}, u32[]{:S(2)}, u32[]{:S(2)}) async-start(bf16[32,128,128]{2,1,0:T(8,128)(2,1)} %bitcast.23), calls=%async_computation.1 | async-start | bytes 2097152 | tf_op jit(solution)/shard_map/all_to_all | solution.py:435
  50.8 8.7 %shard_map.113 = bf16[16,2,8,16,128]{4,3,2,1,0:T(8,128)(2,1)} custom-call(bf16[32,8,16,128]{3,2,1,0:T(8,128)(2,1)S(1)} %bitcast.16, bf16[1024,128]{1,0:T(8,128)(2,1)S(1)} %bitcast.19, bf16[128,1024]{1,0:T(8,128)(2,1)S(1)} %select_reduce_fusion.1.w_ref), custom_call_target="tpu_custom_call" | custom-call | tf_op jit(solution)/shard_map/pallas_call | solution.py:284
  59.5 8.2 %all-to-all-done.1 = bf16[32,128,128]{2,1,0:T(8,128)(2,1)S(1)} async-done(((bf16[32,128,128]{2,1,0:T(8,128)(2,1)}), bf16[32,128,128]{2,1,0:T(8,128)(2,1)S(1)}, u32[]{:S(2)}, u32[]{:S(2)}) %all-to-all-start.1) | async-done | bytes 1048608 | tf_op jit(solution)/shard_map/all_to_all | solution.py:435
  67.7 3.9 %all-to-all-start.2 = ((bf16[32,128,128]{2,1,0:T(8,128)(2,1)}), bf16[32,128,128]{2,1,0:T(8,128)(2,1)S(1)}, u32[]{:S(2)}, u32[]{:S(2)}) async-start(bf16[32,128,128]{2,1,0:T(8,128)(2,1)} %bitcast.9), calls=%async_computation.2 | async-start | bytes 2097152 | tf_op jit(solution)/shard_map/all_to_all | solution.py:435
  71.7 11.6 %shard_map.112.res_hbm = bf16[8,512,128]{2,1,0:T(8,128)(2,1)} custom-call(bf16[4,8,128,128]{3,2,1,0:T(8,128)(2,1)} %bitcast.20, bf16[8,128,128]{2,1,0:T(8,128)(2,1)} %shard_map.110.o0, bf16[8,128,128]{2,1,0:T(8,128)(2,1)} %copy-done.4, bf16[8,128,128]{2,1,0:T(8,128)(2,1)} %copy-done.3, bf16[8,128,128]{2,1,0:T(8,128)(2,1)} %copy-done.5, ...), custom_call_target="tpu_custom_call" | custom-call | tf_op jit(solution)/shard_map/pallas_call | solution.py:284
  83.3 5.3 %all-to-all-done.2 = bf16[32,128,128]{2,1,0:T(8,128)(2,1)S(1)} async-done(((bf16[32,128,128]{2,1,0:T(8,128)(2,1)}), bf16[32,128,128]{2,1,0:T(8,128)(2,1)S(1)}, u32[]{:S(2)}, u32[]{:S(2)}) %all-to-all-start.2) | async-done | bytes 1048608 | tf_op jit(solution)/shard_map/all_to_all | solution.py:435
  88.6 3.2 %shard_map.114 = bf16[4,8,8,16,128]{4,3,2,1,0:T(8,128)(2,1)} custom-call(bf16[8,512,128]{2,1,0:T(8,128)(2,1)} %shard_map.112.res_hbm, bf16[4,8,128,128]{3,2,1,0:T(8,128)(2,1)S(1)} %bitcast.17), custom_call_target="tpu_custom_call" | custom-call | tf_op jit(solution)/shard_map/pallas_call | solution.py:284
  91.8 7.0 %all-to-all-start.3 = ((bf16[256,16,128]{2,1,0:T(8,128)(2,1)}), bf16[256,16,128]{2,1,0:T(8,128)(2,1)S(1)}, u32[]{:S(2)}, u32[]{:S(2)}) async-start(bf16[256,16,128]{2,1,0:T(8,128)(2,1)} %bitcast.21), calls=%async_computation.3 | async-start | bytes 2097152 | tf_op jit(solution)/shard_map/all_to_all | solution.py:435
  98.8 4.5 %shard_map.115.beta_hbm = f32[512,1024]{1,0:T(8,128)} custom-call(bf16[512,1024]{1,0:T(8,128)(2,1)} %c_hbm.2, bf16[1024,1024]{1,0:T(8,128)(2,1)} %bitcast.24), custom_call_target="tpu_custom_call" | custom-call | tf_op jit(solution)/shard_map/pallas_call | solution.py:284
  103.3 27.6 %all-to-all-done.3 = bf16[256,16,128]{2,1,0:T(8,128)(2,1)S(1)} async-done(((bf16[256,16,128]{2,1,0:T(8,128)(2,1)}), bf16[256,16,128]{2,1,0:T(8,128)(2,1)S(1)}, u32[]{:S(2)}, u32[]{:S(2)}) %all-to-all-start.3) | async-done | bytes 1048608 | tf_op jit(solution)/shard_map/all_to_all | solution.py:435
  130.9 3.4 %shard_map.116 = f32[512,1024]{1,0:T(8,128)} custom-call(bf16[4,8,8,16,128]{4,3,2,1,0:T(8,128)(2,1)S(1)} %bitcast.18, f32[512,1024]{1,0:T(8,128)} %shard_map.115.beta_hbm), custom_call_target="tpu_custom_call" | custom-call | tf_op jit(solution)/shard_map/pallas_call | solution.py:284
  (51 shorter events, 2.9 us)
Async XLA Ops:
  3.0 19.0 %copy-start.8 = (s32[32,32,2]{1,2,0:T(2,128)S(1)}, s32[32,32,2]{1,2,0:T(2,128)}, u32[]{:S(2)}) copy-start(s32[32,32,2]{1,2,0:T(2,128)} %param.15) | copy-start | bytes 24580
  3.0 19.1 %copy-start.9 = (s32[128,16]{0,1:T(8,128)S(1)}, s32[128,16]{0,1:T(8,128)}, u32[]{:S(2)}) copy-start(s32[128,16]{0,1:T(8,128)} %param.16) | copy-start | bytes 24580
  3.0 19.2 %copy-start.11 = (s32[128,16]{0,1:T(8,128)S(1)}, s32[128,16]{0,1:T(8,128)}, u32[]{:S(2)}) copy-start(s32[128,16]{0,1:T(8,128)} %param.18) | copy-start | bytes 24580
  3.0 19.3 %copy-start.10 = (s32[128,16]{0,1:T(8,128)S(1)}, s32[128,16]{0,1:T(8,128)}, u32[]{:S(2)}) copy-start(s32[128,16]{0,1:T(8,128)} %param.17) | copy-start | bytes 24580
  3.0 19.4 %copy-start.12 = (s32[128,8]{0,1:T(8,128)S(1)}, s32[128,8]{0,1:T(8,128)}, u32[]{:S(2)}) copy-start(s32[128,8]{0,1:T(8,128)} %param.21) | copy-start | bytes 12292
  3.0 19.4 %copy-start.13 = (s32[128,8]{0,1:T(8,128)S(1)}, s32[128,8]{0,1:T(8,128)}, u32[]{:S(2)}) copy-start(s32[128,8]{0,1:T(8,128)} %param.19) | copy-start | bytes 12292
  3.1 36.9 %all-to-all-start = ((bf16[32,128,128]{2,1,0:T(8,128)(2,1)}), bf16[32,128,128]{2,1,0:T(8,128)(2,1)S(1)}, u32[]{:S(2)}, u32[]{:S(2)}) async-start(bf16[32,128,128]{2,1,0:T(8,128)(2,1)} %bitcast.22), calls=%async_computation | async-start | bytes 2097152 | tf_op jit(solution)/shard_map/all_to_all | solution.py:435
  15.1 9.4 %copy-start.14 = (s32[128,8]{0,1:T(8,128)S(1)}, s32[128,8]{0,1:T(8,128)}, u32[]{:S(2)}) copy-start(s32[128,8]{0,1:T(8,128)} %param.20) | copy-start | bytes 12292
  15.1 9.7 %copy-start.7 = (bf16[8,128,128]{2,1,0:T(8,128)(2,1)S(1)}, bf16[8,128,128]{2,1,0:T(8,128)(2,1)}, u32[]{:S(2)}) copy-start(bf16[8,128,128]{2,1,0:T(8,128)(2,1)} %param.14) | copy-start | bytes 786436
  16.8 14.4 %collective-permute-start.3 = (bf16[8,128,128]{2,1,0:T(8,128)(2,1)}, bf16[8,128,128]{2,1,0:T(8,128)(2,1)S(1)}, u32[]{:S(2)}, u32[]{:S(2)}) collective-permute-start(bf16[8,128,128]{2,1,0:T(8,128)(2,1)} %shard_map.110.o0), channel_id=1, source_target_pairs={{0,192},{32,224},{64,128},{96,160},{128,64},{160,96},{192,0},{224,... | collective-permute-start | bytes 786440 | tf_op jit(solution)/shard_map/ppermute | solution.py:307
  19.6 11.6 %collective-permute-start.2 = (bf16[8,128,128]{2,1,0:T(8,128)(2,1)}, bf16[8,128,128]{2,1,0:T(8,128)(2,1)S(1)}, u32[]{:S(2)}, u32[]{:S(2)}) collective-permute-start(bf16[8,128,128]{2,1,0:T(8,128)(2,1)} %shard_map.110.o0), channel_id=1, source_target_pairs={{0,128},{32,160},{64,192},{96,224},{128,0},{160,32},{192,64},{224,... | collective-permute-start | bytes 786440 | tf_op jit(solution)/shard_map/ppermute | solution.py:307
  20.0 11.6 %collective-permute-start.1 = (bf16[8,128,128]{2,1,0:T(8,128)(2,1)}, bf16[8,128,128]{2,1,0:T(8,128)(2,1)S(1)}, u32[]{:S(2)}, u32[]{:S(2)}) collective-permute-start(bf16[8,128,128]{2,1,0:T(8,128)(2,1)} %shard_map.110.o0), channel_id=1, source_target_pairs={{0,64},{32,96},{64,0},{96,32},{128,192},{160,224},{192,128},{224,1... | collective-permute-start | bytes 786440 | tf_op jit(solution)/shard_map/ppermute | solution.py:307
  20.3 13.6 %collective-permute-start = (bf16[8,128,128]{2,1,0:T(8,128)(2,1)}, bf16[8,128,128]{2,1,0:T(8,128)(2,1)S(1)}, u32[]{:S(2)}, u32[]{:S(2)}) collective-permute-start(bf16[8,128,128]{2,1,0:T(8,128)(2,1)} %shard_map.110.o0), channel_id=1, source_target_pairs={{0,32},{32,0},{64,96},{96,64},{128,160},{160,128},{192,224},{224,1... | collective-permute-start | bytes 786440 | tf_op jit(solution)/shard_map/ppermute | solution.py:307
  31.2 10.0 %copy-start.1 = (bf16[8,128,128]{2,1,0:T(8,128)(2,1)}, bf16[8,128,128]{2,1,0:T(8,128)(2,1)S(1)}, u32[]{:S(2)}) copy-start(bf16[8,128,128]{2,1,0:T(8,128)(2,1)S(1)} %collective-permute-done.3.o6) | copy-start | bytes 786436
  31.2 10.0 %copy-start.2 = (bf16[8,128,128]{2,1,0:T(8,128)(2,1)}, bf16[8,128,128]{2,1,0:T(8,128)(2,1)S(1)}, u32[]{:S(2)}) copy-start(bf16[8,128,128]{2,1,0:T(8,128)(2,1)S(1)} %collective-permute-done.2.o4) | copy-start | bytes 786436
  31.6 9.6 %copy-start.3 = (bf16[8,128,128]{2,1,0:T(8,128)(2,1)}, bf16[8,128,128]{2,1,0:T(8,128)(2,1)S(1)}, u32[]{:S(2)}) copy-start(bf16[8,128,128]{2,1,0:T(8,128)(2,1)S(1)} %collective-permute-done.1.o2) | copy-start | bytes 786436
  31.6 3.0 %collective-permute-start.4 = (bf16[8,128,128]{2,1,0:T(8,128)(2,1)S(1)}, bf16[8,128,128]{2,1,0:T(8,128)(2,1)S(1)}, u32[]{:S(2)}, u32[]{:S(2)}) collective-permute-start(bf16[8,128,128]{2,1,0:T(8,128)(2,1)S(1)} %collective-permute-done.1.o2), channel_id=1, source_target_pairs={{0,32},{32,0},{64,96},{96,64},{128,160},{160,128},{192,224},{224,1... | collective-permute-start | bytes 786440 | tf_op jit(solution)/shard_map/ppermute | solution.py:307
  33.4 1.5 %collective-permute-start.5 = (bf16[8,128,128]{2,1,0:T(8,128)(2,1)S(1)}, bf16[8,128,128]{2,1,0:T(8,128)(2,1)S(1)}, u32[]{:S(2)}, u32[]{:S(2)}) collective-permute-start(bf16[8,128,128]{2,1,0:T(8,128)(2,1)S(1)} %collective-permute-done.2.o4), channel_id=1, source_target_pairs={{0,32},{32,0},{64,96},{96,64},{128,160},{160,128},{192,224},{224,1... | collective-permute-start | bytes 786440 | tf_op jit(solution)/shard_map/ppermute | solution.py:307
  33.4 2.0 %collective-permute-start.6 = (bf16[8,128,128]{2,1,0:T(8,128)(2,1)S(1)}, bf16[8,128,128]{2,1,0:T(8,128)(2,1)}, u32[]{:S(2)}, u32[]{:S(2)}) collective-permute-start(bf16[8,128,128]{2,1,0:T(8,128)(2,1)S(1)} %collective-permute-done.3.o6), channel_id=1, source_target_pairs={{0,32},{32,0},{64,96},{96,64},{128,160},{160,128},{192,224},{224,1... | collective-permute-start | bytes 786440 | tf_op jit(solution)/shard_map/ppermute | solution.py:307
  34.0 7.2 %copy-start.4 = (bf16[8,128,128]{2,1,0:T(8,128)(2,1)}, bf16[8,128,128]{2,1,0:T(8,128)(2,1)S(1)}, u32[]{:S(2)}) copy-start(bf16[8,128,128]{2,1,0:T(8,128)(2,1)S(1)} %collective-permute-done.o1) | copy-start | bytes 786436
  34.6 6.6 %copy-start.5 = (bf16[8,128,128]{2,1,0:T(8,128)(2,1)}, bf16[8,128,128]{2,1,0:T(8,128)(2,1)S(1)}, u32[]{:S(2)}) copy-start(bf16[8,128,128]{2,1,0:T(8,128)(2,1)S(1)} %collective-permute-done.4.o3) | copy-start | bytes 786436
  41.2 26.5 %all-to-all-start.1 = ((bf16[32,128,128]{2,1,0:T(8,128)(2,1)}), bf16[32,128,128]{2,1,0:T(8,128)(2,1)S(1)}, u32[]{:S(2)}, u32[]{:S(2)}) async-start(bf16[32,128,128]{2,1,0:T(8,128)(2,1)} %bitcast.23), calls=%async_computation.1 | async-start | bytes 2097152 | tf_op jit(solution)/shard_map/all_to_all | solution.py:435
  67.7 20.8 %all-to-all-start.2 = ((bf16[32,128,128]{2,1,0:T(8,128)(2,1)}), bf16[32,128,128]{2,1,0:T(8,128)(2,1)S(1)}, u32[]{:S(2)}, u32[]{:S(2)}) async-start(bf16[32,128,128]{2,1,0:T(8,128)(2,1)} %bitcast.9), calls=%async_computation.2 | async-start | bytes 2097152 | tf_op jit(solution)/shard_map/all_to_all | solution.py:435
  91.8 39.2 %all-to-all-start.3 = ((bf16[256,16,128]{2,1,0:T(8,128)(2,1)}), bf16[256,16,128]{2,1,0:T(8,128)(2,1)S(1)}, u32[]{:S(2)}, u32[]{:S(2)}) async-start(bf16[256,16,128]{2,1,0:T(8,128)(2,1)} %bitcast.21), calls=%async_computation.3 | async-start | bytes 2097152 | tf_op jit(solution)/shard_map/all_to_all | solution.py:435
  (2 other events, 10.2 us)

commit v7 on v6

--- a/solution.py
+++ b/solution.py
@@ -41,8 +41,8 @@
     for p in range(ABLK):
         loads[p].wait()
         for t in range(TILES):
-            block = c_ref[p * TILE : (p + 1) * TILE, t * TILE : (t + 1) * TILE].astype(F32)
-            t_ref[p * TILE : (p + 1) * TILE, t * TILE : (t + 1) * TILE] = block.T.astype(BF)
+            block = c_ref[p * TILE : (p + 1) * TILE, t * TILE : (t + 1) * TILE]
+            t_ref[p * TILE : (p + 1) * TILE, t * TILE : (t + 1) * TILE] = block.T
     stores = []
     for k in range(4):
         both = t_ref[:, k * 2 * TILE : (k + 1) * 2 * TILE]
@@ -196,14 +196,14 @@
     order = deinterleave(512, 512)
     stores = []
     for half in range(SECTORS // 2):
-        moved = landed(land_ref, 2 * half, order)
+        moved = landed(land_ref, 2 * half, order).astype(BF)
         loads[half].wait()
         for o in range(2):
             d = 2 * half + o
             blocks = []
             for a in range(ABLK):
                 rows = slice(a * TILE, (a + 1) * TILE)
-                blocks.append(res_ref[d, rows].astype(F32) + moved[rows, o * TILE : (o + 1) * TILE].T)
+                blocks.append(res_ref[d, rows].astype(F32) + moved[rows, o * TILE : (o + 1) * TILE].T.astype(F32))
             sides = []
             for h in range(2):
                 first = blocks[2 * h].reshape(16, 8, TILE)
@@ -233,7 +233,9 @@
         copy.wait()
     for k in range(4):
         cols = slice(k * 2 * TILE, (k + 1) * 2 * TILE)
-        out_ref[:, cols] = jnp.dot(c_ref[...], op_ref[:, cols], preferred_element_type=F32)
+        out_ref[:, cols] = jnp.dot(
+            c_ref[...], op_ref[:, cols], preferred_element_type=F32
+        ).astype(BF)
     store = pltpu.make_async_copy(out_ref, out_hbm, out_sem)
     store.start()
     store.wait()
@@ -256,7 +258,7 @@
         moved = jnp.dot(order, both, preferred_element_type=F32)
         loads[k].wait()
         cols = pl.ds(k * 2 * TILE, 2 * TILE)
-        out_ref[:, cols] = beta_ref[:, cols] + moved
+        out_ref[:, cols] = beta_ref[:, cols].astype(F32) + moved
         stores.append(
             pltpu.make_async_copy(out_ref.at[:, cols], out_hbm.at[:, cols], out_sem.at[k])
         )
@@ -404,14 +406,14 @@
     home = exchange(back.reshape(256, 16, TILE), ("x", "sym", "z"))
     beta_part = call(
         beta_kernel,
-        jax.ShapeDtypeStruct(coeffs.shape, F32),
+        jax.ShapeDtypeStruct(coeffs.shape, BF),
         12,
         [HBM, HBM],
         HBM,
         [
             pltpu.VMEM(coeffs.shape, BF),
             pltpu.VMEM(beta_late.shape, BF),
-            pltpu.VMEM(coeffs.shape, F32),
+            pltpu.VMEM(coeffs.shape, BF),
             sems(2),
             pltpu.SemaphoreType.DMA,
         ],
@@ -422,7 +424,7 @@
         12,
         [VMEM, HBM],
         HBM,
-        [pltpu.VMEM(coeffs.shape, F32), pltpu.VMEM(coeffs.shape, F32), sems(4), sems(4)],
+        [pltpu.VMEM(coeffs.shape, BF), pltpu.VMEM(coeffs.shape, F32), sems(4), sems(4)],
     )(home.reshape(out), beta_part)
 
 

time: 135 us -> 135 us (level)
  no operation moved by 1% of the time
where the time goes in v7:
time: 135 us; the launch traced here: 134 us
  waiting for transfers between devices  52.7 us (39%)
  starting transfers between devices  40 us (30%)
  Pallas kernels  36.8 us (27%)
  other arithmetic  3.47 us (3%)
    all_to_all x4, waiting for transfers between devices, exchange(): return lax.all_to_all(array, axes, split_axis=0, concat_axis=0, tiled=True)  45.9 us
    pallas_call x8, Pallas kernels, placed(): run(*(pltpu.with_memory_space_constraint(x, HBM) if place is HBM else x f...  36.8 us
    all_to_all x4, starting transfers between devices, exchange(): return lax.all_to_all(array, axes, split_axis=0, concat_axis=0, tiled=True)  32.5 us
    ppermute x7, starting transfers between devices, swapped(): return lax.ppermute(array, 'sym', [(s, s ^ mask) for s in range(SECTORS)])  7.54 us
    ppermute x7, waiting for transfers between devices, swapped(): return lax.ppermute(array, 'sym', [(s, s ^ mask) for s in range(SECTORS)])  6.79 us
    reduce_sum x2, other arithmetic, signed_weights(): return jnp.sum(jnp.where(hit, factor[:, :, None], 0.0), axis=1).astype(BF)  3.33 us
  transfers between devices with their start and end apart: 11, of which 9 were waited for; matrix products, arithmetic and copies ran while one was open for 3% of the time, Pallas kernels for 20%

profile of v7, /device:TPU:1, one launch (start us, length us, event | category | flops | bytes accessed | tf_op | source)
XLA Modules:
  0.0 134.3 jit_solution(11830638815958501268)
XLA Ops:
  0.0 2.9 %shard_map.109 = bf16[4,8,128,128]{3,2,1,0:T(8,128)(2,1)} custom-call(bf16[512,1024]{1,0:T(8,128)(2,1)} %c_hbm.2), custom_call_target="tpu_custom_call" | custom-call | tf_op jit(solution)/shard_map/pallas_call | solution.py:286
  3.0 12.0 %all-to-all-start = ((bf16[32,128,128]{2,1,0:T(8,128)(2,1)}), bf16[32,128,128]{2,1,0:T(8,128)(2,1)S(1)}, u32[]{:S(2)}, u32[]{:S(2)}) async-start(bf16[32,128,128]{2,1,0:T(8,128)(2,1)} %bitcast.22), calls=%async_computation | async-start | bytes 2097152 | tf_op jit(solution)/shard_map/all_to_all | solution.py:437
  15.0 1.7 %shard_map.110.o0 = bf16[8,128,128]{2,1,0:T(8,128)(2,1)} custom-call(bf16[1,8,8,128,128]{4,3,2,1,0:T(8,128)(2,1)} %op_hbm), custom_call_target="tpu_custom_call" | custom-call | tf_op jit(solution)/shard_map/pallas_call | solution.py:286
  16.8 2.8 %collective-permute-start.3 = (bf16[8,128,128]{2,1,0:T(8,128)(2,1)}, bf16[8,128,128]{2,1,0:T(8,128)(2,1)S(1)}, u32[]{:S(2)}, u32[]{:S(2)}) collective-permute-start(bf16[8,128,128]{2,1,0:T(8,128)(2,1)} %shard_map.110.o0), channel_id=1, source_target_pairs={{0,192},{32,224},{64,128},{96,160},{128,64},{160,96},{192,0},{224,... | collective-permute-start | bytes 786440 | tf_op jit(solution)/shard_map/ppermute | solution.py:309
  20.3 1.6 %collective-permute-start = (bf16[8,128,128]{2,1,0:T(8,128)(2,1)}, bf16[8,128,128]{2,1,0:T(8,128)(2,1)S(1)}, u32[]{:S(2)}, u32[]{:S(2)}) collective-permute-start(bf16[8,128,128]{2,1,0:T(8,128)(2,1)} %shard_map.110.o0), channel_id=1, source_target_pairs={{0,32},{32,0},{64,96},{96,64},{128,160},{160,128},{192,224},{224,1... | collective-permute-start | bytes 786440 | tf_op jit(solution)/shard_map/ppermute | solution.py:309
  22.5 2.0 %select_reduce_fusion.w_ref = bf16[128,1024]{1,0:T(8,128)(2,1)S(1)} fusion(f32[128,16]{1,0:T(8,128)S(1)} %copy.27, s32[128,16]{1,0:T(8,128)S(1)} %copy.26), kind=kLoop, calls=%fused_computation | loop fusion | flops 6160384 | bytes 278528 | tf_op jit(solution)/shard_map/reduce_sum | solution.py:305
  24.9 1.3 %select_reduce_fusion.1.w_ref = bf16[128,1024]{1,0:T(8,128)(2,1)S(1)} fusion(f32[128,8]{1,0:T(8,128)S(1)} %copy.29, s32[128,8]{1,0:T(8,128)S(1)} %copy.28), kind=kLoop, calls=%fused_computation.2 | loop fusion | flops 3014656 | bytes 270336 | tf_op jit(solution)/shard_map/reduce_sum | solution.py:305
  26.2 4.9 %collective-permute-done.3.o6 = bf16[8,128,128]{2,1,0:T(8,128)(2,1)S(1)} collective-permute-done((bf16[8,128,128]{2,1,0:T(8,128)(2,1)}, bf16[8,128,128]{2,1,0:T(8,128)(2,1)S(1)}, u32[]{:S(2)}, u32[]{:S(2)}) %collective-permute-start.3) | collective-permute-done | bytes 262176 | tf_op jit(solution)/shard_map/ppermute | solution.py:309
  31.5 1.9 %collective-permute-start.4 = (bf16[8,128,128]{2,1,0:T(8,128)(2,1)S(1)}, bf16[8,128,128]{2,1,0:T(8,128)(2,1)S(1)}, u32[]{:S(2)}, u32[]{:S(2)}) collective-permute-start(bf16[8,128,128]{2,1,0:T(8,128)(2,1)S(1)} %collective-permute-done.1.o2), channel_id=1, source_target_pairs={{0,32},{32,0},{64,96},{96,64},{128,160},{160,128},{192,224},{224,1... | collective-permute-start | bytes 786440 | tf_op jit(solution)/shard_map/ppermute | solution.py:309
  33.4 0.5 collective-permute-start.6
  33.9 0.6 collective-permute-done.4.o3
  35.4 4.5 %all-to-all-done = bf16[32,128,128]{2,1,0:T(8,128)(2,1)S(1)} async-done(((bf16[32,128,128]{2,1,0:T(8,128)(2,1)}), bf16[32,128,128]{2,1,0:T(8,128)(2,1)S(1)}, u32[]{:S(2)}, u32[]{:S(2)}) %all-to-all-start) | async-done | bytes 1048608 | tf_op jit(solution)/shard_map/all_to_all | solution.py:437
  39.9 1.2 shard_map.111
  41.2 9.6 %all-to-all-start.1 = ((bf16[32,128,128]{2,1,0:T(8,128)(2,1)}), bf16[32,128,128]{2,1,0:T(8,128)(2,1)S(1)}, u32[]{:S(2)}, u32[]{:S(2)}) async-start(bf16[32,128,128]{2,1,0:T(8,128)(2,1)} %bitcast.23), calls=%async_computation.1 | async-start | bytes 2097152 | tf_op jit(solution)/shard_map/all_to_all | solution.py:437
  50.8 8.7 %shard_map.113 = bf16[16,2,8,16,128]{4,3,2,1,0:T(8,128)(2,1)} custom-call(bf16[32,8,16,128]{3,2,1,0:T(8,128)(2,1)S(1)} %bitcast.16, bf16[1024,128]{1,0:T(8,128)(2,1)S(1)} %bitcast.19, bf16[128,1024]{1,0:T(8,128)(2,1)S(1)} %select_reduce_fusion.1.w_ref), custom_call_target="tpu_custom_call" | custom-call | tf_op jit(solution)/shard_map/pallas_call | solution.py:286
  59.5 8.2 %all-to-all-done.1 = bf16[32,128,128]{2,1,0:T(8,128)(2,1)S(1)} async-done(((bf16[32,128,128]{2,1,0:T(8,128)(2,1)}), bf16[32,128,128]{2,1,0:T(8,128)(2,1)S(1)}, u32[]{:S(2)}, u32[]{:S(2)}) %all-to-all-start.1) | async-done | bytes 1048608 | tf_op jit(solution)/shard_map/all_to_all | solution.py:437
  67.7 3.9 %all-to-all-start.2 = ((bf16[32,128,128]{2,1,0:T(8,128)(2,1)}), bf16[32,128,128]{2,1,0:T(8,128)(2,1)S(1)}, u32[]{:S(2)}, u32[]{:S(2)}) async-start(bf16[32,128,128]{2,1,0:T(8,128)(2,1)} %bitcast.9), calls=%async_computation.2 | async-start | bytes 2097152 | tf_op jit(solution)/shard_map/all_to_all | solution.py:437
  71.6 11.6 %shard_map.112.res_hbm = bf16[8,512,128]{2,1,0:T(8,128)(2,1)} custom-call(bf16[4,8,128,128]{3,2,1,0:T(8,128)(2,1)} %bitcast.20, bf16[8,128,128]{2,1,0:T(8,128)(2,1)} %shard_map.110.o0, bf16[8,128,128]{2,1,0:T(8,128)(2,1)} %copy-done.4, bf16[8,128,128]{2,1,0:T(8,128)(2,1)} %copy-done.3, bf16[8,128,128]{2,1,0:T(8,128)(2,1)} %copy-done.5, ...), custom_call_target="tpu_custom_call" | custom-call | tf_op jit(solution)/shard_map/pallas_call | solution.py:286
  83.3 5.3 %all-to-all-done.2 = bf16[32,128,128]{2,1,0:T(8,128)(2,1)S(1)} async-done(((bf16[32,128,128]{2,1,0:T(8,128)(2,1)}), bf16[32,128,128]{2,1,0:T(8,128)(2,1)S(1)}, u32[]{:S(2)}, u32[]{:S(2)}) %all-to-all-start.2) | async-done | bytes 1048608 | tf_op jit(solution)/shard_map/all_to_all | solution.py:437
  88.5 3.1 %shard_map.114 = bf16[4,8,8,16,128]{4,3,2,1,0:T(8,128)(2,1)} custom-call(bf16[8,512,128]{2,1,0:T(8,128)(2,1)} %shard_map.112.res_hbm, bf16[4,8,128,128]{3,2,1,0:T(8,128)(2,1)S(1)} %bitcast.17), custom_call_target="tpu_custom_call" | custom-call | tf_op jit(solution)/shard_map/pallas_call | solution.py:286
  91.7 7.0 %all-to-all-start.3 = ((bf16[256,16,128]{2,1,0:T(8,128)(2,1)}), bf16[256,16,128]{2,1,0:T(8,128)(2,1)S(1)}, u32[]{:S(2)}, u32[]{:S(2)}) async-start(bf16[256,16,128]{2,1,0:T(8,128)(2,1)} %bitcast.21), calls=%async_computation.3 | async-start | bytes 2097152 | tf_op jit(solution)/shard_map/all_to_all | solution.py:437
  98.7 4.2 %shard_map.115.beta_hbm = bf16[512,1024]{1,0:T(8,128)(2,1)} custom-call(bf16[512,1024]{1,0:T(8,128)(2,1)} %c_hbm.2, bf16[1024,1024]{1,0:T(8,128)(2,1)} %bitcast.24), custom_call_target="tpu_custom_call" | custom-call | tf_op jit(solution)/shard_map/pallas_call | solution.py:286
  102.9 28.0 %all-to-all-done.3 = bf16[256,16,128]{2,1,0:T(8,128)(2,1)S(1)} async-done(((bf16[256,16,128]{2,1,0:T(8,128)(2,1)}), bf16[256,16,128]{2,1,0:T(8,128)(2,1)S(1)}, u32[]{:S(2)}, u32[]{:S(2)}) %all-to-all-start.3) | async-done | bytes 1048608 | tf_op jit(solution)/shard_map/all_to_all | solution.py:437
  130.8 3.3 %shard_map.116 = f32[512,1024]{1,0:T(8,128)} custom-call(bf16[4,8,8,16,128]{4,3,2,1,0:T(8,128)(2,1)S(1)} %bitcast.18, bf16[512,1024]{1,0:T(8,128)(2,1)} %shard_map.115.beta_hbm), custom_call_target="tpu_custom_call" | custom-call | tf_op jit(solution)/shard_map/pallas_call | solution.py:286
  (51 shorter events, 2.9 us)
Async XLA Ops:
  2.9 19.0 %copy-start.8 = (s32[32,32,2]{1,2,0:T(2,128)S(1)}, s32[32,32,2]{1,2,0:T(2,128)}, u32[]{:S(2)}) copy-start(s32[32,32,2]{1,2,0:T(2,128)} %param.15) | copy-start | bytes 24580
  3.0 19.1 %copy-start.9 = (s32[128,16]{0,1:T(8,128)S(1)}, s32[128,16]{0,1:T(8,128)}, u32[]{:S(2)}) copy-start(s32[128,16]{0,1:T(8,128)} %param.16) | copy-start | bytes 24580
  3.0 19.2 %copy-start.11 = (s32[128,16]{0,1:T(8,128)S(1)}, s32[128,16]{0,1:T(8,128)}, u32[]{:S(2)}) copy-start(s32[128,16]{0,1:T(8,128)} %param.18) | copy-start | bytes 24580
  3.0 19.3 %copy-start.10 = (s32[128,16]{0,1:T(8,128)S(1)}, s32[128,16]{0,1:T(8,128)}, u32[]{:S(2)}) copy-start(s32[128,16]{0,1:T(8,128)} %param.17) | copy-start | bytes 24580
  3.0 19.4 %copy-start.12 = (s32[128,8]{0,1:T(8,128)S(1)}, s32[128,8]{0,1:T(8,128)}, u32[]{:S(2)}) copy-start(s32[128,8]{0,1:T(8,128)} %param.21) | copy-start | bytes 12292
  3.0 19.4 %copy-start.13 = (s32[128,8]{0,1:T(8,128)S(1)}, s32[128,8]{0,1:T(8,128)}, u32[]{:S(2)}) copy-start(s32[128,8]{0,1:T(8,128)} %param.19) | copy-start | bytes 12292
  3.0 36.9 %all-to-all-start = ((bf16[32,128,128]{2,1,0:T(8,128)(2,1)}), bf16[32,128,128]{2,1,0:T(8,128)(2,1)S(1)}, u32[]{:S(2)}, u32[]{:S(2)}) async-start(bf16[32,128,128]{2,1,0:T(8,128)(2,1)} %bitcast.22), calls=%async_computation | async-start | bytes 2097152 | tf_op jit(solution)/shard_map/all_to_all | solution.py:437
  15.0 9.4 %copy-start.14 = (s32[128,8]{0,1:T(8,128)S(1)}, s32[128,8]{0,1:T(8,128)}, u32[]{:S(2)}) copy-start(s32[128,8]{0,1:T(8,128)} %param.20) | copy-start | bytes 12292
  15.0 9.7 %copy-start.7 = (bf16[8,128,128]{2,1,0:T(8,128)(2,1)S(1)}, bf16[8,128,128]{2,1,0:T(8,128)(2,1)}, u32[]{:S(2)}) copy-start(bf16[8,128,128]{2,1,0:T(8,128)(2,1)} %param.14) | copy-start | bytes 786436
  16.8 14.4 %collective-permute-start.3 = (bf16[8,128,128]{2,1,0:T(8,128)(2,1)}, bf16[8,128,128]{2,1,0:T(8,128)(2,1)S(1)}, u32[]{:S(2)}, u32[]{:S(2)}) collective-permute-start(bf16[8,128,128]{2,1,0:T(8,128)(2,1)} %shard_map.110.o0), channel_id=1, source_target_pairs={{0,192},{32,224},{64,128},{96,160},{128,64},{160,96},{192,0},{224,... | collective-permute-start | bytes 786440 | tf_op jit(solution)/shard_map/ppermute | solution.py:309
  19.6 11.6 %collective-permute-start.2 = (bf16[8,128,128]{2,1,0:T(8,128)(2,1)}, bf16[8,128,128]{2,1,0:T(8,128)(2,1)S(1)}, u32[]{:S(2)}, u32[]{:S(2)}) collective-permute-start(bf16[8,128,128]{2,1,0:T(8,128)(2,1)} %shard_map.110.o0), channel_id=1, source_target_pairs={{0,128},{32,160},{64,192},{96,224},{128,0},{160,32},{192,64},{224,... | collective-permute-start | bytes 786440 | tf_op jit(solution)/shard_map/ppermute | solution.py:309
  19.9 11.6 %collective-permute-start.1 = (bf16[8,128,128]{2,1,0:T(8,128)(2,1)}, bf16[8,128,128]{2,1,0:T(8,128)(2,1)S(1)}, u32[]{:S(2)}, u32[]{:S(2)}) collective-permute-start(bf16[8,128,128]{2,1,0:T(8,128)(2,1)} %shard_map.110.o0), channel_id=1, source_target_pairs={{0,64},{32,96},{64,0},{96,32},{128,192},{160,224},{192,128},{224,1... | collective-permute-start | bytes 786440 | tf_op jit(solution)/shard_map/ppermute | solution.py:309
  20.3 13.6 %collective-permute-start = (bf16[8,128,128]{2,1,0:T(8,128)(2,1)}, bf16[8,128,128]{2,1,0:T(8,128)(2,1)S(1)}, u32[]{:S(2)}, u32[]{:S(2)}) collective-permute-start(bf16[8,128,128]{2,1,0:T(8,128)(2,1)} %shard_map.110.o0), channel_id=1, source_target_pairs={{0,32},{32,0},{64,96},{96,64},{128,160},{160,128},{192,224},{224,1... | collective-permute-start | bytes 786440 | tf_op jit(solution)/shard_map/ppermute | solution.py:309
  31.2 10.0 %copy-start.1 = (bf16[8,128,128]{2,1,0:T(8,128)(2,1)}, bf16[8,128,128]{2,1,0:T(8,128)(2,1)S(1)}, u32[]{:S(2)}) copy-start(bf16[8,128,128]{2,1,0:T(8,128)(2,1)S(1)} %collective-permute-done.3.o6) | copy-start | bytes 786436
  31.2 10.0 %copy-start.2 = (bf16[8,128,128]{2,1,0:T(8,128)(2,1)}, bf16[8,128,128]{2,1,0:T(8,128)(2,1)S(1)}, u32[]{:S(2)}) copy-start(bf16[8,128,128]{2,1,0:T(8,128)(2,1)S(1)} %collective-permute-done.2.o4) | copy-start | bytes 786436
  31.5 9.6 %copy-start.3 = (bf16[8,128,128]{2,1,0:T(8,128)(2,1)}, bf16[8,128,128]{2,1,0:T(8,128)(2,1)S(1)}, u32[]{:S(2)}) copy-start(bf16[8,128,128]{2,1,0:T(8,128)(2,1)S(1)} %collective-permute-done.1.o2) | copy-start | bytes 786436
  31.5 3.1 %collective-permute-start.4 = (bf16[8,128,128]{2,1,0:T(8,128)(2,1)S(1)}, bf16[8,128,128]{2,1,0:T(8,128)(2,1)S(1)}, u32[]{:S(2)}, u32[]{:S(2)}) collective-permute-start(bf16[8,128,128]{2,1,0:T(8,128)(2,1)S(1)} %collective-permute-done.1.o2), channel_id=1, source_target_pairs={{0,32},{32,0},{64,96},{96,64},{128,160},{160,128},{192,224},{224,1... | collective-permute-start | bytes 786440 | tf_op jit(solution)/shard_map/ppermute | solution.py:309
  33.4 1.5 %collective-permute-start.5 = (bf16[8,128,128]{2,1,0:T(8,128)(2,1)S(1)}, bf16[8,128,128]{2,1,0:T(8,128)(2,1)S(1)}, u32[]{:S(2)}, u32[]{:S(2)}) collective-permute-start(bf16[8,128,128]{2,1,0:T(8,128)(2,1)S(1)} %collective-permute-done.2.o4), channel_id=1, source_target_pairs={{0,32},{32,0},{64,96},{96,64},{128,160},{160,128},{192,224},{224,1... | collective-permute-start | bytes 786440 | tf_op jit(solution)/shard_map/ppermute | solution.py:309
  33.4 2.0 %collective-permute-start.6 = (bf16[8,128,128]{2,1,0:T(8,128)(2,1)S(1)}, bf16[8,128,128]{2,1,0:T(8,128)(2,1)}, u32[]{:S(2)}, u32[]{:S(2)}) collective-permute-start(bf16[8,128,128]{2,1,0:T(8,128)(2,1)S(1)} %collective-permute-done.3.o6), channel_id=1, source_target_pairs={{0,32},{32,0},{64,96},{96,64},{128,160},{160,128},{192,224},{224,1... | collective-permute-start | bytes 786440 | tf_op jit(solution)/shard_map/ppermute | solution.py:309
  33.9 7.2 %copy-start.4 = (bf16[8,128,128]{2,1,0:T(8,128)(2,1)}, bf16[8,128,128]{2,1,0:T(8,128)(2,1)S(1)}, u32[]{:S(2)}) copy-start(bf16[8,128,128]{2,1,0:T(8,128)(2,1)S(1)} %collective-permute-done.o1) | copy-start | bytes 786436
  34.6 6.6 %copy-start.5 = (bf16[8,128,128]{2,1,0:T(8,128)(2,1)}, bf16[8,128,128]{2,1,0:T(8,128)(2,1)S(1)}, u32[]{:S(2)}) copy-start(bf16[8,128,128]{2,1,0:T(8,128)(2,1)S(1)} %collective-permute-done.4.o3) | copy-start | bytes 786436
  41.2 26.5 %all-to-all-start.1 = ((bf16[32,128,128]{2,1,0:T(8,128)(2,1)}), bf16[32,128,128]{2,1,0:T(8,128)(2,1)S(1)}, u32[]{:S(2)}, u32[]{:S(2)}) async-start(bf16[32,128,128]{2,1,0:T(8,128)(2,1)} %bitcast.23), calls=%async_computation.1 | async-start | bytes 2097152 | tf_op jit(solution)/shard_map/all_to_all | solution.py:437
  67.7 20.8 %all-to-all-start.2 = ((bf16[32,128,128]{2,1,0:T(8,128)(2,1)}), bf16[32,128,128]{2,1,0:T(8,128)(2,1)S(1)}, u32[]{:S(2)}, u32[]{:S(2)}) async-start(bf16[32,128,128]{2,1,0:T(8,128)(2,1)} %bitcast.9), calls=%async_computation.2 | async-start | bytes 2097152 | tf_op jit(solution)/shard_map/all_to_all | solution.py:437
  91.7 39.2 %all-to-all-start.3 = ((bf16[256,16,128]{2,1,0:T(8,128)(2,1)}), bf16[256,16,128]{2,1,0:T(8,128)(2,1)S(1)}, u32[]{:S(2)}, u32[]{:S(2)}) async-start(bf16[256,16,128]{2,1,0:T(8,128)(2,1)} %bitcast.21), calls=%async_computation.3 | async-start | bytes 2097152 | tf_op jit(solution)/shard_map/all_to_all | solution.py:437
  (2 other events, 10.2 us)

commit v8 on v7

--- a/solution.py
+++ b/solution.py
@@ -49,12 +49,12 @@
         moved = jnp.dot(order, both, preferred_element_type=F32).astype(BF)
         for o in range(2):
             part = moved[:, o * TILE : (o + 1) * TILE]
-            send_ref[:, 2 * k + o] = part.reshape(XDIM, TILE, TILE)
-        here = pl.ds(2 * k, 2)
-        stores.append(
-            pltpu.make_async_copy(send_ref.at[:, here], send_hbm.at[:, here], out_sem.at[k])
-        )
-        stores[-1].start()
+            u = 2 * k + o
+            send_ref[:, u] = part.reshape(XDIM, TILE, TILE)
+            stores.append(
+                pltpu.make_async_copy(send_ref.at[:, u], send_hbm.at[:, u], out_sem.at[u])
+            )
+            stores[-1].start()
     for copy in stores:
         copy.wait()
 
@@ -329,7 +329,7 @@
         8,
         [HBM],
         HBM,
-        [pltpu.VMEM((512, 1024), BF)] * 2 + [pltpu.VMEM(sent, BF), sems(4), sems(4)],
+        [pltpu.VMEM((512, 1024), BF)] * 2 + [pltpu.VMEM(sent, BF), sems(4), sems(8)],
     )(coeffs)
     send, picked = lax.optimization_barrier((send, mix_op))
     mine = call(

time: 135 us -> 135 us (level)
  no operation moved by 1% of the time
where the time goes in v8:
time: 135 us; the launch traced here: 134 us
  waiting for transfers between devices  52.7 us (39%)
  starting transfers between devices  40 us (30%)
  Pallas kernels  36.9 us (27%)
  other arithmetic  3.47 us (3%)
    all_to_all x4, waiting for transfers between devices, exchange(): return lax.all_to_all(array, axes, split_axis=0, concat_axis=0, tiled=True)  45.9 us
    pallas_call x8, Pallas kernels, placed(): run(*(pltpu.with_memory_space_constraint(x, HBM) if place is HBM else x f...  36.9 us
    all_to_all x4, starting transfers between devices, exchange(): return lax.all_to_all(array, axes, split_axis=0, concat_axis=0, tiled=True)  32.5 us
    ppermute x7, starting transfers between devices, swapped(): return lax.ppermute(array, 'sym', [(s, s ^ mask) for s in range(SECTORS)])  7.54 us
    ppermute x7, waiting for transfers between devices, swapped(): return lax.ppermute(array, 'sym', [(s, s ^ mask) for s in range(SECTORS)])  6.8 us
    reduce_sum x2, other arithmetic, signed_weights(): return jnp.sum(jnp.where(hit, factor[:, :, None], 0.0), axis=1).astype(BF)  3.33 us
  transfers between devices with their start and end apart: 11, of which 9 were waited for; matrix products, arithmetic and copies ran while one was open for 3% of the time, Pallas kernels for 20%

profile of v8, /device:TPU:1, one launch (start us, length us, event | category | flops | bytes accessed | tf_op | source)
XLA Modules:
  0.0 134.3 jit_solution(16488527862659638220)
XLA Ops:
  0.0 3.0 %shard_map.109 = bf16[4,8,128,128]{3,2,1,0:T(8,128)(2,1)} custom-call(bf16[512,1024]{1,0:T(8,128)(2,1)} %c_hbm.2), custom_call_target="tpu_custom_call" | custom-call | tf_op jit(solution)/shard_map/pallas_call | solution.py:286
  3.1 12.0 %all-to-all-start = ((bf16[32,128,128]{2,1,0:T(8,128)(2,1)}), bf16[32,128,128]{2,1,0:T(8,128)(2,1)S(1)}, u32[]{:S(2)}, u32[]{:S(2)}) async-start(bf16[32,128,128]{2,1,0:T(8,128)(2,1)} %bitcast.22), calls=%async_computation | async-start | bytes 2097152 | tf_op jit(solution)/shard_map/all_to_all | solution.py:437
  15.1 1.7 %shard_map.110.o0 = bf16[8,128,128]{2,1,0:T(8,128)(2,1)} custom-call(bf16[1,8,8,128,128]{4,3,2,1,0:T(8,128)(2,1)} %op_hbm), custom_call_target="tpu_custom_call" | custom-call | tf_op jit(solution)/shard_map/pallas_call | solution.py:286
  16.8 2.8 %collective-permute-start.3 = (bf16[8,128,128]{2,1,0:T(8,128)(2,1)}, bf16[8,128,128]{2,1,0:T(8,128)(2,1)S(1)}, u32[]{:S(2)}, u32[]{:S(2)}) collective-permute-start(bf16[8,128,128]{2,1,0:T(8,128)(2,1)} %shard_map.110.o0), channel_id=1, source_target_pairs={{0,192},{32,224},{64,128},{96,160},{128,64},{160,96},{192,0},{224,... | collective-permute-start | bytes 786440 | tf_op jit(solution)/shard_map/ppermute | solution.py:309
  20.3 1.6 %collective-permute-start = (bf16[8,128,128]{2,1,0:T(8,128)(2,1)}, bf16[8,128,128]{2,1,0:T(8,128)(2,1)S(1)}, u32[]{:S(2)}, u32[]{:S(2)}) collective-permute-start(bf16[8,128,128]{2,1,0:T(8,128)(2,1)} %shard_map.110.o0), channel_id=1, source_target_pairs={{0,32},{32,0},{64,96},{96,64},{128,160},{160,128},{192,224},{224,1... | collective-permute-start | bytes 786440 | tf_op jit(solution)/shard_map/ppermute | solution.py:309
  22.5 2.0 %select_reduce_fusion.w_ref = bf16[128,1024]{1,0:T(8,128)(2,1)S(1)} fusion(f32[128,16]{1,0:T(8,128)S(1)} %copy.27, s32[128,16]{1,0:T(8,128)S(1)} %copy.26), kind=kLoop, calls=%fused_computation | loop fusion | flops 6160384 | bytes 278528 | tf_op jit(solution)/shard_map/reduce_sum | solution.py:305
  24.9 1.3 %select_reduce_fusion.1.w_ref = bf16[128,1024]{1,0:T(8,128)(2,1)S(1)} fusion(f32[128,8]{1,0:T(8,128)S(1)} %copy.29, s32[128,8]{1,0:T(8,128)S(1)} %copy.28), kind=kLoop, calls=%fused_computation.2 | loop fusion | flops 3014656 | bytes 270336 | tf_op jit(solution)/shard_map/reduce_sum | solution.py:305
  26.3 4.9 %collective-permute-done.3.o6 = bf16[8,128,128]{2,1,0:T(8,128)(2,1)S(1)} collective-permute-done((bf16[8,128,128]{2,1,0:T(8,128)(2,1)}, bf16[8,128,128]{2,1,0:T(8,128)(2,1)S(1)}, u32[]{:S(2)}, u32[]{:S(2)}) %collective-permute-start.3) | collective-permute-done | bytes 262176 | tf_op jit(solution)/shard_map/ppermute | solution.py:309
  31.6 1.9 %collective-permute-start.4 = (bf16[8,128,128]{2,1,0:T(8,128)(2,1)S(1)}, bf16[8,128,128]{2,1,0:T(8,128)(2,1)S(1)}, u32[]{:S(2)}, u32[]{:S(2)}) collective-permute-start(bf16[8,128,128]{2,1,0:T(8,128)(2,1)S(1)} %collective-permute-done.1.o2), channel_id=1, source_target_pairs={{0,32},{32,0},{64,96},{96,64},{128,160},{160,128},{192,224},{224,1... | collective-permute-start | bytes 786440 | tf_op jit(solution)/shard_map/ppermute | solution.py:309
  33.4 0.5 collective-permute-start.6
  34.0 0.6 collective-permute-done.4.o3
  35.5 4.5 %all-to-all-done = bf16[32,128,128]{2,1,0:T(8,128)(2,1)S(1)} async-done(((bf16[32,128,128]{2,1,0:T(8,128)(2,1)}), bf16[32,128,128]{2,1,0:T(8,128)(2,1)S(1)}, u32[]{:S(2)}, u32[]{:S(2)}) %all-to-all-start) | async-done | bytes 1048608 | tf_op jit(solution)/shard_map/all_to_all | solution.py:437
  39.9 1.2 shard_map.111
  41.2 9.6 %all-to-all-start.1 = ((bf16[32,128,128]{2,1,0:T(8,128)(2,1)}), bf16[32,128,128]{2,1,0:T(8,128)(2,1)S(1)}, u32[]{:S(2)}, u32[]{:S(2)}) async-start(bf16[32,128,128]{2,1,0:T(8,128)(2,1)} %bitcast.23), calls=%async_computation.1 | async-start | bytes 2097152 | tf_op jit(solution)/shard_map/all_to_all | solution.py:437
  50.8 8.7 %shard_map.113 = bf16[16,2,8,16,128]{4,3,2,1,0:T(8,128)(2,1)} custom-call(bf16[32,8,16,128]{3,2,1,0:T(8,128)(2,1)S(1)} %bitcast.16, bf16[1024,128]{1,0:T(8,128)(2,1)S(1)} %bitcast.19, bf16[128,1024]{1,0:T(8,128)(2,1)S(1)} %select_reduce_fusion.1.w_ref), custom_call_target="tpu_custom_call" | custom-call | tf_op jit(solution)/shard_map/pallas_call | solution.py:286
  59.5 8.2 %all-to-all-done.1 = bf16[32,128,128]{2,1,0:T(8,128)(2,1)S(1)} async-done(((bf16[32,128,128]{2,1,0:T(8,128)(2,1)}), bf16[32,128,128]{2,1,0:T(8,128)(2,1)S(1)}, u32[]{:S(2)}, u32[]{:S(2)}) %all-to-all-start.1) | async-done | bytes 1048608 | tf_op jit(solution)/shard_map/all_to_all | solution.py:437
  67.7 3.9 %all-to-all-start.2 = ((bf16[32,128,128]{2,1,0:T(8,128)(2,1)}), bf16[32,128,128]{2,1,0:T(8,128)(2,1)S(1)}, u32[]{:S(2)}, u32[]{:S(2)}) async-start(bf16[32,128,128]{2,1,0:T(8,128)(2,1)} %bitcast.9), calls=%async_computation.2 | async-start | bytes 2097152 | tf_op jit(solution)/shard_map/all_to_all | solution.py:437
  71.7 11.6 %shard_map.112.res_hbm = bf16[8,512,128]{2,1,0:T(8,128)(2,1)} custom-call(bf16[4,8,128,128]{3,2,1,0:T(8,128)(2,1)} %bitcast.20, bf16[8,128,128]{2,1,0:T(8,128)(2,1)} %shard_map.110.o0, bf16[8,128,128]{2,1,0:T(8,128)(2,1)} %copy-done.4, bf16[8,128,128]{2,1,0:T(8,128)(2,1)} %copy-done.3, bf16[8,128,128]{2,1,0:T(8,128)(2,1)} %copy-done.5, ...), custom_call_target="tpu_custom_call" | custom-call | tf_op jit(solution)/shard_map/pallas_call | solution.py:286
  83.3 5.3 %all-to-all-done.2 = bf16[32,128,128]{2,1,0:T(8,128)(2,1)S(1)} async-done(((bf16[32,128,128]{2,1,0:T(8,128)(2,1)}), bf16[32,128,128]{2,1,0:T(8,128)(2,1)S(1)}, u32[]{:S(2)}, u32[]{:S(2)}) %all-to-all-start.2) | async-done | bytes 1048608 | tf_op jit(solution)/shard_map/all_to_all | solution.py:437
  88.6 3.1 %shard_map.114 = bf16[4,8,8,16,128]{4,3,2,1,0:T(8,128)(2,1)} custom-call(bf16[8,512,128]{2,1,0:T(8,128)(2,1)} %shard_map.112.res_hbm, bf16[4,8,128,128]{3,2,1,0:T(8,128)(2,1)S(1)} %bitcast.17), custom_call_target="tpu_custom_call" | custom-call | tf_op jit(solution)/shard_map/pallas_call | solution.py:286
  91.7 7.0 %all-to-all-start.3 = ((bf16[256,16,128]{2,1,0:T(8,128)(2,1)}), bf16[256,16,128]{2,1,0:T(8,128)(2,1)S(1)}, u32[]{:S(2)}, u32[]{:S(2)}) async-start(bf16[256,16,128]{2,1,0:T(8,128)(2,1)} %bitcast.21), calls=%async_computation.3 | async-start | bytes 2097152 | tf_op jit(solution)/shard_map/all_to_all | solution.py:437
  98.7 4.2 %shard_map.115.beta_hbm = bf16[512,1024]{1,0:T(8,128)(2,1)} custom-call(bf16[512,1024]{1,0:T(8,128)(2,1)} %c_hbm.2, bf16[1024,1024]{1,0:T(8,128)(2,1)} %bitcast.24), custom_call_target="tpu_custom_call" | custom-call | tf_op jit(solution)/shard_map/pallas_call | solution.py:286
  102.9 28.0 %all-to-all-done.3 = bf16[256,16,128]{2,1,0:T(8,128)(2,1)S(1)} async-done(((bf16[256,16,128]{2,1,0:T(8,128)(2,1)}), bf16[256,16,128]{2,1,0:T(8,128)(2,1)S(1)}, u32[]{:S(2)}, u32[]{:S(2)}) %all-to-all-start.3) | async-done | bytes 1048608 | tf_op jit(solution)/shard_map/all_to_all | solution.py:437
  130.9 3.3 %shard_map.116 = f32[512,1024]{1,0:T(8,128)} custom-call(bf16[4,8,8,16,128]{4,3,2,1,0:T(8,128)(2,1)S(1)} %bitcast.18, bf16[512,1024]{1,0:T(8,128)(2,1)} %shard_map.115.beta_hbm), custom_call_target="tpu_custom_call" | custom-call | tf_op jit(solution)/shard_map/pallas_call | solution.py:286
  (51 shorter events, 2.9 us)
Async XLA Ops:
  3.0 19.0 %copy-start.8 = (s32[32,32,2]{1,2,0:T(2,128)S(1)}, s32[32,32,2]{1,2,0:T(2,128)}, u32[]{:S(2)}) copy-start(s32[32,32,2]{1,2,0:T(2,128)} %param.15) | copy-start | bytes 24580
  3.0 19.1 %copy-start.9 = (s32[128,16]{0,1:T(8,128)S(1)}, s32[128,16]{0,1:T(8,128)}, u32[]{:S(2)}) copy-start(s32[128,16]{0,1:T(8,128)} %param.16) | copy-start | bytes 24580
  3.0 19.2 %copy-start.11 = (s32[128,16]{0,1:T(8,128)S(1)}, s32[128,16]{0,1:T(8,128)}, u32[]{:S(2)}) copy-start(s32[128,16]{0,1:T(8,128)} %param.18) | copy-start | bytes 24580
  3.0 19.3 %copy-start.10 = (s32[128,16]{0,1:T(8,128)S(1)}, s32[128,16]{0,1:T(8,128)}, u32[]{:S(2)}) copy-start(s32[128,16]{0,1:T(8,128)} %param.17) | copy-start | bytes 24580
  3.0 19.4 %copy-start.12 = (s32[128,8]{0,1:T(8,128)S(1)}, s32[128,8]{0,1:T(8,128)}, u32[]{:S(2)}) copy-start(s32[128,8]{0,1:T(8,128)} %param.21) | copy-start | bytes 12292
  3.1 19.4 %copy-start.13 = (s32[128,8]{0,1:T(8,128)S(1)}, s32[128,8]{0,1:T(8,128)}, u32[]{:S(2)}) copy-start(s32[128,8]{0,1:T(8,128)} %param.19) | copy-start | bytes 12292
  3.1 36.9 %all-to-all-start = ((bf16[32,128,128]{2,1,0:T(8,128)(2,1)}), bf16[32,128,128]{2,1,0:T(8,128)(2,1)S(1)}, u32[]{:S(2)}, u32[]{:S(2)}) async-start(bf16[32,128,128]{2,1,0:T(8,128)(2,1)} %bitcast.22), calls=%async_computation | async-start | bytes 2097152 | tf_op jit(solution)/shard_map/all_to_all | solution.py:437
  15.1 9.4 %copy-start.14 = (s32[128,8]{0,1:T(8,128)S(1)}, s32[128,8]{0,1:T(8,128)}, u32[]{:S(2)}) copy-start(s32[128,8]{0,1:T(8,128)} %param.20) | copy-start | bytes 12292
  15.1 9.6 %copy-start.7 = (bf16[8,128,128]{2,1,0:T(8,128)(2,1)S(1)}, bf16[8,128,128]{2,1,0:T(8,128)(2,1)}, u32[]{:S(2)}) copy-start(bf16[8,128,128]{2,1,0:T(8,128)(2,1)} %param.14) | copy-start | bytes 786436
  16.8 14.4 %collective-permute-start.3 = (bf16[8,128,128]{2,1,0:T(8,128)(2,1)}, bf16[8,128,128]{2,1,0:T(8,128)(2,1)S(1)}, u32[]{:S(2)}, u32[]{:S(2)}) collective-permute-start(bf16[8,128,128]{2,1,0:T(8,128)(2,1)} %shard_map.110.o0), channel_id=1, source_target_pairs={{0,192},{32,224},{64,128},{96,160},{128,64},{160,96},{192,0},{224,... | collective-permute-start | bytes 786440 | tf_op jit(solution)/shard_map/ppermute | solution.py:309
  19.6 11.6 %collective-permute-start.2 = (bf16[8,128,128]{2,1,0:T(8,128)(2,1)}, bf16[8,128,128]{2,1,0:T(8,128)(2,1)S(1)}, u32[]{:S(2)}, u32[]{:S(2)}) collective-permute-start(bf16[8,128,128]{2,1,0:T(8,128)(2,1)} %shard_map.110.o0), channel_id=1, source_target_pairs={{0,128},{32,160},{64,192},{96,224},{128,0},{160,32},{192,64},{224,... | collective-permute-start | bytes 786440 | tf_op jit(solution)/shard_map/ppermute | solution.py:309
  20.0 11.6 %collective-permute-start.1 = (bf16[8,128,128]{2,1,0:T(8,128)(2,1)}, bf16[8,128,128]{2,1,0:T(8,128)(2,1)S(1)}, u32[]{:S(2)}, u32[]{:S(2)}) collective-permute-start(bf16[8,128,128]{2,1,0:T(8,128)(2,1)} %shard_map.110.o0), channel_id=1, source_target_pairs={{0,64},{32,96},{64,0},{96,32},{128,192},{160,224},{192,128},{224,1... | collective-permute-start | bytes 786440 | tf_op jit(solution)/shard_map/ppermute | solution.py:309
  20.3 13.6 %collective-permute-start = (bf16[8,128,128]{2,1,0:T(8,128)(2,1)}, bf16[8,128,128]{2,1,0:T(8,128)(2,1)S(1)}, u32[]{:S(2)}, u32[]{:S(2)}) collective-permute-start(bf16[8,128,128]{2,1,0:T(8,128)(2,1)} %shard_map.110.o0), channel_id=1, source_target_pairs={{0,32},{32,0},{64,96},{96,64},{128,160},{160,128},{192,224},{224,1... | collective-permute-start | bytes 786440 | tf_op jit(solution)/shard_map/ppermute | solution.py:309
  31.2 10.0 %copy-start.1 = (bf16[8,128,128]{2,1,0:T(8,128)(2,1)}, bf16[8,128,128]{2,1,0:T(8,128)(2,1)S(1)}, u32[]{:S(2)}) copy-start(bf16[8,128,128]{2,1,0:T(8,128)(2,1)S(1)} %collective-permute-done.3.o6) | copy-start | bytes 786436
  31.2 10.0 %copy-start.2 = (bf16[8,128,128]{2,1,0:T(8,128)(2,1)}, bf16[8,128,128]{2,1,0:T(8,128)(2,1)S(1)}, u32[]{:S(2)}) copy-start(bf16[8,128,128]{2,1,0:T(8,128)(2,1)S(1)} %collective-permute-done.2.o4) | copy-start | bytes 786436
  31.6 9.6 %copy-start.3 = (bf16[8,128,128]{2,1,0:T(8,128)(2,1)}, bf16[8,128,128]{2,1,0:T(8,128)(2,1)S(1)}, u32[]{:S(2)}) copy-start(bf16[8,128,128]{2,1,0:T(8,128)(2,1)S(1)} %collective-permute-done.1.o2) | copy-start | bytes 786436
  31.6 3.1 %collective-permute-start.4 = (bf16[8,128,128]{2,1,0:T(8,128)(2,1)S(1)}, bf16[8,128,128]{2,1,0:T(8,128)(2,1)S(1)}, u32[]{:S(2)}, u32[]{:S(2)}) collective-permute-start(bf16[8,128,128]{2,1,0:T(8,128)(2,1)S(1)} %collective-permute-done.1.o2), channel_id=1, source_target_pairs={{0,32},{32,0},{64,96},{96,64},{128,160},{160,128},{192,224},{224,1... | collective-permute-start | bytes 786440 | tf_op jit(solution)/shard_map/ppermute | solution.py:309
  33.4 1.5 %collective-permute-start.5 = (bf16[8,128,128]{2,1,0:T(8,128)(2,1)S(1)}, bf16[8,128,128]{2,1,0:T(8,128)(2,1)S(1)}, u32[]{:S(2)}, u32[]{:S(2)}) collective-permute-start(bf16[8,128,128]{2,1,0:T(8,128)(2,1)S(1)} %collective-permute-done.2.o4), channel_id=1, source_target_pairs={{0,32},{32,0},{64,96},{96,64},{128,160},{160,128},{192,224},{224,1... | collective-permute-start | bytes 786440 | tf_op jit(solution)/shard_map/ppermute | solution.py:309
  33.4 2.0 %collective-permute-start.6 = (bf16[8,128,128]{2,1,0:T(8,128)(2,1)S(1)}, bf16[8,128,128]{2,1,0:T(8,128)(2,1)}, u32[]{:S(2)}, u32[]{:S(2)}) collective-permute-start(bf16[8,128,128]{2,1,0:T(8,128)(2,1)S(1)} %collective-permute-done.3.o6), channel_id=1, source_target_pairs={{0,32},{32,0},{64,96},{96,64},{128,160},{160,128},{192,224},{224,1... | collective-permute-start | bytes 786440 | tf_op jit(solution)/shard_map/ppermute | solution.py:309
  34.0 7.2 %copy-start.4 = (bf16[8,128,128]{2,1,0:T(8,128)(2,1)}, bf16[8,128,128]{2,1,0:T(8,128)(2,1)S(1)}, u32[]{:S(2)}) copy-start(bf16[8,128,128]{2,1,0:T(8,128)(2,1)S(1)} %collective-permute-done.o1) | copy-start | bytes 786436
  34.6 6.6 %copy-start.5 = (bf16[8,128,128]{2,1,0:T(8,128)(2,1)}, bf16[8,128,128]{2,1,0:T(8,128)(2,1)S(1)}, u32[]{:S(2)}) copy-start(bf16[8,128,128]{2,1,0:T(8,128)(2,1)S(1)} %collective-permute-done.4.o3) | copy-start | bytes 786436
  41.2 26.5 %all-to-all-start.1 = ((bf16[32,128,128]{2,1,0:T(8,128)(2,1)}), bf16[32,128,128]{2,1,0:T(8,128)(2,1)S(1)}, u32[]{:S(2)}, u32[]{:S(2)}) async-start(bf16[32,128,128]{2,1,0:T(8,128)(2,1)} %bitcast.23), calls=%async_computation.1 | async-start | bytes 2097152 | tf_op jit(solution)/shard_map/all_to_all | solution.py:437
  67.7 20.8 %all-to-all-start.2 = ((bf16[32,128,128]{2,1,0:T(8,128)(2,1)}), bf16[32,128,128]{2,1,0:T(8,128)(2,1)S(1)}, u32[]{:S(2)}, u32[]{:S(2)}) async-start(bf16[32,128,128]{2,1,0:T(8,128)(2,1)} %bitcast.9), calls=%async_computation.2 | async-start | bytes 2097152 | tf_op jit(solution)/shard_map/all_to_all | solution.py:437
  91.7 39.2 %all-to-all-start.3 = ((bf16[256,16,128]{2,1,0:T(8,128)(2,1)}), bf16[256,16,128]{2,1,0:T(8,128)(2,1)S(1)}, u32[]{:S(2)}, u32[]{:S(2)}) async-start(bf16[256,16,128]{2,1,0:T(8,128)(2,1)} %bitcast.21), calls=%async_computation.3 | async-start | bytes 2097152 | tf_op jit(solution)/shard_map/all_to_all | solution.py:437
  (2 other events, 10.2 us)
